TPU v7x, 512 devices: a whole 4x4x16 slice. The times are simulated.
512 devices in a mesh: sta: 16 (over x_lo, y, core), src: 32 (over z, x_hi).
Axes of the slice: x: 4 (x_hi: 2, x_lo: 2; x = x_hi * 2 + x_lo), y: 4, z: 16, core: 2. Of those that a mesh axis runs over, the one named last changes fastest.
Arguments:
- features: bfloat16 [512, 1024, 128], P('sta', 'src'), may hold values from -6 to 6
- station_lists: int32 [512, 16], replicated, may hold values from 0 to 511, as said below
- station_counts: int32 [512], replicated, may hold values from 1 to 16
- source_lists: int32 [1024, 16], replicated, may hold values from 0 to 1023, as said below
- source_counts: int32 [1024], replicated, may hold values from 1 to 16
- picks: int32 [2, 512], P(None, 'sta'), may hold values 0 or 1
- targets: float32 [2, 1024], P(None, 'src'), may hold values from 0 to 1
- layer_weights: bfloat16 [2, 3, 64, 64], replicated, may hold values from -0.75 to 0.75
- readout_vector: bfloat16 [64], replicated, may hold values from -0.75 to 0.75
Outputs:
- likelihood: float32 [2, 1024], P(None, 'src')
- feature_grad: bfloat16 [512, 1024, 128], P('sta', 'src')
- weight_grad: float32 [2, 3, 64, 64], replicated
- vector_grad: float32 [64], replicated
Inputs may be any that keep to these rules, and one draw needn't show every extreme that they name: `station_lists`: every entry of a station's list lies within 16 rows of that station; entries past its count are padding. `source_lists`: every entry of a source node's list lies within 16 rows of that source node; entries past its count are padding.
All inputs are finite; a program needn't handle non-finite values. No bound on the sum of `picks` on one device may be relied on, other than what follows from the above.
Results may differ from a plain program's by a relative error of at most 0.015.
Values may be sent and summed in bfloat16 or wider, within the bound.
No kernel may reach another device: no remote copies, remote signals or barrier semaphores. Data moves between devices by JAX's collectives and lax.ppermute only.
A program may use at most 64 MiB of HBM per device.

v0:
```python
import jax
import jax.numpy as jnp
from jax import lax
from jax.sharding import PartitionSpec as P

LAYERS = 2
HW = 16


def padded_2(cells, sides, width):
    for axis, dim in sides:
        count = lax.axis_size(axis)
        ends = count - 1
        head = lax.slice_in_dim(cells, 0, width, axis=dim)
        tail = lax.slice_in_dim(cells, cells.shape[dim] - width, cells.shape[dim], axis=dim)
        cells = jnp.concatenate(
            [
                lax.ppermute(tail, axis, [(i, (i + 1) % count) for i in range(ends)]),
                cells,
                lax.ppermute(head, axis, [((i + 1) % count, i) for i in range(ends)]),
            ],
            axis=dim,
        )
    return cells


def count_matrix(lists, counts, first_row, span):
    list_width = lists.shape[1]
    in_list = jnp.arange(list_width)[None, :] < counts[:, None]
    shifted = lists - first_row
    matches = (shifted[:, :, None] == jnp.arange(span)[None, None, :]) & in_list[:, :, None]
    return jnp.sum(matches.astype(jnp.float32), axis=1).astype(jnp.bfloat16)


def blocked(matrix, windows):
    return jnp.kron(jnp.eye(windows, dtype=jnp.bfloat16), matrix)


def apply_block(values, matrix):
    channels = values.shape[-1]
    flat = values.reshape(-1, channels)
    return jnp.dot(flat, matrix, preferred_element_type=jnp.float32).reshape(values.shape)


def outer_sum(left, right, feature):
    return jnp.einsum(
        "nf,ng->fg",
        left.reshape(-1, feature),
        right.reshape(-1, feature),
        preferred_element_type=jnp.float32,
    )


def shards(
    features,
    station_lists,
    station_counts,
    source_lists,
    source_counts,
    picks,
    targets,
    layer_weights,
    readout_vector,
):
    sta_rows, src_rows, channels = features.shape
    feature = layer_weights.shape[-1]
    windows = channels // feature
    sta_first = lax.axis_index("sta") * sta_rows
    src_first = lax.axis_index("src") * src_rows
    own_slists = lax.dynamic_slice_in_dim(station_lists, sta_first, sta_rows, 0)
    own_scounts = lax.dynamic_slice_in_dim(station_counts, sta_first, sta_rows, 0)
    own_rlists = lax.dynamic_slice_in_dim(source_lists, src_first, src_rows, 0)
    own_rcounts = lax.dynamic_slice_in_dim(source_counts, src_first, src_rows, 0)
    sta_mix = count_matrix(own_slists, own_scounts, sta_first - HW, sta_rows + 2 * HW)
    src_mix = count_matrix(own_rlists, own_rcounts, src_first - HW, src_rows + 2 * HW)
    sta_div = own_scounts.astype(jnp.float32)[:, None, None]
    src_div = own_rcounts.astype(jnp.float32)[None, :, None]
    blocks = [
        [blocked(layer_weights[layer_idx, which], windows) for which in range(3)]
        for layer_idx in range(LAYERS)
    ]
    states = features
    saved = []
    for layer_idx in range(LAYERS):
        padded = padded_2(states, (("sta", 0), ("src", 1)), HW)
        along_sta = jnp.einsum(
            "im,mjc->ijc",
            sta_mix,
            padded[:, HW : HW + src_rows],
            preferred_element_type=jnp.float32,
        )
        sta_mean = (along_sta / sta_div).astype(jnp.bfloat16)
        along_src = jnp.einsum(
            "jm,imc->ijc", src_mix, padded[HW : HW + sta_rows], preferred_element_type=jnp.float32
        )
        src_mean = (along_src / src_div).astype(jnp.bfloat16)
        linear = (
            apply_block(states, blocks[layer_idx][0])
            + apply_block(sta_mean, blocks[layer_idx][1])
            + apply_block(src_mean, blocks[layer_idx][2])
        )
        squashed = jnp.tanh(linear)
        saved.append((states, sta_mean, src_mean, squashed))
        states = (states.astype(jnp.float32) + squashed).astype(jnp.bfloat16)
    vector_cols = (
        jnp.eye(windows, dtype=jnp.bfloat16)[:, None, :] * readout_vector[None, :, None]
    ).reshape(channels, windows)
    score = jnp.dot(
        states.reshape(-1, channels), vector_cols, preferred_element_type=jnp.float32
    ).reshape(sta_rows, src_rows, windows)
    picked = picks.astype(jnp.float32)
    partial_sum = jnp.sum(picked.T[:, None, :] * score, axis=0).T
    local_count = jnp.sum(picked, axis=1)
    summed, count = lax.psum((partial_sum, local_count), "sta")
    root = jnp.sqrt(jnp.maximum(count, 1.0))
    likelihood = summed / root[:, None]
    error = jax.nn.sigmoid(likelihood) - targets
    d_score = (picked.T[:, None, :] * error.T[None, :, :]).astype(jnp.bfloat16)
    v_sum = jnp.einsum(
        "nw,nwf->f",
        d_score.reshape(-1, windows),
        states.reshape(-1, windows, feature),
        preferred_element_type=jnp.float32,
    )
    grad = (d_score.astype(jnp.float32)[..., None] * readout_vector.astype(jnp.float32)).reshape(
        sta_rows, src_rows, channels
    )
    w_rows = []
    for layer_idx in reversed(range(LAYERS)):
        before, sta_mean, src_mean, squashed = saved[layer_idx]
        delta = (grad * (1.0 - squashed * squashed)).astype(jnp.bfloat16)
        w_rows.append(
            jnp.stack(
                [
                    outer_sum(before, delta, feature),
                    outer_sum(sta_mean, delta, feature),
                    outer_sum(src_mean, delta, feature),
                ]
            )
        )
        u_sta = (apply_block(delta, blocks[layer_idx][1].T) / sta_div).astype(jnp.bfloat16)
        u_src = (apply_block(delta, blocks[layer_idx][2].T) / src_div).astype(jnp.bfloat16)
        direct = grad + apply_block(delta, blocks[layer_idx][0].T)
        spread_sta = jnp.einsum("im,ijc->mjc", sta_mix, u_sta, preferred_element_type=jnp.float32)
        rim_rows = jnp.concatenate([spread_sta[:HW], spread_sta[sta_rows + HW :]], 0)
        got_rows = padded_2(rim_rows.astype(jnp.bfloat16), (("sta", 0),), HW).astype(rim_rows.dtype)
        from_sta = spread_sta[HW : sta_rows + HW]
        from_sta = from_sta + jnp.pad(got_rows[:HW], ((0, sta_rows - HW), (0, 0), (0, 0)))
        from_sta = from_sta + jnp.pad(got_rows[3 * HW :], ((sta_rows - HW, 0), (0, 0), (0, 0)))
        spread_src = jnp.einsum("jm,ijc->imc", src_mix, u_src, preferred_element_type=jnp.float32)
        rim_cols = jnp.concatenate([spread_src[:, :HW], spread_src[:, src_rows + HW :]], 1)
        got_cols = padded_2(rim_cols.astype(jnp.bfloat16), (("src", 1),), HW).astype(rim_cols.dtype)
        from_src = spread_src[:, HW : src_rows + HW]
        from_src = from_src + jnp.pad(got_cols[:, :HW], ((0, 0), (0, src_rows - HW), (0, 0)))
        from_src = from_src + jnp.pad(got_cols[:, 3 * HW :], ((0, 0), (src_rows - HW, 0), (0, 0)))
        grad = direct + from_sta + from_src
    w_sum = jnp.stack(w_rows[::-1])
    w_total, v_total = lax.psum((w_sum, v_sum), ("sta", "src"))
    node_total = jnp.float32(sta_rows * lax.axis_size("sta")) * jnp.float32(
        src_rows * lax.axis_size("src")
    )
    factor = 1.0 / jnp.sqrt(node_total)
    return (likelihood, grad.astype(jnp.bfloat16), w_total * factor, v_total * factor)


def solution(mesh):
    in_specs = (P("sta", "src", None), P(), P(), P(), P(), P(None, "sta"), P(None, "src"), P(), P())
    out_specs = (P(None, "src"), P("sta", "src", None), P(), P())
    return jax.shard_map(shards, mesh=mesh, in_specs=in_specs, out_specs=out_specs, check_vma=False)
```

profile of v0, /device:TPU:1, one launch (start us, length us, event | category | flops | bytes accessed | tf_op | source)
XLA Modules:
  0.0 722.8 jit_solution(12138712805420795126)
XLA Ops:
  7.2 1.0 fusion.68
  8.3 4.6 collective-permute-start
  12.9 5.5 collective-permute-start.1
  18.5 0.7 copy-done.31
  19.1 1.2 fusion.59
  20.5 1.3 fusion.60
  21.9 0.8 dynamic-slice_subtract_fusion.1
  23.2 0.8 dynamic-slice_subtract_fusion
  24.5 0.6 convert_reduce_fusion.2
  25.3 1.0 reshape.263
  28.5 0.7 reshape.272
  29.4 0.7 reshape.276
  30.3 0.8 convert_reduce_fusion
  31.4 1.3 collective-permute-start.2
  32.7 1.3 collective-permute-start.3
  34.4 1.1 reshape.264
  35.4 1.0 convolution_add_fusion.5
  36.4 7.6 %collective-permute-done.2 = bf16[64,16,128]{2,0,1:T(8,128)(2,1)S(1)} collective-permute-done((bf16[64,16,128]{2,0,1:T(8,128)(2,1)S(1)}, bf16[64,16,128]{2,0,1:T(8,128)(2,1)S(1)}, u32[]{:S(2)}, u32[]{:S(2)}) %collective-permute-start.2) | collective-permute-done | bytes 262176 | tf_op jit(solution)/shard_map/ppermute | solution.py:18
  45.0 1.1 reshape.265
  46.1 1.0 add_convert_fusion.1
  47.1 1.0 reshape.266
  48.2 3.6 collective-permute-start.4
  51.8 1.9 collective-permute-start.5
  53.9 4.1 collective-permute-done.5
  58.2 5.6 collective-permute-start.6
  63.8 1.3 collective-permute-start.7
  65.5 1.1 reshape.268
  67.3 5.6 collective-permute-done.7
  73.2 1.1 reshape.269
  74.5 1.1 reshape.270
  76.1 0.7 copy-done.40
  76.8 25.8 %all-reduce.4 = (f32[2,32]{1,0:T(2,128)S(1)}, f32[2]{0:T(128)S(1)}) all-reduce(f32[2,32]{1,0:T(2,128)S(1)} %bitcast.115, f32[2]{0:T(128)S(1)} %copy-done.40), channel_id=1, replica_groups=mesh['sta'=16,'src'=32] {'sta'}, use_global_device_ids=true, to_apply=%region_3.4 | all-reduce | flops 66 | bytes 528 | tf_op jit(solution)/shard_map/psum | solution.py:114
  102.6 0.7 copy-done.32
  103.3 0.6 fusion.51
  103.9 0.7 copy-done.21
  104.9 1.2 mul.284
  108.7 1.4 copy.149
  110.7 2.4 fusion.69
  113.4 115.2 %psum.31 = f32[64]{0:T(128)S(1)} all-reduce(f32[64]{0:T(128)S(1)} %convolution_bitcast_fusion.9), channel_id=1, replica_groups=mesh['sta'=16,'src'=32] {'sta','src'}, use_global_device_ids=true, to_apply=%region_7.8 | all-reduce | flops 64 | bytes 512 | tf_op jit(solution)/shard_map/psum | solution.py:158
  229.5 0.7 copy-done.6
  230.2 0.9 convolution_bitcast_fusion.4
  231.3 2.9 collective-permute-start.8
  234.2 1.9 collective-permute-start.9
  236.2 3.5 collective-permute-start.10
  239.6 1.5 collective-permute-start.11
  241.1 0.9 convolution_bitcast_fusion.5
  242.2 5.4 collective-permute-done.11
  247.8 0.9 copy-done.8
  248.7 1.2 multiply_convert_fusion
  251.1 0.6 copy.148
  251.8 0.6 copy.107
  252.4 1.7 fusion.70
  254.4 0.7 copy-done.3
  255.5 0.7 copy-done.2
  257.0 0.7 pad_maximum_fusion.11
  257.7 4.3 collective-permute-start.12
  262.0 1.9 collective-permute-start.13
  264.0 4.2 collective-permute-start.14
  268.2 1.3 collective-permute-start.15
  269.5 442.2 %all-reduce.7.cloned.1.call-done = f32[2,3,64,64]{2,3,1,0:T(8,128)} async-done(((f32[2,3,64,64]{2,3,1,0:T(8,128)}), f32[2,3,64,64]{2,3,1,0:T(8,128)}) %all-reduce.7.cloned.1.call-update) | async-done | bytes 98320 | tf_op jit(solution)/shard_map/psum | solution.py:158
  711.7 0.9 broadcast_multiply_fusion
  712.7 0.8 copy.116
  713.8 1.0 copy-done.11
  715.0 1.0 fusion.17
  (161 shorter events, 16.2 us)
Async XLA Ops:
  7.2 704.5 %all-reduce.7.cloned.1.call-start = ((), (), s32[]{:S(2)}) async-start(), calls=%async_computation | async-start | bytes 393216 | tf_op jit(solution)/shard_map/psum | solution.py:158
  8.3 22.9 %collective-permute-start = (bf16[16,32,128]{2,0,1:T(8,128)(2,1)S(1)}, bf16[16,32,128]{2,0,1:T(8,128)(2,1)S(1)}, u32[]{:S(2)}, u32[]{:S(2)}) collective-permute-start(bf16[16,32,128]{2,0,1:T(8,128)(2,1)S(1)} %copy.146), channel_id=1, source_target_pairs={{0,32},{32,64},{64,96},{96,128},{128,160},{160,192},{192,224},{224... | collective-permute-start | bytes 393224 | tf_op jit(solution)/shard_map/ppermute | solution.py:18
  12.9 9.9 %copy-start.19 = (bf16[2,3,64,64]{3,2,1,0:T(8,128)(2,1)S(1)}, bf16[2,3,64,64]{3,2,1,0:T(8,128)(2,1)}, u32[]{:S(2)}) copy-start(bf16[2,3,64,64]{3,2,1,0:T(8,128)(2,1)} %param.16) | copy-start | bytes 147460
  12.9 18.4 %collective-permute-start.1 = (bf16[16,32,128]{2,0,1:T(8,128)(2,1)S(1)}, bf16[16,32,128]{2,0,1:T(8,128)(2,1)S(1)}, u32[]{:S(2)}, u32[]{:S(2)}) collective-permute-start(bf16[16,32,128]{2,0,1:T(8,128)(2,1)S(1)} %copy.147), channel_id=1, source_target_pairs={{32,0},{64,32},{96,64},{128,96},{160,128},{192,160},{224,192},{256... | collective-permute-start | bytes 393224 | tf_op jit(solution)/shard_map/ppermute | solution.py:20
  18.5 0.7 copy-start.31
  19.1 56.8 %copy-start.20 = (f32[32,2]{0,1:T(2,128)}, f32[32,2]{0,1:T(2,128)S(1)}, u32[]{:S(2)}) copy-start(f32[32,2]{0,1:T(2,128)S(1)} %convert_bitcast_fusion) | copy-start | bytes 772
  22.7 1.5 copy-start
  24.2 40.9 %copy-start.22 = (bf16[32,64]{1,0:T(8,128)(2,1)}, bf16[32,64]{1,0:T(8,128)(2,1)S(1)}, u32[]{:S(2)}) copy-start(bf16[32,64]{1,0:T(8,128)(2,1)S(1)} %convert_reduce_fusion.1) | copy-start | bytes 12292
  26.5 0.7 copy-start.39
  31.4 12.6 %collective-permute-start.2 = (bf16[64,16,128]{2,0,1:T(8,128)(2,1)S(1)}, bf16[64,16,128]{2,0,1:T(8,128)(2,1)S(1)}, u32[]{:S(2)}, u32[]{:S(2)}) collective-permute-start(bf16[64,16,128]{2,0,1:T(8,128)(2,1)S(1)} %get-tuple-element.38), channel_id=1, source_target_pairs={{0,1},{1,2},{2,3},{3,4},{4,5},{5,6},{6,7},{7,8},{8,9},{9,10},{10,1... | collective-permute-start | bytes 786440 | tf_op jit(solution)/shard_map/ppermute | solution.py:18
  32.7 1.3 copy-start.36
  32.7 11.4 %collective-permute-start.3 = (bf16[64,16,128]{2,0,1:T(8,128)(2,1)S(1)}, bf16[64,16,128]{2,0,1:T(8,128)(2,1)S(1)}, u32[]{:S(2)}, u32[]{:S(2)}) collective-permute-start(bf16[64,16,128]{2,0,1:T(8,128)(2,1)S(1)} %get-tuple-element.39), channel_id=1, source_target_pairs={{1,0},{2,1},{3,2},{4,3},{5,4},{6,5},{7,6},{8,7},{9,8},{10,9},{11,1... | collective-permute-start | bytes 786440 | tf_op jit(solution)/shard_map/ppermute | solution.py:20
  36.4 7.8 %copy-start.25 = (bf16[32,64]{1,0:T(8,128)(2,1)S(1)}, bf16[32,64]{1,0:T(8,128)(2,1)}, u32[]{:S(2)}) copy-start(bf16[32,64]{1,0:T(8,128)(2,1)} %convert_reduce_fusion) | copy-start | bytes 12292
  44.2 0.6 copy-start.34
  48.2 5.7 collective-permute-start.4
  51.8 6.3 collective-permute-start.5
  58.2 6.9 copy-start.37
  58.2 9.1 %collective-permute-start.6 = (bf16[64,16,128]{2,1,0:T(8,128)(2,1)S(1)}, bf16[64,16,128]{2,1,0:T(8,128)(2,1)S(1)}, u32[]{:S(2)}, u32[]{:S(2)}) collective-permute-start(bf16[64,16,128]{2,1,0:T(8,128)(2,1)S(1)} %get-tuple-element.36), channel_id=1, source_target_pairs={{0,1},{1,2},{2,3},{3,4},{4,5},{5,6},{6,7},{7,8},{8,9},{9,10},{10,1... | collective-permute-start | bytes 786440 | tf_op jit(solution)/shard_map/ppermute | solution.py:18
  63.8 9.1 %collective-permute-start.7 = (bf16[64,16,128]{2,1,0:T(8,128)(2,1)S(1)}, bf16[64,16,128]{2,1,0:T(8,128)(2,1)S(1)}, u32[]{:S(2)}, u32[]{:S(2)}) collective-permute-start(bf16[64,16,128]{2,1,0:T(8,128)(2,1)S(1)} %get-tuple-element.37), channel_id=1, source_target_pairs={{1,0},{2,1},{3,2},{4,3},{5,4},{6,5},{7,6},{8,7},{9,8},{10,9},{11,1... | collective-permute-start | bytes 786440 | tf_op jit(solution)/shard_map/ppermute | solution.py:20
  65.5 1.1 copy-start.18
  66.6 6.3 copy-start.26
  74.5 1.1 copy-start.33
  76.1 0.7 copy-start.40
  102.6 0.7 copy-start.32
  103.9 0.7 copy-start.21
  106.8 0.6 copy-start.29
  107.5 0.7 copy-start.23
  110.7 2.5 copy-start.1
  113.1 116.0 %copy-start.7 = (bf16[2048,64]{1,0:T(8,128)(2,1)S(1)}, bf16[2048,64]{1,0:T(8,128)(2,1)}, u32[]{:S(2)}) copy-start(bf16[2048,64]{1,0:T(8,128)(2,1)} %reshape.269) | copy-start | bytes 786436
  229.2 1.0 copy-start.6
  230.2 1.0 copy-start.10
  230.2 5.9 copy-start.16
  231.2 9.9 %copy-start.5 = (bf16[2048,64]{1,0:T(8,128)(2,1)S(1)}, bf16[2048,64]{1,0:T(8,128)(2,1)}, u32[]{:S(2)}) copy-start(bf16[2048,64]{1,0:T(8,128)(2,1)} %reshape.266) | copy-start | bytes 786436
  231.3 10.8 %collective-permute-start.8 = (bf16[16,32,128]{2,1,0:T(8,128)(2,1)S(1)}, bf16[16,32,128]{2,1,0:T(8,128)(2,1)S(1)}, u32[]{:S(2)}, u32[]{:S(2)}) collective-permute-start(bf16[16,32,128]{2,1,0:T(8,128)(2,1)S(1)} %get-tuple-element.32), channel_id=1, source_target_pairs={{0,32},{32,64},{64,96},{96,128},{128,160},{160,192},{192,224},{224... | collective-permute-start | bytes 393224 | tf_op jit(solution)/shard_map/ppermute | solution.py:18
  234.2 7.9 %collective-permute-start.9 = (bf16[16,32,128]{2,1,0:T(8,128)(2,1)S(1)}, bf16[16,32,128]{2,1,0:T(8,128)(2,1)S(1)}, u32[]{:S(2)}, u32[]{:S(2)}) collective-permute-start(bf16[16,32,128]{2,1,0:T(8,128)(2,1)S(1)} %get-tuple-element.33), channel_id=1, source_target_pairs={{32,0},{64,32},{96,64},{128,96},{160,128},{192,160},{224,192},{256... | collective-permute-start | bytes 393224 | tf_op jit(solution)/shard_map/ppermute | solution.py:20
  236.2 6.0 collective-permute-start.10
  239.6 8.0 %collective-permute-start.11 = (bf16[32,16,128]{2,1,0:T(8,128)(2,1)S(1)}, bf16[32,16,128]{2,1,0:T(8,128)(2,1)S(1)}, u32[]{:S(2)}, u32[]{:S(2)}) collective-permute-start(bf16[32,16,128]{2,1,0:T(8,128)(2,1)S(1)} %get-tuple-element.35), channel_id=1, source_target_pairs={{1,0},{2,1},{3,2},{4,3},{5,4},{6,5},{7,6},{8,7},{9,8},{10,9},{11,1... | collective-permute-start | bytes 393224 | tf_op jit(solution)/shard_map/ppermute | solution.py:20
  242.2 5.6 copy-start.12
  247.6 1.0 copy-start.8
  247.8 0.9 copy-start.28
  247.8 0.9 copy-start.30
  249.9 0.8 copy-start.17
  249.9 0.8 copy-start.24
  249.9 0.8 copy-start.38
  251.7 0.7 copy-start.27
  251.7 0.7 copy-start.35
  252.4 1.7 copy-start.4
  254.1 1.0 copy-start.3
  255.1 1.0 copy-start.2
  256.2 0.8 copy-start.13
  256.2 0.8 copy-start.14
  257.0 7.0 copy-start.15
  257.7 455.7 %collective-permute-start.12 = (bf16[16,32,128]{2,1,0:T(8,128)(2,1)S(1)}, bf16[16,32,128]{2,1,0:T(8,128)(2,1)S(1)}, u32[]{:S(2)}, u32[]{:S(2)}) collective-permute-start(bf16[16,32,128]{2,1,0:T(8,128)(2,1)S(1)} %get-tuple-element.28), channel_id=1, source_target_pairs={{0,32},{32,64},{64,96},{96,128},{128,160},{160,192},{192,224},{224... | collective-permute-start | bytes 393224 | tf_op jit(solution)/shard_map/ppermute | solution.py:18
  262.0 451.4 %collective-permute-start.13 = (bf16[16,32,128]{2,1,0:T(8,128)(2,1)S(1)}, bf16[16,32,128]{2,1,0:T(8,128)(2,1)S(1)}, u32[]{:S(2)}, u32[]{:S(2)}) collective-permute-start(bf16[16,32,128]{2,1,0:T(8,128)(2,1)S(1)} %get-tuple-element.29), channel_id=1, source_target_pairs={{32,0},{64,32},{96,64},{128,96},{160,128},{192,160},{224,192},{256... | collective-permute-start | bytes 393224 | tf_op jit(solution)/shard_map/ppermute | solution.py:20
  264.0 449.6 %collective-permute-start.14 = (bf16[32,16,128]{2,1,0:T(8,128)(2,1)S(1)}, bf16[32,16,128]{2,1,0:T(8,128)(2,1)S(1)}, u32[]{:S(2)}, u32[]{:S(2)}) collective-permute-start(bf16[32,16,128]{2,1,0:T(8,128)(2,1)S(1)} %get-tuple-element.30), channel_id=1, source_target_pairs={{0,1},{1,2},{2,3},{3,4},{4,5},{5,6},{6,7},{7,8},{8,9},{9,10},{10,1... | collective-permute-start | bytes 393224 | tf_op jit(solution)/shard_map/ppermute | solution.py:18
  268.2 445.4 %collective-permute-start.15 = (bf16[32,16,128]{2,1,0:T(8,128)(2,1)S(1)}, bf16[32,16,128]{2,1,0:T(8,128)(2,1)S(1)}, u32[]{:S(2)}, u32[]{:S(2)}) collective-permute-start(bf16[32,16,128]{2,1,0:T(8,128)(2,1)S(1)} %get-tuple-element.31), channel_id=1, source_target_pairs={{1,0},{2,1},{3,2},{4,3},{5,4},{6,5},{7,6},{8,7},{9,8},{10,9},{11,1... | collective-permute-start | bytes 393224 | tf_op jit(solution)/shard_map/ppermute | solution.py:20
  713.6 1.2 copy-start.11
  713.6 1.3 copy-start.9
Sparse Core Ops, SparseCore 0:
  257.8 453.8 all-reduce.6
where the time goes:
time: 724 us; the launch traced here: 723 us
  waiting for transfers between devices  466 us (64%)
  blocking collectives  141 us (19%)
  starting transfers between devices  46.6 us (6%)
  local copies, waits for them, and re-layouts  29.8 us (4%)
  matrix products  14.8 us (2%)
  between operations  14.8 us (2%)
  other arithmetic  10.1 us (1%)
    psum x1, waiting for transfers between devices, shards(): w_total, v_total = lax.psum((w_sum, v_sum), ('sta', 'src'))  442 us
    psum x1, blocking collectives, shards(): w_total, v_total = lax.psum((w_sum, v_sum), ('sta', 'src'))  115 us
    ppermute x8, starting transfers between devices, padded_2(): lax.ppermute(tail, axis, [(i, (i + 1) % count) for i in range(ends)])  30 us
    psum x1, blocking collectives, shards(): summed, count = lax.psum((partial_sum, local_count), 'sta')  25.8 us
    ppermute x8, starting transfers between devices, padded_2(): lax.ppermute(head, axis, [((i + 1) % count, i) for i in range(ends)])  16.6 us
    ppermute x8, waiting for transfers between devices, padded_2(): lax.ppermute(head, axis, [((i + 1) % count, i) for i in range(ends)])  15.3 us
  transfers between devices with their start and end apart: 17, of which 7 were waited for; matrix products, arithmetic and copies ran while one was open for 3% of the time, Pallas kernels for 0%

commit v1 on v0

v1 whole, which is shorter than its diff:
```python
import jax
import jax.numpy as jnp
from jax import lax
from jax.experimental import pallas as pl
from jax.experimental.pallas import tpu as pltpu
from jax.sharding import Mesh
from jax.sharding import PartitionSpec as P

LAYERS = 2
HW = 16
BF = jnp.bfloat16
F32 = jnp.float32
PLANE = ("sta", "xh")
SRC = ("z", "xh")
NT = (((1,), (1,)), ((), ()))
TN = (((0,), (0,)), ((), ()))
VMEM_LIMIT = 40 * 1024 * 1024


def iota(shape, dim):
    return lax.broadcasted_iota(jnp.int32, shape, dim)


def dot(a, b):
    return jnp.dot(a, b, preferred_element_type=F32)


def dot_nt(a, b, precision=None):
    return lax.dot_general(a, b, NT, precision=precision, preferred_element_type=F32)


def onehot(mask):
    return jnp.where(mask, 1.0, 0.0).astype(BF)


def call(body, outs, *args):
    vm = pl.BlockSpec(memory_space=pltpu.VMEM)
    return pl.pallas_call(
        body,
        out_shape=[jax.ShapeDtypeStruct(s, d) for s, d in outs],
        in_specs=[vm] * len(args),
        out_specs=[vm] * len(outs),
        compiler_params=pltpu.CompilerParams(vmem_limit_bytes=VMEM_LIMIT),
    )(*args)


def count_rows(counts_ref, first, rows):
    total = counts_ref.shape[1]
    hit = onehot(iota((rows, total), 1) == iota((rows, total), 0) + first)
    every = jnp.broadcast_to(counts_ref[...].astype(F32), (128, total)).astype(BF)
    return dot_nt(hit, every)


def list_counts(lists, counts, first, span):
    rows = lists.shape[0]
    shifted = lists - first
    cols = iota((rows, span), 1)
    acc = jnp.zeros((rows, span), F32)
    for k in range(lists.shape[1]):
        hit = (shifted[:, k : k + 1] == cols) & (counts[:, :span] > k)
        acc = acc + jnp.where(hit, 1.0, 0.0)
    return acc.astype(BF)


def mixes(lists_ref, counts_ref, first, own):
    total = lists_ref.shape[0]
    lo = pl.multiple_of(jnp.maximum(first - HW, 0), HW)
    mid = pl.multiple_of(first, HW)
    hi = pl.multiple_of(jnp.minimum(first + own, total - HW), HW)
    mine = lists_ref[pl.ds(mid, own), :]
    wide = jnp.concatenate([lists_ref[pl.ds(lo, HW), :], mine, lists_ref[pl.ds(hi, HW), :]], 0)
    own_counts = count_rows(counts_ref, first, own)
    wide_counts = count_rows(counts_ref, first - HW, own + 2 * HW)
    span = own + 2 * HW
    gather = list_counts(mine, own_counts, first - HW, span)
    scatter = list_counts(wide, wide_counts, first, own)
    return gather, scatter, own_counts


def prep_body(sta_rows, src_rows, *refs):
    (slists, scounts, rlists, rcounts, picks, targets, weights, readout) = refs[:8]
    (sk, tk, rk, qk, sinv, rinv, wf, wb, px, cnt, tgt, rl) = refs[8:]
    sta_first = lax.axis_index("sta") * sta_rows
    src_first = (lax.axis_index("z") * lax.axis_size("xh") + lax.axis_index("xh")) * src_rows
    feature = weights.shape[-1]
    channels = 2 * feature

    gather, scatter, own_counts = mixes(slists, scounts, sta_first, sta_rows)
    ext = sta_rows + 2 * HW
    spread_cols = onehot(iota((ext, ext * HW), 1) >> 4 == iota((ext, ext * HW), 0))
    step = 128
    per = step // HW
    lane_mask = (iota((step, ext * HW), 0) & 15) == (iota((step, ext * HW), 1) & 15)
    for part in range(sta_rows * HW // step):
        pick_rows = onehot((iota((step, sta_rows), 0) >> 4) + part * per == iota((step, sta_rows), 1))
        for source, target, form in ((gather, sk, dot), (scatter, tk, dot_nt)):
            rows = form(pick_rows, source).astype(BF)
            full = dot(rows, spread_cols)
            target[part * step : (part + 1) * step, :] = jnp.where(lane_mask, full, 0.0).astype(BF)
        inverse = 1.0 / dot(pick_rows, own_counts.astype(BF))
        sinv[part * step : (part + 1) * step, :] = inverse

    gather, scatter, own_counts = mixes(rlists, rcounts, src_first, src_rows)
    ext = src_rows + 2 * HW
    rows_n, cols_n = 4 * src_rows, 4 * ext
    pick_rows = onehot((iota((rows_n, src_rows), 0) & (src_rows - 1)) == iota((rows_n, src_rows), 1))
    spread_cols = onehot((iota((ext, cols_n), 1) & (ext - 1)) == iota((ext, cols_n), 0))
    block_mask = (iota((rows_n, cols_n), 0) >> 5) == (iota((rows_n, cols_n), 1) >> 6)
    for source, target, form in ((gather, rk, dot), (scatter, qk, dot_nt)):
        full = dot(form(pick_rows, source).astype(BF), spread_cols)
        target[...] = jnp.where(block_mask, full, 0.0).astype(BF)
    rinv[...] = 1.0 / dot(pick_rows, own_counts.astype(BF))

    twice = onehot((iota((feature, channels), 1) & (feature - 1)) == iota((feature, channels), 0))
    unit = onehot(iota((feature, feature), 0) == iota((feature, feature), 1))
    left = iota((feature, channels), 1) < feature
    for layer in range(LAYERS):
        for which in range(3):
            matrix = weights[layer, which]
            plain = dot(matrix, twice)
            turned = dot_nt(unit, jnp.concatenate([matrix, matrix], 0))
            at = which * channels
            wf[layer, at : at + feature, :] = jnp.where(left, plain, 0.0).astype(BF)
            wf[layer, at + feature : at + channels, :] = jnp.where(left, 0.0, plain).astype(BF)
            wb[layer, :feature, at : at + channels] = jnp.where(left, turned, 0.0).astype(BF)
            wb[layer, feature:, at : at + channels] = jnp.where(left, 0.0, turned).astype(BF)
    rl[...] = dot(jnp.broadcast_to(readout[...].astype(F32), (16, feature)).astype(BF), twice)[:8]

    window = iota((16, sta_rows), 0)
    picked = picks[...].astype(F32)
    rows = jnp.where(window == 0, picked[0:1, :], jnp.where(window == 1, picked[1:2, :], 0.0)).astype(BF)
    choose = onehot((iota((16, channels), 1) >> 6) == iota((16, channels), 0))
    chunk = 256
    for part in range(sta_rows * src_rows // chunk):
        at = part * chunk
        own = onehot((iota((chunk, sta_rows), 0) + at) >> 5 == iota((chunk, sta_rows), 1))
        wide = dot(dot_nt(own, rows).astype(BF), choose).astype(BF)
        span = chunk // src_rows
        px[part * span : (part + 1) * span] = wide.reshape(span, src_rows, channels)
    cnt[...] = dot(rows, jnp.ones((sta_rows, channels), BF))[:8]
    line = iota((8, src_rows), 0)
    aims = targets[...]
    tgt[...] = jnp.where(line == 0, aims[0:1, :], jnp.where(line == 1, aims[1:2, :], 0.0))


def edge_body(x, hi, lo, right, left):
    store_edges(x, x, hi, lo, right, left)


def store_edges(rows, cols, hi, lo, right, left):
    hi[...] = rows[rows.shape[0] - HW :]
    lo[...] = rows[:HW]
    right[...] = cols[:, cols.shape[1] - HW :]
    left[...] = cols[:, :HW]


def mix_sta(mix, up, own, down):
    span = own.shape[0] + 2 * HW
    parts = []
    for g in range(own.shape[1] // HW):
        cut = slice(g * HW, (g + 1) * HW)
        parts.append(
            jnp.concatenate([up[:, cut], own[:, cut], down[:, cut]], 0).reshape(span * HW, 128)
        )
    out = dot(mix[...], jnp.concatenate(parts, 1))
    return [out[:, g * 128 : (g + 1) * 128] for g in range(len(parts))]


def mix_src(mix, left, own, right, first):
    parts = []
    for at in (first, first + 4):
        cut = slice(at, at + 4)
        joined = jnp.concatenate([left[cut], own[cut], right[cut]], 1)
        parts.append(joined.reshape(4 * joined.shape[1], 128))
    out = dot(mix[...], jnp.concatenate(parts, 1))
    return jnp.concatenate([out[:, :128], out[:, 128:]], 0)


def forward_parts(h, up, down, left, right, sk, rk, sinv, rinv, wf, states, keep, layer):
    rows, cols, _ = h.shape
    for g, part in enumerate(mix_sta(sk, up, h, down)):
        mean = (part * sinv[...]).astype(BF).reshape(rows, HW, 128)
        states[:, g * HW : (g + 1) * HW, 128:256] = mean
    states[:, :, :128] = h[...]
    both = jnp.concatenate([rinv[...], rinv[...]], 0)
    for p in range(rows // 8):
        cut = slice(8 * p, 8 * p + 8)
        mean = (mix_src(rk, left, h, right, 8 * p) * both).astype(BF)
        states[cut, :, 256:384] = mean.reshape(8, cols, 128)
        z = dot(states[cut].reshape(8 * cols, 384), wf[layer])
        t = jnp.tanh(z)
        keep[cut] = (1.0 - t * t).reshape(8, cols, 128)
        before = h[cut].reshape(8 * cols, 128).astype(F32)
        yield cut, (before + t).astype(BF)


def forward0_body(h, up, down, left, right, sk, rk, sinv, rinv, wf, nxt, hi, lo, rgt, lft, states, keep):
    cols = h.shape[1]
    for cut, after in forward_parts(h, up, down, left, right, sk, rk, sinv, rinv, wf, states, keep, 0):
        nxt[cut] = after.reshape(8, cols, 128)
    store_edges(nxt, nxt, hi, lo, rgt, lft)


def forward1_body(h, up, down, left, right, sk, rk, sinv, rinv, wf, px, cnt, rl, states, keep, xsum, block):
    cols = h.shape[1]
    acc = jnp.zeros((cols, 128), F32)
    for cut, after in forward_parts(h, up, down, left, right, sk, rk, sinv, rinv, wf, states, keep, 1):
        part = after.astype(F32).reshape(8, cols, 128) * px[cut].astype(F32)
        acc = acc + jnp.sum(part, axis=0)
    xsum[...] = acc
    read = jnp.where((iota((8, 128), 1) >> 6) == iota((8, 128), 0), rl[...], 0.0)
    padded = jnp.concatenate([acc, jnp.zeros((128 - cols, 128), F32)], 0)
    sums = dot_nt(read, padded, precision=lax.Precision.HIGHEST)
    mixed = jnp.where(iota((8, 128), 1) < 64, sums, cnt[...])
    block[...] = jnp.broadcast_to(mixed[None], block.shape)


def backward_tail(make, q, states, wb, sinv, rinv, layer, delta, direct, usta, usrc, edges):
    rows, cols, _ = q.shape
    both = jnp.concatenate([rinv[...], rinv[...]], 0)
    for p in range(rows // 8):
        cut = slice(8 * p, 8 * p + 8)
        grad = make(p)
        d = (grad * q[cut].reshape(8 * cols, 128)).astype(BF)
        delta[8 * cols * p : 8 * cols * (p + 1), :] = d
        u = dot(d, wb[layer])
        direct[cut] = (grad + u[:, :128]).reshape(8, cols, 128)
        scale = sinv[8 * HW * p : 8 * HW * (p + 1), :].reshape(8, HW, 128)
        scale = jnp.concatenate([scale] * (cols // HW), 1)
        usta[cut] = (u[:, 128:256].reshape(8, cols, 128) * scale).astype(BF)
        usrc[cut] = (u[:, 256:384] * both).astype(BF).reshape(8, cols, 128)
    store_edges(usta, usrc, *edges)
    flat = states[...].reshape(rows * cols, 384)
    outer = lax.dot_general(flat, delta[...], TN, preferred_element_type=F32)
    pairs = []
    for which in range(3):
        top = outer[which * 128 : which * 128 + 64]
        low = outer[which * 128 + 64 : which * 128 + 128]
        pairs.append((top + pltpu.roll(low, 64, 1), pltpu.roll(top, 64, 1) + low))
    return pairs


def backward1_body(total, tgt, px, q, states, xsum, rl, wb, sinv, rinv, lik, direct, usta, usrc, hi, lo, rgt, lft, wpart, delta):
    rows, cols, _ = q.shape
    sums = jnp.sum(total[...], axis=0)
    counts = pltpu.roll(sums, 64, 1)[:, :cols]
    logits = sums[:, :cols] / jnp.sqrt(jnp.maximum(counts, 1.0))
    lik[...] = logits[:2, :]
    error = jax.nn.sigmoid(logits) - tgt[...]
    error = jnp.concatenate([error, jnp.zeros((8, cols), F32)], 0).astype(BF)
    unit = onehot(iota((cols, cols), 0) == iota((cols, cols), 1))
    choose = onehot((iota((16, 128), 1) >> 6) == iota((16, 128), 0))
    wide = dot(dot_nt(unit, error).astype(BF), choose)
    read = rl[0:1, :]

    def make(p):
        score = px[8 * p : 8 * p + 8].astype(F32) * wide[None]
        return score.reshape(8 * cols, 128) * read

    pairs = backward_tail(make, q, states, wb, sinv, rinv, 1, delta, direct, usta, usrc, (hi, lo, rgt, lft))
    lane = iota((64, 128), 1) < 64
    wpart[0:64, :] = jnp.where(lane, pairs[0][0], pairs[1][1])
    wpart[64:128, :] = pairs[2][0]
    v = jnp.sum(wide * xsum[...], axis=0, keepdims=True)
    v = jnp.broadcast_to(v, (8, 128))
    wpart[128:136, :] = v + pltpu.roll(v, 64, 1)


def gathered(direct, usta, usrc, up, down, left, right, tk, qk, hold):
    rows, cols, _ = direct.shape
    for g, part in enumerate(mix_sta(tk, up, usta, down)):
        hold[:, g * HW : (g + 1) * HW, :] = part.reshape(rows, HW, 128)

    def make(p):
        cut = slice(8 * p, 8 * p + 8)
        base = (direct[cut] + hold[cut]).reshape(8 * cols, 128)
        return base + mix_src(qk, left, usrc, right, 8 * p)

    return make


def backward0_body(direct1, usta1, usrc1, up, down, left, right, tk, qk, q, states, wb, sinv, rinv, wpart, direct, usta, usrc, hi, lo, rgt, lft, pay, delta, hold):
    make = gathered(direct1, usta1, usrc1, up, down, left, right, tk, qk, hold)
    pairs = backward_tail(make, q, states, wb, sinv, rinv, 0, delta, direct, usta, usrc, (hi, lo, rgt, lft))
    lane = iota((64, 128), 1) < 64
    pay[0:64, :] = wpart[0:64, :]
    pay[64:128, :] = jnp.where(lane, wpart[64:128, :], pairs[2][1])
    pay[128:192, :] = jnp.where(lane, pairs[0][0], pairs[1][1])
    pay[192:200, :] = wpart[128:136, :]
    pay[200:, :] = jnp.zeros((pay.shape[0] - 200, 128), F32)


def last_body(direct, usta, usrc, up, down, left, right, tk, qk, out, hold):
    make = gathered(direct, usta, usrc, up, down, left, right, tk, qk, hold)
    cols = direct.shape[1]
    for p in range(direct.shape[0] // 8):
        out[8 * p : 8 * p + 8] = make(p).astype(BF).reshape(8, cols, 128)


def sum_body(x, out):
    out[...] = jnp.broadcast_to(jnp.sum(x[...], axis=0)[None], out.shape)


def unpack_body(factor, x, w, v):
    flat = x[...].reshape(-1, 128) * factor
    first = flat[0:64]
    second = flat[64:128]
    third = flat[128:192]
    w[1, 0] = first[:, :64]
    w[1, 1] = pltpu.roll(first, 64, 1)[:, :64]
    w[1, 2] = second[:, :64]
    w[0, 2] = pltpu.roll(second, 64, 1)[:, :64]
    w[0, 0] = third[:, :64]
    w[0, 1] = pltpu.roll(third, 64, 1)[:, :64]
    v[...] = flat[192:193, :64]


def scratch_call(body, outs, scratch, *args):
    vm = pl.BlockSpec(memory_space=pltpu.VMEM)
    return pl.pallas_call(
        body,
        out_shape=[jax.ShapeDtypeStruct(s, d) for s, d in outs],
        in_specs=[vm] * len(args),
        out_specs=[vm] * len(outs),
        scratch_shapes=[pltpu.VMEM(s, d) for s, d in scratch],
        compiler_params=pltpu.CompilerParams(vmem_limit_bytes=VMEM_LIMIT),
    )(*args)


def halo(hi, lo, right, left):
    sta, src = lax.axis_size("sta"), lax.axis_size("z") * lax.axis_size("xh")
    ups = [(i, i + 1) for i in range(sta - 1)]
    rights = [(i, i + 1) for i in range(src - 1)]
    from_up = lax.ppermute(hi, "sta", ups)
    from_down = lax.ppermute(lo, "sta", [(b, a) for a, b in ups])
    from_left = lax.ppermute(right, SRC, rights)
    from_right = lax.ppermute(left, SRC, [(b, a) for a, b in rights])
    return from_up, from_down, from_left, from_right


def shards(features, station_lists, station_counts, source_lists, source_counts, picks, targets, layer_weights, readout_vector):
    rows, cols, channels = features.shape
    n_sta = lax.axis_size("sta")
    n_z = lax.axis_size("z")
    n_plane = n_sta * lax.axis_size("xh")
    whole = (rows, cols, channels)
    edge_outs = [((HW, cols, channels), BF)] * 2 + [((rows, HW, channels), BF)] * 2
    ext_sta, ext_src = rows + 2 * HW, cols + 2 * HW

    edges = call(edge_body, edge_outs, features)
    sk, tk, rk, qk, sinv, rinv, wf, wb, px, cnt, tgt, rl = call(
        lambda *refs: prep_body(rows, cols, *refs),
        [
            ((rows * HW, ext_sta * HW), BF),
            ((rows * HW, ext_sta * HW), BF),
            ((4 * cols, 4 * ext_src), BF),
            ((4 * cols, 4 * ext_src), BF),
            ((rows * HW, channels), F32),
            ((4 * cols, channels), F32),
            ((LAYERS, 3 * channels, channels), BF),
            ((LAYERS, channels, 3 * channels), BF),
            (whole, BF),
            ((8, channels), F32),
            ((8, cols), F32),
            ((8, channels), F32),
        ],
        station_lists,
        station_counts.reshape(1, -1),
        source_lists,
        source_counts.reshape(1, -1),
        picks,
        targets,
        layer_weights,
        readout_vector.reshape(1, -1),
    )
    state_outs = [((rows, cols, 3 * channels), BF), (whole, F32)]
    got = halo(*edges)
    h1, *edges, states0, q0 = call(
        forward0_body, [(whole, BF)] + edge_outs + state_outs, features, *got, sk, rk, sinv, rinv, wf
    )
    got = halo(*edges)
    states1, q1, xsum, block = call(
        forward1_body,
        state_outs + [((cols, channels), F32), ((n_sta, 8, channels), F32)],
        h1,
        *got,
        sk,
        rk,
        sinv,
        rinv,
        wf,
        px,
        cnt,
        rl,
    )
    total = lax.all_to_all(block, "sta", 0, 0)
    grad_outs = [(whole, F32), (whole, BF), (whole, BF)] + edge_outs
    flat = ((rows * cols, channels), BF)
    likelihood, direct, usta, usrc, *edges, wpart = scratch_call(
        backward1_body,
        [((2, cols), F32)] + grad_outs + [((136, channels), F32)],
        [flat],
        total,
        tgt,
        px,
        q1,
        states1,
        xsum,
        rl,
        wb,
        sinv,
        rinv,
    )
    got = halo(*edges)
    per = -(-200 // (8 * n_plane)) * 8
    direct, usta, usrc, *edges, pay = scratch_call(
        backward0_body,
        grad_outs + [((per * n_plane, channels), F32)],
        [flat, (whole, F32)],
        direct,
        usta,
        usrc,
        *got,
        tk,
        qk,
        q0,
        states0,
        wb,
        sinv,
        rinv,
        wpart,
    )
    got = halo(*edges)
    (feature_grad,) = scratch_call(last_body, [(whole, BF)], [(whole, F32)], direct, usta, usrc, *got, tk, qk)
    part = lax.all_to_all(pay.reshape(n_plane, per, channels), PLANE, 0, 0)
    (part,) = call(sum_body, [((n_z, per, channels), F32)], part)
    part = lax.all_to_all(part, "z", 0, 0)
    (part,) = call(sum_body, [((n_plane, per, channels), F32)], part)
    part = lax.all_to_all(part, PLANE, 0, 0)
    nodes = float(rows * n_sta * cols * lax.axis_size("z") * lax.axis_size("xh"))
    feature = layer_weights.shape[-1]
    weight_grad, vector_grad = call(
        lambda *refs: unpack_body(nodes**-0.5, *refs),
        [(layer_weights.shape, F32), ((1, feature), F32)],
        part,
    )
    return likelihood, feature_grad, weight_grad, vector_grad.reshape(feature)


def solution(mesh):
    n_sta, n_src = mesh.devices.shape
    near = 2
    fine = Mesh(mesh.devices.reshape(n_sta, n_src // near, near), ("sta",) + SRC)
    in_specs = (P("sta", SRC, None), P(), P(), P(), P(), P(None, "sta"), P(None, SRC), P(), P())
    out_specs = (P(None, SRC), P("sta", SRC, None), P(), P())
    return jax.shard_map(shards, mesh=fine, in_specs=in_specs, out_specs=out_specs, check_vma=False)
```

time: 724 us -> 136 us (0.19)
  waiting for transfers between devices: 466 us -> 25.6 us
  blocking collectives: 141 us -> 29.7 us
  local copies, waits for them, and re-layouts: 29.8 us -> 1.98 us
  starting transfers between devices: 46.6 us -> 64.6 us
  matrix products: 14.8 us -> 0 us
  between operations: 14.8 us -> 0.99 us
  Pallas kernels: 0 us -> 12.1 us
  other arithmetic: 10.1 us -> 0 us
    psum x1 -> x0, waiting for transfers between devices: 442 us -> none  [shards(): w_total, v_total = lax.psum((w_sum, v_sum), ('sta', 'src'))]
    psum x2 -> x0, blocking collectives: 141 us -> none  [the longest x1 115 us: shards(): w_total, v_total = lax.psum((w_sum, v_sum), ('sta', 'src'))]
    all_to_all x0 -> x2, blocking collectives: none -> 29.7 us  [the longest x1 15.2 us: shards(): part = lax.all_to_all(pay.reshape(n_plane, per, channels), PLANE, 0, 0)]
    all_to_all x0 -> x2, starting transfers between devices: none -> 21.5 us  [the longest x1 14.7 us: shards(): part = lax.all_to_all(part, 'z', 0, 0)]
    dot_general x24 -> x0, matrix products: 14.8 us -> none  [the longest x8 5.07 us: apply_block(): jnp.dot(flat, matrix, preferred_element_type=jnp.float32)]
    pallas_call x0 -> x10, Pallas kernels: none -> 12.1 us  [the longest x7 7.96 us: call(): pl.pallas_call(body, out_shape=[jax.ShapeDtypeStruct(s, d) for s, d in ou...]
    unnamed x87 -> x22, local copies, waits for them, and re-layouts: 11.3 us -> 1.98 us
    all_to_all x0 -> x2, waiting for transfers between devices: none -> 8.89 us  [the longest x1 6.44 us: shards(): part = lax.all_to_all(part, PLANE, 0, 0)]
  transfers between devices with their start and end apart: 17 -> 18, of which waited for: 7 -> 7; matrix products, arithmetic and copies ran while one was open for 3% -> 0% of each run, Pallas kernels for 0% -> 4%
where the time goes in v1:
time: 136 us; the launch traced here: 135 us
  starting transfers between devices  64.6 us (47%)
  blocking collectives  29.7 us (22%)
  waiting for transfers between devices  25.6 us (19%)
  Pallas kernels  12.1 us (9%)
  local copies, waits for them, and re-layouts  1.98 us (1%)
    all_to_all x1, blocking collectives, shards(): part = lax.all_to_all(pay.reshape(n_plane, per, channels), PLANE, 0, 0)  15.2 us
    all_to_all x1, starting transfers between devices, shards(): part = lax.all_to_all(part, 'z', 0, 0)  14.7 us
    all_to_all x1, blocking collectives, shards(): total = lax.all_to_all(block, 'sta', 0, 0)  14.5 us
    ppermute x4, waiting for transfers between devices, halo(): from_right = lax.ppermute(left, SRC, [(b, a) for a, b in rights])  14.3 us
    ppermute x4, starting transfers between devices, halo(): from_up = lax.ppermute(hi, 'sta', ups)  13.5 us
    ppermute x4, starting transfers between devices, halo(): from_left = lax.ppermute(right, SRC, rights)  13.1 us
    ppermute x4, starting transfers between devices, halo(): from_down = lax.ppermute(lo, 'sta', [(b, a) for a, b in ups])  11.3 us
    pallas_call x7, Pallas kernels, call(): pl.pallas_call(body, out_shape=[jax.ShapeDtypeStruct(s, d) for s, d in ou...  7.96 us
  transfers between devices with their start and end apart: 18, of which 7 were waited for; matrix products, arithmetic and copies ran while one was open for 0% of the time, Pallas kernels for 4%

profile of v1, /device:TPU:1, one launch (start us, length us, event | category | flops | bytes accessed | tf_op | source)
XLA Modules:
  0.0 135.0 jit_solution(2302363897424292042)
XLA Ops:
  0.6 0.0 copy-start
  0.6 0.9 copy-done
  1.6 0.1 shard_map.120
  1.7 4.6 %collective-permute-start = (bf16[16,32,128]{2,1,0:T(8,128)(2,1)S(1)}, bf16[16,32,128]{2,1,0:T(8,128)(2,1)S(1)}, u32[]{:S(2)}, u32[]{:S(2)}) collective-permute-start(bf16[16,32,128]{2,1,0:T(8,128)(2,1)S(1)} %get-tuple-element.50), channel_id=1, source_target_pairs={{0,32},{32,64},{64,96},{96,128},{128,160},{160,192},{192,224},{224... | collective-permute-start | bytes 393224 | tf_op jit(solution)/shard_map/ppermute | solution.py:334
  6.3 5.5 %collective-permute-start.1 = (bf16[16,32,128]{2,1,0:T(8,128)(2,1)S(1)}, bf16[16,32,128]{2,1,0:T(8,128)(2,1)S(1)}, u32[]{:S(2)}, u32[]{:S(2)}) collective-permute-start(bf16[16,32,128]{2,1,0:T(8,128)(2,1)S(1)} %get-tuple-element.51), channel_id=1, source_target_pairs={{32,0},{64,32},{96,64},{128,96},{160,128},{192,160},{224,192},{256... | collective-permute-start | bytes 393224 | tf_op jit(solution)/shard_map/ppermute | solution.py:335
  11.8 1.3 collective-permute-start.2
  13.1 0.0 copy-start.8
  13.1 1.4 %collective-permute-start.3 = (bf16[32,16,128]{2,1,0:T(8,128)(2,1)S(1)}, bf16[32,16,128]{2,1,0:T(8,128)(2,1)S(1)}, u32[]{:S(2)}, u32[]{:S(2)}) collective-permute-start(bf16[32,16,128]{2,1,0:T(8,128)(2,1)S(1)} %get-tuple-element.53), channel_id=1, source_target_pairs={{1,0},{2,1},{3,2},{4,3},{5,4},{6,5},{7,6},{8,7},{9,8},{10,9},{11,1... | collective-permute-start | bytes 393224 | tf_op jit(solution)/shard_map/ppermute | solution.py:337
  14.5 0.1 copy.13.refs_0_
  14.6 0.0 copy-done.8
  14.7 0.0 copy-start.2
  14.7 0.0 copy-start.4
  14.7 0.0 copy-start.6
  14.7 0.2 copy.14.refs_2_
  14.9 0.0 copy-start.3
  14.9 0.0 copy-start.5
  14.9 0.0 copy-start.7
  14.9 0.6 copy-done.2
  15.6 0.0 copy-done.4
  15.6 0.0 copy-done.3
  15.6 0.0 copy-done.5
  15.6 2.9 %shard_map.121 = (bf16[512,1024]{1,0:T(8,128)(2,1)S(1)}, bf16[512,1024]{1,0:T(8,128)(2,1)S(1)}, bf16[128,256]{1,0:T(8,128)(2,1)S(1)}, bf16[128,256]{1,0:T(8,128)...) custom-call(s32[512,16]{1,0:T(8,128)S(1)} %copy.13.refs_0_, ...), custom_call_target="tpu_custom_call" | custom-call | tf_op jit(solution)/shard_map/pallas_call | solution.py:38
  18.5 0.0 collective-permute-done.up
  18.5 0.0 collective-permute-done.1.down
  18.5 0.0 collective-permute-done.2.left
  18.6 3.3 %collective-permute-done.3.right = bf16[32,16,128]{2,1,0:T(8,128)(2,1)S(1)} collective-permute-done((bf16[32,16,128]{2,1,0:T(8,128)(2,1)S(1)}, bf16[32,16,128]{2,1,0:T(8,128)(2,1)S(1)}, u32[]{:S(2)}, u32[]{:S(2)}) %collective-permute-start.3) | collective-permute-done | bytes 131104 | tf_op jit(solution)/shard_map/ppermute | solution.py:337
  21.8 1.4 %shard_map.122 = (bf16[32,32,128]{2,1,0:T(8,128)(2,1)S(1)}, bf16[16,32,128]{2,1,0:T(8,128)(2,1)S(1)}, bf16[16,32,128]{2,1,0:T(8,128)(2,1)S(1)}, bf16[32,16,128]{...) custom-call(bf16[32,32,128]{2,1,0:T(8,128)(2,1)S(1)} %copy-done.1, ...), custom_call_target="tpu_custom_call" | custom-call | tf_op jit(solution)/shard_map/pallas_call | solution.py:38
  23.2 3.6 %collective-permute-start.4 = (bf16[16,32,128]{2,1,0:T(8,128)(2,1)S(1)}, bf16[16,32,128]{2,1,0:T(8,128)(2,1)S(1)}, u32[]{:S(2)}, u32[]{:S(2)}) collective-permute-start(bf16[16,32,128]{2,1,0:T(8,128)(2,1)S(1)} %get-tuple-element.60), channel_id=1, source_target_pairs={{0,32},{32,64},{64,96},{96,128},{128,160},{160,192},{192,224},{224... | collective-permute-start | bytes 393224 | tf_op jit(solution)/shard_map/ppermute | solution.py:334
  26.8 1.9 %collective-permute-start.5 = (bf16[16,32,128]{2,1,0:T(8,128)(2,1)S(1)}, bf16[16,32,128]{2,1,0:T(8,128)(2,1)S(1)}, u32[]{:S(2)}, u32[]{:S(2)}) collective-permute-start(bf16[16,32,128]{2,1,0:T(8,128)(2,1)S(1)} %get-tuple-element.61), channel_id=1, source_target_pairs={{32,0},{64,32},{96,64},{128,96},{160,128},{192,160},{224,192},{256... | collective-permute-start | bytes 393224 | tf_op jit(solution)/shard_map/ppermute | solution.py:335
  28.7 4.4 %collective-permute-start.6 = (bf16[32,16,128]{2,1,0:T(8,128)(2,1)S(1)}, bf16[32,16,128]{2,1,0:T(8,128)(2,1)S(1)}, u32[]{:S(2)}, u32[]{:S(2)}) collective-permute-start(bf16[32,16,128]{2,1,0:T(8,128)(2,1)S(1)} %get-tuple-element.62), channel_id=1, source_target_pairs={{0,1},{1,2},{2,3},{3,4},{4,5},{5,6},{6,7},{7,8},{8,9},{9,10},{10,1... | collective-permute-start | bytes 393224 | tf_op jit(solution)/shard_map/ppermute | solution.py:336
  33.1 1.3 collective-permute-start.7
  34.4 0.0 collective-permute-done.4.up
  34.4 0.0 collective-permute-done.5.down
  34.4 0.6 collective-permute-done.6.left
  35.0 5.3 %collective-permute-done.7.right = bf16[32,16,128]{2,1,0:T(8,128)(2,1)S(1)} collective-permute-done((bf16[32,16,128]{2,1,0:T(8,128)(2,1)S(1)}, bf16[32,16,128]{2,1,0:T(8,128)(2,1)S(1)}, u32[]{:S(2)}, u32[]{:S(2)}) %collective-permute-start.7) | collective-permute-done | bytes 131104 | tf_op jit(solution)/shard_map/ppermute | solution.py:337
  40.3 1.5 %shard_map.123 = (bf16[32,32,384]{2,1,0:T(8,128)(2,1)S(1)}, f32[32,32,128]{2,1,0:T(8,128)S(1)}, f32[32,128]{1,0:T(8,128)S(1)}, f32[16,8,128]{2,1,0:T(8,128)S(1)}) custom-call(bf16[32,32,128]{2,1,0:T(8,128)(2,1)S(1)} %get-tuple-element.59.h, bf16[16,32,128]{2,1,0:T(8,128)(2,1)S(1)} %collective-permute-done.4.up, ...), custom_call_target="tpu_custom_call" | custom-call | tf_op jit(solution)/shard_map/pallas_call | solution.py:38
  41.8 14.5 %all_to_all.20.total = f32[16,8,128]{2,1,0:T(8,128)S(1)} all-to-all(f32[16,8,128]{2,1,0:T(8,128)S(1)} %get-tuple-element.67), channel_id=1, replica_groups=mesh['sta'=16,'z'=16,'xh'=2] {'sta'}, dimensions={0} | all-to-all | bytes 131072 | tf_op jit(solution)/shard_map/all_to_all | solution.py:396
  56.3 1.4 %shard_map.124 = (f32[2,32]{1,0:T(2,128)}, f32[32,32,128]{2,1,0:T(8,128)S(1)}, bf16[32,32,128]{2,1,0:T(8,128)(2,1)S(1)}, bf16[32,32,128]{2,1,0:T(8,128)(2,1)S(1)...) custom-call(f32[16,8,128]{2,1,0:T(8,128)S(1)} %all_to_all.20.total, ...), custom_call_target="tpu_custom_call" | custom-call | tf_op jit(solution)/shard_map/pallas_call | solution.py:320
  57.7 2.5 %collective-permute-start.8 = (bf16[16,32,128]{2,1,0:T(8,128)(2,1)S(1)}, bf16[16,32,128]{2,1,0:T(8,128)(2,1)S(1)}, u32[]{:S(2)}, u32[]{:S(2)}) collective-permute-start(bf16[16,32,128]{2,1,0:T(8,128)(2,1)S(1)} %get-tuple-element.77), channel_id=1, source_target_pairs={{0,32},{32,64},{64,96},{96,128},{128,160},{160,192},{192,224},{224... | collective-permute-start | bytes 393224 | tf_op jit(solution)/shard_map/ppermute | solution.py:334
  60.2 1.9 %collective-permute-start.9 = (bf16[16,32,128]{2,1,0:T(8,128)(2,1)S(1)}, bf16[16,32,128]{2,1,0:T(8,128)(2,1)S(1)}, u32[]{:S(2)}, u32[]{:S(2)}) collective-permute-start(bf16[16,32,128]{2,1,0:T(8,128)(2,1)S(1)} %get-tuple-element.78), channel_id=1, source_target_pairs={{32,0},{64,32},{96,64},{128,96},{160,128},{192,160},{224,192},{256... | collective-permute-start | bytes 393224 | tf_op jit(solution)/shard_map/ppermute | solution.py:335
  62.1 4.4 %collective-permute-start.10 = (bf16[32,16,128]{2,1,0:T(8,128)(2,1)S(1)}, bf16[32,16,128]{2,1,0:T(8,128)(2,1)S(1)}, u32[]{:S(2)}, u32[]{:S(2)}) collective-permute-start(bf16[32,16,128]{2,1,0:T(8,128)(2,1)S(1)} %get-tuple-element.79), channel_id=1, source_target_pairs={{0,1},{1,2},{2,3},{3,4},{4,5},{5,6},{6,7},{7,8},{8,9},{9,10},{10,1... | collective-permute-start | bytes 393224 | tf_op jit(solution)/shard_map/ppermute | solution.py:336
  66.5 1.3 collective-permute-start.11
  67.8 0.0 collective-permute-done.8.up
  67.8 0.0 collective-permute-done.9.down
  67.8 1.7 %collective-permute-done.10.left = bf16[32,16,128]{2,1,0:T(8,128)(2,1)S(1)} collective-permute-done((bf16[32,16,128]{2,1,0:T(8,128)(2,1)S(1)}, bf16[32,16,128]{2,1,0:T(8,128)(2,1)S(1)}, u32[]{:S(2)}, u32[]{:S(2)}) %collective-permute-start.10) | collective-permute-done | bytes 131104 | tf_op jit(solution)/shard_map/ppermute | solution.py:336
  69.5 5.8 %collective-permute-done.11.right = bf16[32,16,128]{2,1,0:T(8,128)(2,1)S(1)} collective-permute-done((bf16[32,16,128]{2,1,0:T(8,128)(2,1)S(1)}, bf16[32,16,128]{2,1,0:T(8,128)(2,1)S(1)}, u32[]{:S(2)}, u32[]{:S(2)}) %collective-permute-start.11) | collective-permute-done | bytes 131104 | tf_op jit(solution)/shard_map/ppermute | solution.py:337
  75.3 1.6 %shard_map.125 = (f32[32,32,128]{2,1,0:T(8,128)S(1)}, bf16[32,32,128]{2,1,0:T(8,128)(2,1)S(1)}, bf16[32,32,128]{2,1,0:T(8,128)(2,1)S(1)}, bf16[16,32,128]{2,1,0:...) custom-call(f32[32,32,128]{2,1,0:T(8,128)S(1)} %get-tuple-element.74, ...), custom_call_target="tpu_custom_call" | custom-call | tf_op jit(solution)/shard_map/pallas_call | solution.py:320
  76.9 15.2 %all_to_all.21.x = f32[32,8,128]{2,1,0:T(8,128)S(1)} all-to-all(f32[32,8,128]{2,1,0:T(8,128)S(1)} %bitcast.5), channel_id=1, replica_groups=mesh['sta'=16,'z'=16,'xh'=2] {'sta','xh'}, dimensions={0} | all-to-all | bytes 262144 | tf_op jit(solution)/shard_map/all_to_all | solution.py:435
  92.2 0.7 shard_map.127
  92.8 14.7 %all-to-all-start.2 = ((f32[16,8,128]{2,1,0:T(8,128)}), f32[16,8,128]{2,1,0:T(8,128)S(1)}, u32[]{:S(2)}, u32[]{:S(2)}) async-start(f32[16,8,128]{2,1,0:T(8,128)} %shard_map.127), calls=%async_computation.2 | async-start | bytes 131072 | tf_op jit(solution)/shard_map/all_to_all | solution.py:437
  107.5 2.9 %collective-permute-start.12 = (bf16[16,32,128]{2,1,0:T(8,128)(2,1)S(1)}, bf16[16,32,128]{2,1,0:T(8,128)(2,1)S(1)}, u32[]{:S(2)}, u32[]{:S(2)}) collective-permute-start(bf16[16,32,128]{2,1,0:T(8,128)(2,1)S(1)} %get-tuple-element.89), channel_id=1, source_target_pairs={{0,32},{32,64},{64,96},{96,128},{128,160},{160,192},{192,224},{224... | collective-permute-start | bytes 393224 | tf_op jit(solution)/shard_map/ppermute | solution.py:334
  110.4 1.9 %collective-permute-start.13 = (bf16[16,32,128]{2,1,0:T(8,128)(2,1)S(1)}, bf16[16,32,128]{2,1,0:T(8,128)(2,1)S(1)}, u32[]{:S(2)}, u32[]{:S(2)}) collective-permute-start(bf16[16,32,128]{2,1,0:T(8,128)(2,1)S(1)} %get-tuple-element.90), channel_id=1, source_target_pairs={{32,0},{64,32},{96,64},{128,96},{160,128},{192,160},{224,192},{256... | collective-permute-start | bytes 393224 | tf_op jit(solution)/shard_map/ppermute | solution.py:335
  112.3 3.0 %collective-permute-start.14 = (bf16[32,16,128]{2,1,0:T(8,128)(2,1)S(1)}, bf16[32,16,128]{2,1,0:T(8,128)(2,1)S(1)}, u32[]{:S(2)}, u32[]{:S(2)}) collective-permute-start(bf16[32,16,128]{2,1,0:T(8,128)(2,1)S(1)} %get-tuple-element.91), channel_id=1, source_target_pairs={{0,1},{1,2},{2,3},{3,4},{4,5},{5,6},{6,7},{7,8},{8,9},{9,10},{10,1... | collective-permute-start | bytes 393224 | tf_op jit(solution)/shard_map/ppermute | solution.py:336
  115.3 1.3 collective-permute-start.15
  116.6 2.4 %all-to-all-done.2.x = f32[16,8,128]{2,1,0:T(8,128)S(1)} async-done(((f32[16,8,128]{2,1,0:T(8,128)}), f32[16,8,128]{2,1,0:T(8,128)S(1)}, u32[]{:S(2)}, u32[]{:S(2)}) %all-to-all-start.2) | async-done | bytes 65568 | tf_op jit(solution)/shard_map/all_to_all | solution.py:437
  119.1 0.7 shard_map.128
  119.8 6.8 %all-to-all-start.3 = ((f32[32,8,128]{2,1,0:T(8,128)}), f32[32,8,128]{2,1,0:T(8,128)S(1)}, u32[]{:S(2)}, u32[]{:S(2)}) async-start(f32[32,8,128]{2,1,0:T(8,128)} %shard_map.128), calls=%async_computation.3 | async-start | bytes 262144 | tf_op jit(solution)/shard_map/all_to_all | solution.py:439
  126.6 0.0 collective-permute-done.12.up
  126.6 0.0 collective-permute-done.13.down
  126.6 0.0 collective-permute-done.14.left
  126.6 0.0 collective-permute-done.15.right
  126.6 1.2 shard_map.126
  127.8 6.4 %all-to-all-done.3.refs_0_ = f32[32,8,128]{2,1,0:T(8,128)S(1)} async-done(((f32[32,8,128]{2,1,0:T(8,128)}), f32[32,8,128]{2,1,0:T(8,128)S(1)}, u32[]{:S(2)}, u32[]{:S(2)}) %all-to-all-start.3) | async-done | bytes 131104 | tf_op jit(solution)/shard_map/all_to_all | solution.py:439
  134.3 0.8 shard_map.129
  (6 shorter events, 0.0 us)
Async XLA Ops:
  0.6 1.0 copy-start
  1.6 12.9 %copy-start.9 = (s32[512,16]{0,1:T(8,128)S(1)}, s32[512,16]{0,1:T(8,128)}, u32[]{:S(2)}) copy-start(s32[512,16]{0,1:T(8,128)} %param.10) | copy-start | bytes 98308
  1.7 16.9 %collective-permute-start = (bf16[16,32,128]{2,1,0:T(8,128)(2,1)S(1)}, bf16[16,32,128]{2,1,0:T(8,128)(2,1)S(1)}, u32[]{:S(2)}, u32[]{:S(2)}) collective-permute-start(bf16[16,32,128]{2,1,0:T(8,128)(2,1)S(1)} %get-tuple-element.50), channel_id=1, source_target_pairs={{0,32},{32,64},{64,96},{96,128},{128,160},{160,192},{192,224},{224... | collective-permute-start | bytes 393224 | tf_op jit(solution)/shard_map/ppermute | solution.py:334
  6.3 12.3 %collective-permute-start.1 = (bf16[16,32,128]{2,1,0:T(8,128)(2,1)S(1)}, bf16[16,32,128]{2,1,0:T(8,128)(2,1)S(1)}, u32[]{:S(2)}, u32[]{:S(2)}) collective-permute-start(bf16[16,32,128]{2,1,0:T(8,128)(2,1)S(1)} %get-tuple-element.51), channel_id=1, source_target_pairs={{32,0},{64,32},{96,64},{128,96},{160,128},{192,160},{224,192},{256... | collective-permute-start | bytes 393224 | tf_op jit(solution)/shard_map/ppermute | solution.py:335
  11.8 6.8 %collective-permute-start.2 = (bf16[32,16,128]{2,1,0:T(8,128)(2,1)S(1)}, bf16[32,16,128]{2,1,0:T(8,128)(2,1)S(1)}, u32[]{:S(2)}, u32[]{:S(2)}) collective-permute-start(bf16[32,16,128]{2,1,0:T(8,128)(2,1)S(1)} %get-tuple-element.52), channel_id=1, source_target_pairs={{0,1},{1,2},{2,3},{3,4},{4,5},{5,6},{6,7},{7,8},{8,9},{9,10},{10,1... | collective-permute-start | bytes 393224 | tf_op jit(solution)/shard_map/ppermute | solution.py:336
  13.1 1.6 %copy-start.8 = (s32[1024,16]{0,1:T(8,128)S(1)}, s32[1024,16]{0,1:T(8,128)}, u32[]{:S(2)}) copy-start(s32[1024,16]{0,1:T(8,128)} %param.12) | copy-start | bytes 196612
  13.1 8.7 %collective-permute-start.3 = (bf16[32,16,128]{2,1,0:T(8,128)(2,1)S(1)}, bf16[32,16,128]{2,1,0:T(8,128)(2,1)S(1)}, u32[]{:S(2)}, u32[]{:S(2)}) collective-permute-start(bf16[32,16,128]{2,1,0:T(8,128)(2,1)S(1)} %get-tuple-element.53), channel_id=1, source_target_pairs={{1,0},{2,1},{3,2},{4,3},{5,4},{6,5},{7,6},{8,7},{9,8},{10,9},{11,1... | collective-permute-start | bytes 393224 | tf_op jit(solution)/shard_map/ppermute | solution.py:337
  14.7 0.9 copy-start.2
  14.7 0.9 copy-start.4
  14.7 0.9 copy-start.6
  14.9 0.7 copy-start.3
  14.9 0.7 copy-start.5
  14.9 0.7 copy-start.7
  15.6 6.2 %copy-start.1 = (bf16[32,32,128]{2,1,0:T(8,128)(2,1)S(1)}, bf16[32,32,128]{2,1,0:T(8,128)(2,1)}, u32[]{:S(2)}) copy-start(bf16[32,32,128]{2,1,0:T(8,128)(2,1)} %h.1) | copy-start | bytes 786436
  23.2 11.2 %collective-permute-start.4 = (bf16[16,32,128]{2,1,0:T(8,128)(2,1)S(1)}, bf16[16,32,128]{2,1,0:T(8,128)(2,1)S(1)}, u32[]{:S(2)}, u32[]{:S(2)}) collective-permute-start(bf16[16,32,128]{2,1,0:T(8,128)(2,1)S(1)} %get-tuple-element.60), channel_id=1, source_target_pairs={{0,32},{32,64},{64,96},{96,128},{128,160},{160,192},{192,224},{224... | collective-permute-start | bytes 393224 | tf_op jit(solution)/shard_map/ppermute | solution.py:334
  26.8 7.6 %collective-permute-start.5 = (bf16[16,32,128]{2,1,0:T(8,128)(2,1)S(1)}, bf16[16,32,128]{2,1,0:T(8,128)(2,1)S(1)}, u32[]{:S(2)}, u32[]{:S(2)}) collective-permute-start(bf16[16,32,128]{2,1,0:T(8,128)(2,1)S(1)} %get-tuple-element.61), channel_id=1, source_target_pairs={{32,0},{64,32},{96,64},{128,96},{160,128},{192,160},{224,192},{256... | collective-permute-start | bytes 393224 | tf_op jit(solution)/shard_map/ppermute | solution.py:335
  28.7 6.3 %collective-permute-start.6 = (bf16[32,16,128]{2,1,0:T(8,128)(2,1)S(1)}, bf16[32,16,128]{2,1,0:T(8,128)(2,1)S(1)}, u32[]{:S(2)}, u32[]{:S(2)}) collective-permute-start(bf16[32,16,128]{2,1,0:T(8,128)(2,1)S(1)} %get-tuple-element.62), channel_id=1, source_target_pairs={{0,1},{1,2},{2,3},{3,4},{4,5},{5,6},{6,7},{7,8},{8,9},{9,10},{10,1... | collective-permute-start | bytes 393224 | tf_op jit(solution)/shard_map/ppermute | solution.py:336
  33.1 7.2 %collective-permute-start.7 = (bf16[32,16,128]{2,1,0:T(8,128)(2,1)S(1)}, bf16[32,16,128]{2,1,0:T(8,128)(2,1)S(1)}, u32[]{:S(2)}, u32[]{:S(2)}) collective-permute-start(bf16[32,16,128]{2,1,0:T(8,128)(2,1)S(1)} %get-tuple-element.63), channel_id=1, source_target_pairs={{1,0},{2,1},{3,2},{4,3},{5,4},{6,5},{7,6},{8,7},{9,8},{10,9},{11,1... | collective-permute-start | bytes 393224 | tf_op jit(solution)/shard_map/ppermute | solution.py:337
  57.7 10.1 %collective-permute-start.8 = (bf16[16,32,128]{2,1,0:T(8,128)(2,1)S(1)}, bf16[16,32,128]{2,1,0:T(8,128)(2,1)S(1)}, u32[]{:S(2)}, u32[]{:S(2)}) collective-permute-start(bf16[16,32,128]{2,1,0:T(8,128)(2,1)S(1)} %get-tuple-element.77), channel_id=1, source_target_pairs={{0,32},{32,64},{64,96},{96,128},{128,160},{160,192},{192,224},{224... | collective-permute-start | bytes 393224 | tf_op jit(solution)/shard_map/ppermute | solution.py:334
  60.2 7.6 %collective-permute-start.9 = (bf16[16,32,128]{2,1,0:T(8,128)(2,1)S(1)}, bf16[16,32,128]{2,1,0:T(8,128)(2,1)S(1)}, u32[]{:S(2)}, u32[]{:S(2)}) collective-permute-start(bf16[16,32,128]{2,1,0:T(8,128)(2,1)S(1)} %get-tuple-element.78), channel_id=1, source_target_pairs={{32,0},{64,32},{96,64},{128,96},{160,128},{192,160},{224,192},{256... | collective-permute-start | bytes 393224 | tf_op jit(solution)/shard_map/ppermute | solution.py:335
  62.1 7.4 %collective-permute-start.10 = (bf16[32,16,128]{2,1,0:T(8,128)(2,1)S(1)}, bf16[32,16,128]{2,1,0:T(8,128)(2,1)S(1)}, u32[]{:S(2)}, u32[]{:S(2)}) collective-permute-start(bf16[32,16,128]{2,1,0:T(8,128)(2,1)S(1)} %get-tuple-element.79), channel_id=1, source_target_pairs={{0,1},{1,2},{2,3},{3,4},{4,5},{5,6},{6,7},{7,8},{8,9},{9,10},{10,1... | collective-permute-start | bytes 393224 | tf_op jit(solution)/shard_map/ppermute | solution.py:336
  66.5 8.9 %collective-permute-start.11 = (bf16[32,16,128]{2,1,0:T(8,128)(2,1)S(1)}, bf16[32,16,128]{2,1,0:T(8,128)(2,1)S(1)}, u32[]{:S(2)}, u32[]{:S(2)}) collective-permute-start(bf16[32,16,128]{2,1,0:T(8,128)(2,1)S(1)} %get-tuple-element.80), channel_id=1, source_target_pairs={{1,0},{2,1},{3,2},{4,3},{5,4},{6,5},{7,6},{8,7},{9,8},{10,9},{11,1... | collective-permute-start | bytes 393224 | tf_op jit(solution)/shard_map/ppermute | solution.py:337
  92.8 26.2 %all-to-all-start.2 = ((f32[16,8,128]{2,1,0:T(8,128)}), f32[16,8,128]{2,1,0:T(8,128)S(1)}, u32[]{:S(2)}, u32[]{:S(2)}) async-start(f32[16,8,128]{2,1,0:T(8,128)} %shard_map.127), calls=%async_computation.2 | async-start | bytes 131072 | tf_op jit(solution)/shard_map/all_to_all | solution.py:437
  107.5 19.1 %collective-permute-start.12 = (bf16[16,32,128]{2,1,0:T(8,128)(2,1)S(1)}, bf16[16,32,128]{2,1,0:T(8,128)(2,1)S(1)}, u32[]{:S(2)}, u32[]{:S(2)}) collective-permute-start(bf16[16,32,128]{2,1,0:T(8,128)(2,1)S(1)} %get-tuple-element.89), channel_id=1, source_target_pairs={{0,32},{32,64},{64,96},{96,128},{128,160},{160,192},{192,224},{224... | collective-permute-start | bytes 393224 | tf_op jit(solution)/shard_map/ppermute | solution.py:334
  110.4 16.2 %collective-permute-start.13 = (bf16[16,32,128]{2,1,0:T(8,128)(2,1)S(1)}, bf16[16,32,128]{2,1,0:T(8,128)(2,1)S(1)}, u32[]{:S(2)}, u32[]{:S(2)}) collective-permute-start(bf16[16,32,128]{2,1,0:T(8,128)(2,1)S(1)} %get-tuple-element.90), channel_id=1, source_target_pairs={{32,0},{64,32},{96,64},{128,96},{160,128},{192,160},{224,192},{256... | collective-permute-start | bytes 393224 | tf_op jit(solution)/shard_map/ppermute | solution.py:335
  112.3 14.3 %collective-permute-start.14 = (bf16[32,16,128]{2,1,0:T(8,128)(2,1)S(1)}, bf16[32,16,128]{2,1,0:T(8,128)(2,1)S(1)}, u32[]{:S(2)}, u32[]{:S(2)}) collective-permute-start(bf16[32,16,128]{2,1,0:T(8,128)(2,1)S(1)} %get-tuple-element.91), channel_id=1, source_target_pairs={{0,1},{1,2},{2,3},{3,4},{4,5},{5,6},{6,7},{7,8},{8,9},{9,10},{10,1... | collective-permute-start | bytes 393224 | tf_op jit(solution)/shard_map/ppermute | solution.py:336
  115.3 11.3 %collective-permute-start.15 = (bf16[32,16,128]{2,1,0:T(8,128)(2,1)S(1)}, bf16[32,16,128]{2,1,0:T(8,128)(2,1)S(1)}, u32[]{:S(2)}, u32[]{:S(2)}) collective-permute-start(bf16[32,16,128]{2,1,0:T(8,128)(2,1)S(1)} %get-tuple-element.92), channel_id=1, source_target_pairs={{1,0},{2,1},{3,2},{4,3},{5,4},{6,5},{7,6},{8,7},{9,8},{10,9},{11,1... | collective-permute-start | bytes 393224 | tf_op jit(solution)/shard_map/ppermute | solution.py:337
  119.8 14.5 %all-to-all-start.3 = ((f32[32,8,128]{2,1,0:T(8,128)}), f32[32,8,128]{2,1,0:T(8,128)S(1)}, u32[]{:S(2)}, u32[]{:S(2)}) async-start(f32[32,8,128]{2,1,0:T(8,128)} %shard_map.128), calls=%async_computation.3 | async-start | bytes 262144 | tf_op jit(solution)/shard_map/all_to_all | solution.py:439

commit v2 on v1

--- a/solution.py
+++ b/solution.py
@@ -194,14 +194,14 @@
         yield cut, (before + t).astype(BF)
 
 
-def forward0_body(h, up, down, left, right, sk, rk, sinv, rinv, wf, nxt, hi, lo, rgt, lft, states, keep):
+def forward0_body(h, left, right, up, down, sk, rk, sinv, rinv, wf, nxt, hi, lo, rgt, lft, states, keep):
     cols = h.shape[1]
     for cut, after in forward_parts(h, up, down, left, right, sk, rk, sinv, rinv, wf, states, keep, 0):
         nxt[cut] = after.reshape(8, cols, 128)
     store_edges(nxt, nxt, hi, lo, rgt, lft)
 
 
-def forward1_body(h, up, down, left, right, sk, rk, sinv, rinv, wf, px, cnt, rl, states, keep, xsum, block):
+def forward1_body(h, left, right, up, down, sk, rk, sinv, rinv, wf, px, cnt, rl, states, keep, xsum, block):
     cols = h.shape[1]
     acc = jnp.zeros((cols, 128), F32)
     for cut, after in forward_parts(h, up, down, left, right, sk, rk, sinv, rinv, wf, states, keep, 1):
@@ -279,7 +279,7 @@
     return make
 
 
-def backward0_body(direct1, usta1, usrc1, up, down, left, right, tk, qk, q, states, wb, sinv, rinv, wpart, direct, usta, usrc, hi, lo, rgt, lft, pay, delta, hold):
+def backward0_body(direct1, usta1, usrc1, left, right, up, down, tk, qk, q, states, wb, sinv, rinv, wpart, direct, usta, usrc, hi, lo, rgt, lft, pay, delta, hold):
     make = gathered(direct1, usta1, usrc1, up, down, left, right, tk, qk, hold)
     pairs = backward_tail(make, q, states, wb, sinv, rinv, 0, delta, direct, usta, usrc, (hi, lo, rgt, lft))
     lane = iota((64, 128), 1) < 64
@@ -290,7 +290,7 @@
     pay[200:, :] = jnp.zeros((pay.shape[0] - 200, 128), F32)
 
 
-def last_body(direct, usta, usrc, up, down, left, right, tk, qk, out, hold):
+def last_body(direct, usta, usrc, left, right, up, down, tk, qk, out, hold):
     make = gathered(direct, usta, usrc, up, down, left, right, tk, qk, hold)
     cols = direct.shape[1]
     for p in range(direct.shape[0] // 8):
@@ -327,15 +327,23 @@
     )(*args)
 
 
+def shifts(axis):
+    count = 1
+    for name in axis if isinstance(axis, tuple) else (axis,):
+        count *= lax.axis_size(name)
+    ups = [(i, i + 1) for i in range(count - 1)]
+    return ups, [(b, a) for a, b in ups]
+
+
+def trade(high, low, axis):
+    ups, downs = shifts(axis)
+    return lax.ppermute(high, axis, ups), lax.ppermute(low, axis, downs)
+
+
 def halo(hi, lo, right, left):
-    sta, src = lax.axis_size("sta"), lax.axis_size("z") * lax.axis_size("xh")
-    ups = [(i, i + 1) for i in range(sta - 1)]
-    rights = [(i, i + 1) for i in range(src - 1)]
-    from_up = lax.ppermute(hi, "sta", ups)
-    from_down = lax.ppermute(lo, "sta", [(b, a) for a, b in ups])
-    from_left = lax.ppermute(right, SRC, rights)
-    from_right = lax.ppermute(left, SRC, [(b, a) for a, b in rights])
-    return from_up, from_down, from_left, from_right
+    from_left, from_right = trade(right, left, SRC)
+    from_up, from_down = trade(hi, lo, "sta")
+    return from_left, from_right, from_up, from_down
 
 
 def shards(features, station_lists, station_counts, source_lists, source_counts, picks, targets, layer_weights, readout_vector):
@@ -430,13 +438,30 @@
         rinv,
         wpart,
     )
-    got = halo(*edges)
-    (feature_grad,) = scratch_call(last_body, [(whole, BF)], [(whole, F32)], direct, usta, usrc, *got, tk, qk)
+    hi, lo, right, left = edges
+    from_left, from_right = trade(right, left, SRC)
     part = lax.all_to_all(pay.reshape(n_plane, per, channels), PLANE, 0, 0)
+    part, from_left, from_right, hi, lo = lax.optimization_barrier((part, from_left, from_right, hi, lo))
     (part,) = call(sum_body, [((n_z, per, channels), F32)], part)
     part = lax.all_to_all(part, "z", 0, 0)
+    from_up, from_down = trade(hi, lo, "sta")
+    part, from_up, from_down = lax.optimization_barrier((part, from_up, from_down))
     (part,) = call(sum_body, [((n_plane, per, channels), F32)], part)
     part = lax.all_to_all(part, PLANE, 0, 0)
+    (feature_grad,) = scratch_call(
+        last_body,
+        [(whole, BF)],
+        [(whole, F32)],
+        direct,
+        usta,
+        usrc,
+        from_left,
+        from_right,
+        from_up,
+        from_down,
+        tk,
+        qk,
+    )
     nodes = float(rows * n_sta * cols * lax.axis_size("z") * lax.axis_size("xh"))
     feature = layer_weights.shape[-1]
     weight_grad, vector_grad = call(

time: 136 us -> 145 us (1.066)
  starting transfers between devices: 64.6 us -> 75.4 us
  waiting for transfers between devices: 25.6 us -> 22.3 us
  blocking collectives: 29.7 us -> 31.3 us
    ppermute x16, starting transfers between devices: 43.1 us -> 50.1 us  [trade(): return (lax.ppermute(high, axis, ups), lax.ppermute(low, axis, downs))]
    all_to_all x1, starting transfers between devices: 14.7 us -> 19.6 us  [shards(): part = lax.all_to_all(part, 'z', 0, 0)]
    all_to_all x1, blocking collectives: 15.2 us -> 18.4 us  [shards(): part = lax.all_to_all(pay.reshape(n_plane, per, channels), PLANE, 0, 0)]
    ppermute x16, waiting for transfers between devices: 16.7 us -> 13.7 us  [trade(): return (lax.ppermute(high, axis, ups), lax.ppermute(low, axis, downs))]
    all_to_all x1, blocking collectives: 14.5 us -> 12.9 us  [shards(): total = lax.all_to_all(block, 'sta', 0, 0)]
  transfers between devices with their start and end apart: 18 -> 18, of which waited for: 7 -> 8; matrix products, arithmetic and copies ran while one was open for 0% -> 0% of each run, Pallas kernels for 4% -> 3%
where the time goes in v2:
time: 145 us; the launch traced here: 144 us
  starting transfers between devices  75.4 us (52%)
  blocking collectives  31.3 us (22%)
  waiting for transfers between devices  22.3 us (15%)
  Pallas kernels  12.2 us (8%)
  local copies, waits for them, and re-layouts  1.98 us (1%)
    ppermute x16, starting transfers between devices, trade(): return (lax.ppermute(high, axis, ups), lax.ppermute(low, axis, downs))  50.1 us
    all_to_all x1, starting transfers between devices, shards(): part = lax.all_to_all(part, 'z', 0, 0)  19.6 us
    all_to_all x1, blocking collectives, shards(): part = lax.all_to_all(pay.reshape(n_plane, per, channels), PLANE, 0, 0)  18.4 us
    ppermute x16, waiting for transfers between devices, trade(): return (lax.ppermute(high, axis, ups), lax.ppermute(low, axis, downs))  13.7 us
    all_to_all x1, blocking collectives, shards(): total = lax.all_to_all(block, 'sta', 0, 0)  12.9 us
    pallas_call x7, Pallas kernels, call(): pl.pallas_call(body, out_shape=[jax.ShapeDtypeStruct(s, d) for s, d in ou...  7.97 us
    all_to_all x1, waiting for transfers between devices, shards(): part = lax.all_to_all(part, PLANE, 0, 0)  6.55 us
    all_to_all x1, starting transfers between devices, shards(): part = lax.all_to_all(part, PLANE, 0, 0)  5.72 us
  transfers between devices with their start and end apart: 18, of which 8 were waited for; matrix products, arithmetic and copies ran while one was open for 0% of the time, Pallas kernels for 3%

profile of v2, /device:TPU:1, one launch (start us, length us, event | category | flops | bytes accessed | tf_op | source)
XLA Modules:
  0.0 144.2 jit_solution(4536014697466943316)
XLA Ops:
  0.6 0.0 copy-start
  0.6 0.9 copy-done
  1.6 0.1 shard_map.120
  1.7 5.5 %collective-permute-start = (bf16[32,16,128]{2,1,0:T(8,128)(2,1)S(1)}, bf16[32,16,128]{2,1,0:T(8,128)(2,1)S(1)}, u32[]{:S(2)}, u32[]{:S(2)}) collective-permute-start(bf16[32,16,128]{2,1,0:T(8,128)(2,1)S(1)} %get-tuple-element.58), channel_id=1, source_target_pairs={{0,1},{1,2},{2,3},{3,4},{4,5},{5,6},{6,7},{7,8},{8,9},{9,10},{10,1... | collective-permute-start | bytes 393224 | tf_op jit(solution)/shard_map/ppermute | solution.py:340
  7.2 1.3 collective-permute-start.1
  8.5 4.0 %collective-permute-start.2 = (bf16[16,32,128]{2,1,0:T(8,128)(2,1)S(1)}, bf16[16,32,128]{2,1,0:T(8,128)(2,1)S(1)}, u32[]{:S(2)}, u32[]{:S(2)}) collective-permute-start(bf16[16,32,128]{2,1,0:T(8,128)(2,1)S(1)} %get-tuple-element.60), channel_id=1, source_target_pairs={{0,32},{32,64},{64,96},{96,128},{128,160},{160,192},{192,224},{224... | collective-permute-start | bytes 393224 | tf_op jit(solution)/shard_map/ppermute | solution.py:340
  12.5 0.0 copy-start.8
  12.5 2.1 %collective-permute-start.3 = (bf16[16,32,128]{2,1,0:T(8,128)(2,1)S(1)}, bf16[16,32,128]{2,1,0:T(8,128)(2,1)S(1)}, u32[]{:S(2)}, u32[]{:S(2)}) collective-permute-start(bf16[16,32,128]{2,1,0:T(8,128)(2,1)S(1)} %get-tuple-element.61), channel_id=1, source_target_pairs={{32,0},{64,32},{96,64},{128,96},{160,128},{192,160},{224,192},{256... | collective-permute-start | bytes 393224 | tf_op jit(solution)/shard_map/ppermute | solution.py:340
  14.6 0.0 copy-done.9
  14.6 0.1 copy.13.refs_0_
  14.7 0.0 copy-done.8
  14.7 0.0 copy-start.2
  14.7 0.0 copy-start.4
  14.7 0.0 copy-start.6
  14.8 0.2 copy.14.refs_2_
  15.0 0.0 copy-start.3
  15.0 0.0 copy-start.5
  15.0 0.0 copy-start.7
  15.0 0.6 copy-done.2
  15.6 0.0 copy-done.3
  15.7 0.0 copy-done.5
  15.7 2.9 %shard_map.121 = (bf16[512,1024]{1,0:T(8,128)(2,1)S(1)}, bf16[512,1024]{1,0:T(8,128)(2,1)S(1)}, bf16[128,256]{1,0:T(8,128)(2,1)S(1)}, bf16[128,256]{1,0:T(8,128)...) custom-call(s32[512,16]{1,0:T(8,128)S(1)} %copy.13.refs_0_, ...), custom_call_target="tpu_custom_call" | custom-call | tf_op jit(solution)/shard_map/pallas_call | solution.py:38
  18.6 0.0 collective-permute-done.left
  18.6 0.0 collective-permute-done.1.right
  18.6 0.0 collective-permute-done.2.up
  18.6 0.3 collective-permute-done.3.down
  18.9 1.4 shard_map.122
  20.3 5.8 %collective-permute-start.4 = (bf16[32,16,128]{2,1,0:T(8,128)(2,1)S(1)}, bf16[32,16,128]{2,1,0:T(8,128)(2,1)S(1)}, u32[]{:S(2)}, u32[]{:S(2)}) collective-permute-start(bf16[32,16,128]{2,1,0:T(8,128)(2,1)S(1)} %get-tuple-element.68), channel_id=1, source_target_pairs={{0,1},{1,2},{2,3},{3,4},{4,5},{5,6},{6,7},{7,8},{8,9},{9,10},{10,1... | collective-permute-start | bytes 393224 | tf_op jit(solution)/shard_map/ppermute | solution.py:340
  26.1 1.3 collective-permute-start.5
  27.4 3.6 %collective-permute-start.6 = (bf16[16,32,128]{2,1,0:T(8,128)(2,1)S(1)}, bf16[16,32,128]{2,1,0:T(8,128)(2,1)S(1)}, u32[]{:S(2)}, u32[]{:S(2)}) collective-permute-start(bf16[16,32,128]{2,1,0:T(8,128)(2,1)S(1)} %get-tuple-element.70), channel_id=1, source_target_pairs={{0,32},{32,64},{64,96},{96,128},{128,160},{160,192},{192,224},{224... | collective-permute-start | bytes 393224 | tf_op jit(solution)/shard_map/ppermute | solution.py:340
  31.1 1.9 %collective-permute-start.7 = (bf16[16,32,128]{2,1,0:T(8,128)(2,1)S(1)}, bf16[16,32,128]{2,1,0:T(8,128)(2,1)S(1)}, u32[]{:S(2)}, u32[]{:S(2)}) collective-permute-start(bf16[16,32,128]{2,1,0:T(8,128)(2,1)S(1)} %get-tuple-element.71), channel_id=1, source_target_pairs={{32,0},{64,32},{96,64},{128,96},{160,128},{192,160},{224,192},{256... | collective-permute-start | bytes 393224 | tf_op jit(solution)/shard_map/ppermute | solution.py:340
  33.0 0.0 collective-permute-done.4.left
  33.0 1.6 %collective-permute-done.5.right = bf16[32,16,128]{2,1,0:T(8,128)(2,1)S(1)} collective-permute-done((bf16[32,16,128]{2,1,0:T(8,128)(2,1)S(1)}, bf16[32,16,128]{2,1,0:T(8,128)(2,1)S(1)}, u32[]{:S(2)}, u32[]{:S(2)}) %collective-permute-start.5) | collective-permute-done | bytes 131104 | tf_op jit(solution)/shard_map/ppermute | solution.py:340
  34.6 0.0 collective-permute-done.6.up
  34.6 2.8 %collective-permute-done.7.down = bf16[16,32,128]{2,1,0:T(8,128)(2,1)S(1)} collective-permute-done((bf16[16,32,128]{2,1,0:T(8,128)(2,1)S(1)}, bf16[16,32,128]{2,1,0:T(8,128)(2,1)S(1)}, u32[]{:S(2)}, u32[]{:S(2)}) %collective-permute-start.7) | collective-permute-done | bytes 131104 | tf_op jit(solution)/shard_map/ppermute | solution.py:340
  37.3 1.5 %shard_map.123 = (bf16[32,32,384]{2,1,0:T(8,128)(2,1)S(1)}, f32[32,32,128]{2,1,0:T(8,128)S(1)}, f32[32,128]{1,0:T(8,128)S(1)}, f32[16,8,128]{2,1,0:T(8,128)S(1)}) custom-call(bf16[32,32,128]{2,1,0:T(8,128)(2,1)S(1)} %get-tuple-element.67.h, bf16[32,16,128]{2,1,0:T(8,128)(2,1)S(1)} %collective-permute-done.4.left, ...), custom_call_target="tpu_custom_call" | custom-call | tf_op jit(solution)/shard_map/pallas_call | solution.py:38
  38.8 12.9 %all_to_all.20.total = f32[16,8,128]{2,1,0:T(8,128)S(1)} all-to-all(f32[16,8,128]{2,1,0:T(8,128)S(1)} %get-tuple-element.75), channel_id=1, replica_groups=mesh['sta'=16,'z'=16,'xh'=2] {'sta'}, dimensions={0} | all-to-all | bytes 131072 | tf_op jit(solution)/shard_map/all_to_all | solution.py:404
  51.8 1.4 shard_map.124
  53.2 6.5 %collective-permute-start.8 = (bf16[32,16,128]{2,1,0:T(8,128)(2,1)S(1)}, bf16[32,16,128]{2,1,0:T(8,128)(2,1)S(1)}, u32[]{:S(2)}, u32[]{:S(2)}) collective-permute-start(bf16[32,16,128]{2,1,0:T(8,128)(2,1)S(1)} %get-tuple-element.85), channel_id=1, source_target_pairs={{0,1},{1,2},{2,3},{3,4},{4,5},{5,6},{6,7},{7,8},{8,9},{9,10},{10,1... | collective-permute-start | bytes 393224 | tf_op jit(solution)/shard_map/ppermute | solution.py:340
  59.7 1.3 collective-permute-start.9
  61.0 2.8 %collective-permute-start.10 = (bf16[16,32,128]{2,1,0:T(8,128)(2,1)S(1)}, bf16[16,32,128]{2,1,0:T(8,128)(2,1)S(1)}, u32[]{:S(2)}, u32[]{:S(2)}) collective-permute-start(bf16[16,32,128]{2,1,0:T(8,128)(2,1)S(1)} %get-tuple-element.87), channel_id=1, source_target_pairs={{0,32},{32,64},{64,96},{96,128},{128,160},{160,192},{192,224},{224... | collective-permute-start | bytes 393224 | tf_op jit(solution)/shard_map/ppermute | solution.py:340
  63.7 1.9 %collective-permute-start.11 = (bf16[16,32,128]{2,1,0:T(8,128)(2,1)S(1)}, bf16[16,32,128]{2,1,0:T(8,128)(2,1)S(1)}, u32[]{:S(2)}, u32[]{:S(2)}) collective-permute-start(bf16[16,32,128]{2,1,0:T(8,128)(2,1)S(1)} %get-tuple-element.88), channel_id=1, source_target_pairs={{32,0},{64,32},{96,64},{128,96},{160,128},{192,160},{224,192},{256... | collective-permute-start | bytes 393224 | tf_op jit(solution)/shard_map/ppermute | solution.py:340
  65.7 0.0 collective-permute-done.8.left
  65.7 2.6 %collective-permute-done.9.right = bf16[32,16,128]{2,1,0:T(8,128)(2,1)S(1)} collective-permute-done((bf16[32,16,128]{2,1,0:T(8,128)(2,1)S(1)}, bf16[32,16,128]{2,1,0:T(8,128)(2,1)S(1)}, u32[]{:S(2)}, u32[]{:S(2)}) %collective-permute-start.9) | collective-permute-done | bytes 131104 | tf_op jit(solution)/shard_map/ppermute | solution.py:340
  68.3 0.0 collective-permute-done.10.up
  68.3 1.7 %collective-permute-done.11.down = bf16[16,32,128]{2,1,0:T(8,128)(2,1)S(1)} collective-permute-done((bf16[16,32,128]{2,1,0:T(8,128)(2,1)S(1)}, bf16[16,32,128]{2,1,0:T(8,128)(2,1)S(1)}, u32[]{:S(2)}, u32[]{:S(2)}) %collective-permute-start.11) | collective-permute-done | bytes 131104 | tf_op jit(solution)/shard_map/ppermute | solution.py:340
  70.0 1.6 %shard_map.125 = (f32[32,32,128]{2,1,0:T(8,128)S(1)}, bf16[32,32,128]{2,1,0:T(8,128)(2,1)S(1)}, bf16[32,32,128]{2,1,0:T(8,128)(2,1)S(1)}, bf16[16,32,128]{2,1,0:...) custom-call(f32[32,32,128]{2,1,0:T(8,128)S(1)} %get-tuple-element.82, ...), custom_call_target="tpu_custom_call" | custom-call | tf_op jit(solution)/shard_map/pallas_call | solution.py:320
  71.6 6.1 %collective-permute-start.12 = (bf16[32,16,128]{2,1,0:T(8,128)(2,1)S(1)}, bf16[32,16,128]{2,1,0:T(8,128)(2,1)S(1)}, u32[]{:S(2)}, u32[]{:S(2)}) collective-permute-start(bf16[32,16,128]{2,1,0:T(8,128)(2,1)S(1)} %get-tuple-element.98), channel_id=1, source_target_pairs={{0,1},{1,2},{2,3},{3,4},{4,5},{5,6},{6,7},{7,8},{8,9},{9,10},{10,1... | collective-permute-start | bytes 393224 | tf_op jit(solution)/shard_map/ppermute | solution.py:340
  77.7 1.3 collective-permute-start.13
  79.0 18.4 %all_to_all.21.x = f32[32,8,128]{2,1,0:T(8,128)S(1)} all-to-all(f32[32,8,128]{2,1,0:T(8,128)S(1)} %bitcast.5), channel_id=1, replica_groups=mesh['sta'=16,'z'=16,'xh'=2] {'sta','xh'}, dimensions={0} | all-to-all | bytes 262144 | tf_op jit(solution)/shard_map/all_to_all | solution.py:443
  97.4 0.0 collective-permute-done.12.left
  97.4 0.0 collective-permute-done.13.right
  97.4 0.7 shard_map.126
  98.0 19.6 %all-to-all-start.2 = ((f32[16,8,128]{2,1,0:T(8,128)}), f32[16,8,128]{2,1,0:T(8,128)S(1)}, u32[]{:S(2)}, u32[]{:S(2)}) async-start(f32[16,8,128]{2,1,0:T(8,128)} %shard_map.126), calls=%async_computation.2 | async-start | bytes 131072 | tf_op jit(solution)/shard_map/all_to_all | solution.py:446
  117.6 2.9 %collective-permute-start.14 = (bf16[16,32,128]{2,1,0:T(8,128)(2,1)S(1)}, bf16[16,32,128]{2,1,0:T(8,128)(2,1)S(1)}, u32[]{:S(2)}, u32[]{:S(2)}) collective-permute-start(bf16[16,32,128]{2,1,0:T(8,128)(2,1)S(1)} %get-tuple-element.105), channel_id=1, source_target_pairs={{0,32},{32,64},{64,96},{96,128},{128,160},{160,192},{192,224},{224... | collective-permute-start | bytes 393224 | tf_op jit(solution)/shard_map/ppermute | solution.py:340
  120.5 1.9 %collective-permute-start.15 = (bf16[16,32,128]{2,1,0:T(8,128)(2,1)S(1)}, bf16[16,32,128]{2,1,0:T(8,128)(2,1)S(1)}, u32[]{:S(2)}, u32[]{:S(2)}) collective-permute-start(bf16[16,32,128]{2,1,0:T(8,128)(2,1)S(1)} %get-tuple-element.106), channel_id=1, source_target_pairs={{32,0},{64,32},{96,64},{128,96},{160,128},{192,160},{224,192},{256... | collective-permute-start | bytes 393224 | tf_op jit(solution)/shard_map/ppermute | solution.py:340
  122.4 0.0 collective-permute-done.14.up
  122.4 4.6 %collective-permute-done.15.down = bf16[16,32,128]{2,1,0:T(8,128)(2,1)S(1)} collective-permute-done((bf16[16,32,128]{2,1,0:T(8,128)(2,1)S(1)}, bf16[16,32,128]{2,1,0:T(8,128)(2,1)S(1)}, u32[]{:S(2)}, u32[]{:S(2)}) %collective-permute-start.15) | collective-permute-done | bytes 131104 | tf_op jit(solution)/shard_map/ppermute | solution.py:340
  127.1 2.1 %all-to-all-done.2.x = f32[16,8,128]{2,1,0:T(8,128)S(1)} async-done(((f32[16,8,128]{2,1,0:T(8,128)}), f32[16,8,128]{2,1,0:T(8,128)S(1)}, u32[]{:S(2)}, u32[]{:S(2)}) %all-to-all-start.2) | async-done | bytes 65568 | tf_op jit(solution)/shard_map/all_to_all | solution.py:446
  129.2 0.7 shard_map.128
  129.9 5.7 %all-to-all-start.3 = ((f32[32,8,128]{2,1,0:T(8,128)}), f32[32,8,128]{2,1,0:T(8,128)S(1)}, u32[]{:S(2)}, u32[]{:S(2)}) async-start(f32[32,8,128]{2,1,0:T(8,128)} %shard_map.128), calls=%async_computation.3 | async-start | bytes 262144 | tf_op jit(solution)/shard_map/all_to_all | solution.py:450
  135.6 1.2 shard_map.127
  136.8 6.6 %all-to-all-done.3.refs_0_ = f32[32,8,128]{2,1,0:T(8,128)S(1)} async-done(((f32[32,8,128]{2,1,0:T(8,128)}), f32[32,8,128]{2,1,0:T(8,128)S(1)}, u32[]{:S(2)}, u32[]{:S(2)}) %all-to-all-start.3) | async-done | bytes 131104 | tf_op jit(solution)/shard_map/all_to_all | solution.py:450
  143.4 0.8 shard_map.129
  (6 shorter events, 0.0 us)
Async XLA Ops:
  0.6 1.0 copy-start
  1.6 13.0 %copy-start.9 = (s32[512,16]{0,1:T(8,128)S(1)}, s32[512,16]{0,1:T(8,128)}, u32[]{:S(2)}) copy-start(s32[512,16]{0,1:T(8,128)} %param.10) | copy-start | bytes 98308
  1.7 16.9 %collective-permute-start = (bf16[32,16,128]{2,1,0:T(8,128)(2,1)S(1)}, bf16[32,16,128]{2,1,0:T(8,128)(2,1)S(1)}, u32[]{:S(2)}, u32[]{:S(2)}) collective-permute-start(bf16[32,16,128]{2,1,0:T(8,128)(2,1)S(1)} %get-tuple-element.58), channel_id=1, source_target_pairs={{0,1},{1,2},{2,3},{3,4},{4,5},{5,6},{6,7},{7,8},{8,9},{9,10},{10,1... | collective-permute-start | bytes 393224 | tf_op jit(solution)/shard_map/ppermute | solution.py:340
  7.2 11.5 %collective-permute-start.1 = (bf16[32,16,128]{2,1,0:T(8,128)(2,1)S(1)}, bf16[32,16,128]{2,1,0:T(8,128)(2,1)S(1)}, u32[]{:S(2)}, u32[]{:S(2)}) collective-permute-start(bf16[32,16,128]{2,1,0:T(8,128)(2,1)S(1)} %get-tuple-element.59), channel_id=1, source_target_pairs={{1,0},{2,1},{3,2},{4,3},{5,4},{6,5},{7,6},{8,7},{9,8},{10,9},{11,1... | collective-permute-start | bytes 393224 | tf_op jit(solution)/shard_map/ppermute | solution.py:340
  8.5 10.2 %collective-permute-start.2 = (bf16[16,32,128]{2,1,0:T(8,128)(2,1)S(1)}, bf16[16,32,128]{2,1,0:T(8,128)(2,1)S(1)}, u32[]{:S(2)}, u32[]{:S(2)}) collective-permute-start(bf16[16,32,128]{2,1,0:T(8,128)(2,1)S(1)} %get-tuple-element.60), channel_id=1, source_target_pairs={{0,32},{32,64},{64,96},{96,128},{128,160},{160,192},{192,224},{224... | collective-permute-start | bytes 393224 | tf_op jit(solution)/shard_map/ppermute | solution.py:340
  12.5 2.2 %copy-start.8 = (s32[1024,16]{0,1:T(8,128)S(1)}, s32[1024,16]{0,1:T(8,128)}, u32[]{:S(2)}) copy-start(s32[1024,16]{0,1:T(8,128)} %param.12) | copy-start | bytes 196612
  12.5 6.4 %collective-permute-start.3 = (bf16[16,32,128]{2,1,0:T(8,128)(2,1)S(1)}, bf16[16,32,128]{2,1,0:T(8,128)(2,1)S(1)}, u32[]{:S(2)}, u32[]{:S(2)}) collective-permute-start(bf16[16,32,128]{2,1,0:T(8,128)(2,1)S(1)} %get-tuple-element.61), channel_id=1, source_target_pairs={{32,0},{64,32},{96,64},{128,96},{160,128},{192,160},{224,192},{256... | collective-permute-start | bytes 393224 | tf_op jit(solution)/shard_map/ppermute | solution.py:340
  14.7 0.9 copy-start.2
  14.7 0.9 copy-start.4
  14.7 0.9 copy-start.6
  15.0 0.7 copy-start.3
  15.0 0.7 copy-start.5
  15.0 0.7 copy-start.7
  15.7 3.3 %copy-start.1 = (bf16[32,32,128]{2,1,0:T(8,128)(2,1)S(1)}, bf16[32,32,128]{2,1,0:T(8,128)(2,1)}, u32[]{:S(2)}) copy-start(bf16[32,32,128]{2,1,0:T(8,128)(2,1)} %h.1) | copy-start | bytes 786436
  20.3 12.7 %collective-permute-start.4 = (bf16[32,16,128]{2,1,0:T(8,128)(2,1)S(1)}, bf16[32,16,128]{2,1,0:T(8,128)(2,1)S(1)}, u32[]{:S(2)}, u32[]{:S(2)}) collective-permute-start(bf16[32,16,128]{2,1,0:T(8,128)(2,1)S(1)} %get-tuple-element.68), channel_id=1, source_target_pairs={{0,1},{1,2},{2,3},{3,4},{4,5},{5,6},{6,7},{7,8},{8,9},{9,10},{10,1... | collective-permute-start | bytes 393224 | tf_op jit(solution)/shard_map/ppermute | solution.py:340
  26.1 8.4 %collective-permute-start.5 = (bf16[32,16,128]{2,1,0:T(8,128)(2,1)S(1)}, bf16[32,16,128]{2,1,0:T(8,128)(2,1)S(1)}, u32[]{:S(2)}, u32[]{:S(2)}) collective-permute-start(bf16[32,16,128]{2,1,0:T(8,128)(2,1)S(1)} %get-tuple-element.69), channel_id=1, source_target_pairs={{1,0},{2,1},{3,2},{4,3},{5,4},{6,5},{7,6},{8,7},{9,8},{10,9},{11,1... | collective-permute-start | bytes 393224 | tf_op jit(solution)/shard_map/ppermute | solution.py:340
  27.4 7.2 %collective-permute-start.6 = (bf16[16,32,128]{2,1,0:T(8,128)(2,1)S(1)}, bf16[16,32,128]{2,1,0:T(8,128)(2,1)S(1)}, u32[]{:S(2)}, u32[]{:S(2)}) collective-permute-start(bf16[16,32,128]{2,1,0:T(8,128)(2,1)S(1)} %get-tuple-element.70), channel_id=1, source_target_pairs={{0,32},{32,64},{64,96},{96,128},{128,160},{160,192},{192,224},{224... | collective-permute-start | bytes 393224 | tf_op jit(solution)/shard_map/ppermute | solution.py:340
  31.1 6.3 %collective-permute-start.7 = (bf16[16,32,128]{2,1,0:T(8,128)(2,1)S(1)}, bf16[16,32,128]{2,1,0:T(8,128)(2,1)S(1)}, u32[]{:S(2)}, u32[]{:S(2)}) collective-permute-start(bf16[16,32,128]{2,1,0:T(8,128)(2,1)S(1)} %get-tuple-element.71), channel_id=1, source_target_pairs={{32,0},{64,32},{96,64},{128,96},{160,128},{192,160},{224,192},{256... | collective-permute-start | bytes 393224 | tf_op jit(solution)/shard_map/ppermute | solution.py:340
  53.2 12.5 %collective-permute-start.8 = (bf16[32,16,128]{2,1,0:T(8,128)(2,1)S(1)}, bf16[32,16,128]{2,1,0:T(8,128)(2,1)S(1)}, u32[]{:S(2)}, u32[]{:S(2)}) collective-permute-start(bf16[32,16,128]{2,1,0:T(8,128)(2,1)S(1)} %get-tuple-element.85), channel_id=1, source_target_pairs={{0,1},{1,2},{2,3},{3,4},{4,5},{5,6},{6,7},{7,8},{8,9},{9,10},{10,1... | collective-permute-start | bytes 393224 | tf_op jit(solution)/shard_map/ppermute | solution.py:340
  59.7 8.6 %collective-permute-start.9 = (bf16[32,16,128]{2,1,0:T(8,128)(2,1)S(1)}, bf16[32,16,128]{2,1,0:T(8,128)(2,1)S(1)}, u32[]{:S(2)}, u32[]{:S(2)}) collective-permute-start(bf16[32,16,128]{2,1,0:T(8,128)(2,1)S(1)} %get-tuple-element.86), channel_id=1, source_target_pairs={{1,0},{2,1},{3,2},{4,3},{5,4},{6,5},{7,6},{8,7},{9,8},{10,9},{11,1... | collective-permute-start | bytes 393224 | tf_op jit(solution)/shard_map/ppermute | solution.py:340
  61.0 7.3 %collective-permute-start.10 = (bf16[16,32,128]{2,1,0:T(8,128)(2,1)S(1)}, bf16[16,32,128]{2,1,0:T(8,128)(2,1)S(1)}, u32[]{:S(2)}, u32[]{:S(2)}) collective-permute-start(bf16[16,32,128]{2,1,0:T(8,128)(2,1)S(1)} %get-tuple-element.87), channel_id=1, source_target_pairs={{0,32},{32,64},{64,96},{96,128},{128,160},{160,192},{192,224},{224... | collective-permute-start | bytes 393224 | tf_op jit(solution)/shard_map/ppermute | solution.py:340
  63.7 6.3 %collective-permute-start.11 = (bf16[16,32,128]{2,1,0:T(8,128)(2,1)S(1)}, bf16[16,32,128]{2,1,0:T(8,128)(2,1)S(1)}, u32[]{:S(2)}, u32[]{:S(2)}) collective-permute-start(bf16[16,32,128]{2,1,0:T(8,128)(2,1)S(1)} %get-tuple-element.88), channel_id=1, source_target_pairs={{32,0},{64,32},{96,64},{128,96},{160,128},{192,160},{224,192},{256... | collective-permute-start | bytes 393224 | tf_op jit(solution)/shard_map/ppermute | solution.py:340
  71.6 25.8 %collective-permute-start.12 = (bf16[32,16,128]{2,1,0:T(8,128)(2,1)S(1)}, bf16[32,16,128]{2,1,0:T(8,128)(2,1)S(1)}, u32[]{:S(2)}, u32[]{:S(2)}) collective-permute-start(bf16[32,16,128]{2,1,0:T(8,128)(2,1)S(1)} %get-tuple-element.98), channel_id=1, source_target_pairs={{0,1},{1,2},{2,3},{3,4},{4,5},{5,6},{6,7},{7,8},{8,9},{9,10},{10,1... | collective-permute-start | bytes 393224 | tf_op jit(solution)/shard_map/ppermute | solution.py:340
  77.7 19.7 %collective-permute-start.13 = (bf16[32,16,128]{2,1,0:T(8,128)(2,1)S(1)}, bf16[32,16,128]{2,1,0:T(8,128)(2,1)S(1)}, u32[]{:S(2)}, u32[]{:S(2)}) collective-permute-start(bf16[32,16,128]{2,1,0:T(8,128)(2,1)S(1)} %get-tuple-element.99), channel_id=1, source_target_pairs={{1,0},{2,1},{3,2},{4,3},{5,4},{6,5},{7,6},{8,7},{9,8},{10,9},{11,1... | collective-permute-start | bytes 393224 | tf_op jit(solution)/shard_map/ppermute | solution.py:340
  98.0 31.2 %all-to-all-start.2 = ((f32[16,8,128]{2,1,0:T(8,128)}), f32[16,8,128]{2,1,0:T(8,128)S(1)}, u32[]{:S(2)}, u32[]{:S(2)}) async-start(f32[16,8,128]{2,1,0:T(8,128)} %shard_map.126), calls=%async_computation.2 | async-start | bytes 131072 | tf_op jit(solution)/shard_map/all_to_all | solution.py:446
  117.6 4.8 %collective-permute-start.14 = (bf16[16,32,128]{2,1,0:T(8,128)(2,1)S(1)}, bf16[16,32,128]{2,1,0:T(8,128)(2,1)S(1)}, u32[]{:S(2)}, u32[]{:S(2)}) collective-permute-start(bf16[16,32,128]{2,1,0:T(8,128)(2,1)S(1)} %get-tuple-element.105), channel_id=1, source_target_pairs={{0,32},{32,64},{64,96},{96,128},{128,160},{160,192},{192,224},{224... | collective-permute-start | bytes 393224 | tf_op jit(solution)/shard_map/ppermute | solution.py:340
  120.5 6.6 %collective-permute-start.15 = (bf16[16,32,128]{2,1,0:T(8,128)(2,1)S(1)}, bf16[16,32,128]{2,1,0:T(8,128)(2,1)S(1)}, u32[]{:S(2)}, u32[]{:S(2)}) collective-permute-start(bf16[16,32,128]{2,1,0:T(8,128)(2,1)S(1)} %get-tuple-element.106), channel_id=1, source_target_pairs={{32,0},{64,32},{96,64},{128,96},{160,128},{192,160},{224,192},{256... | collective-permute-start | bytes 393224 | tf_op jit(solution)/shard_map/ppermute | solution.py:340
  129.9 13.5 %all-to-all-start.3 = ((f32[32,8,128]{2,1,0:T(8,128)}), f32[32,8,128]{2,1,0:T(8,128)S(1)}, u32[]{:S(2)}, u32[]{:S(2)}) async-start(f32[32,8,128]{2,1,0:T(8,128)} %shard_map.128), calls=%async_computation.3 | async-start | bytes 262144 | tf_op jit(solution)/shard_map/all_to_all | solution.py:450

commit v3 on v1

v3 whole, which is shorter than its diff:
```python
import jax
import jax.numpy as jnp
from jax import lax
from jax.experimental import pallas as pl
from jax.experimental.pallas import tpu as pltpu
from jax.sharding import Mesh
from jax.sharding import PartitionSpec as P

LAYERS = 2
HW = 16
BF = jnp.bfloat16
F32 = jnp.float32
PLANE = ("sta", "xh")
SRC = ("z", "xh")
NT = (((1,), (1,)), ((), ()))
TN = (((0,), (0,)), ((), ()))
VMEM_LIMIT = 16 * 1024 * 1024


def iota(shape, dim):
    return lax.broadcasted_iota(jnp.int32, shape, dim)


def dot(a, b):
    return jnp.dot(a, b, preferred_element_type=F32)


def dot_nt(a, b, precision=None):
    return lax.dot_general(a, b, NT, precision=precision, preferred_element_type=F32)


def onehot(mask):
    return jnp.where(mask, 1.0, 0.0).astype(BF)


def call(body, outs, *args):
    vm = pl.BlockSpec(memory_space=pltpu.VMEM)
    return pl.pallas_call(
        body,
        out_shape=[jax.ShapeDtypeStruct(s, d) for s, d in outs],
        in_specs=[vm] * len(args),
        out_specs=[vm] * len(outs),
        compiler_params=pltpu.CompilerParams(vmem_limit_bytes=VMEM_LIMIT),
    )(*args)


def even(axis):
    at = jnp.int32(0)
    for name in axis if isinstance(axis, tuple) else (axis,):
        at = at * lax.axis_size(name) + lax.axis_index(name)
    return (at & 1) == 0, at


def offsets(spot, own, flag):
    jump = own + HW
    first = jnp.where(flag, spot, spot - jump)
    second = jnp.where(flag, spot - HW - jump, spot - HW)
    return jnp.where(spot < own, spot, jnp.where(spot < own + HW, first, second))


def count_rows(counts_ref, first, rows, own, flag):
    total = counts_ref.shape[1]
    hit = onehot(iota((rows, total), 1) == offsets(iota((rows, total), 0), own, flag) + first)
    every = jnp.broadcast_to(counts_ref[...].astype(F32), (128, total)).astype(BF)
    return dot_nt(hit, every)


def list_counts(lists, counts, first, places):
    span = places.shape[1]
    shifted = lists - first
    acc = jnp.zeros(places.shape, F32)
    for k in range(lists.shape[1]):
        hit = (shifted[:, k : k + 1] == places) & (counts[:, :span] > k)
        acc = acc + jnp.where(hit, 1.0, 0.0)
    return acc.astype(BF)


def gather_counts(lists_ref, counts_ref, first, own, flag):
    span = own + 2 * HW
    mine = lists_ref[pl.ds(pl.multiple_of(first, HW), own), :]
    counts = count_rows(counts_ref, first, own, own, flag)
    return list_counts(mine, counts, first, offsets(iota((own, span), 1), own, flag)), counts


def scatter_counts(lists_ref, counts_ref, first, own, flag):
    total = lists_ref.shape[0]
    above = jnp.maximum(first - HW, 0)
    below = jnp.minimum(first + own, total - HW)
    parts = [lists_ref[pl.ds(pl.multiple_of(first, HW), own), :]]
    for start in (jnp.where(flag, below, above), jnp.where(flag, above, below)):
        parts.append(lists_ref[pl.ds(pl.multiple_of(start, HW), HW), :])
    counts = count_rows(counts_ref, first, own + 2 * HW, own, flag)
    return list_counts(jnp.concatenate(parts, 0), counts, first, iota((own + 2 * HW, own), 1))


def wide_sta(mix, target, form, own):
    ext = own + 2 * HW
    step = 128
    per = step // HW
    spread_cols = onehot(iota((ext, ext * HW), 1) >> 4 == iota((ext, ext * HW), 0))
    lane_mask = (iota((step, ext * HW), 0) & 15) == (iota((step, ext * HW), 1) & 15)
    for part in range(own * HW // step):
        pick_rows = onehot((iota((step, own), 0) >> 4) + part * per == iota((step, own), 1))
        full = dot(form(pick_rows, mix).astype(BF), spread_cols)
        target[part * step : (part + 1) * step, :] = jnp.where(lane_mask, full, 0.0).astype(BF)


def src_picks(own):
    return onehot((iota((4 * own, own), 0) & (own - 1)) == iota((4 * own, own), 1))


def wide_src(mix, target, form, own):
    ext = own + 2 * HW
    spread_cols = onehot((iota((ext, 4 * ext), 1) & (ext - 1)) == iota((ext, 4 * ext), 0))
    block_mask = (iota((4 * own, 4 * ext), 0) >> 5) == (iota((4 * own, 4 * ext), 1) >> 6)
    full = dot(form(src_picks(own), mix).astype(BF), spread_cols)
    target[...] = jnp.where(block_mask, full, 0.0).astype(BF)


def doubling(feature):
    channels = 2 * feature
    return onehot((iota((feature, channels), 1) & (feature - 1)) == iota((feature, channels), 0))


def prep0_body(sta_rows, src_rows, slists, scounts, rlists, rcounts, weights, sk, rk, sinv, rinv, wf):
    flag, at = even("sta")
    gather, counts = gather_counts(slists, scounts, at * sta_rows, sta_rows, flag)
    wide_sta(gather, sk, dot, sta_rows)
    pick_rows = onehot((iota((sta_rows * HW, sta_rows), 0) >> 4) == iota((sta_rows * HW, sta_rows), 1))
    sinv[...] = 1.0 / dot(pick_rows, counts.astype(BF))
    flag, at = even(SRC)
    gather, counts = gather_counts(rlists, rcounts, at * src_rows, src_rows, flag)
    wide_src(gather, rk, dot, src_rows)
    rinv[...] = 1.0 / dot(src_picks(src_rows), counts.astype(BF))
    feature = weights.shape[-1]
    channels = 2 * feature
    twice = doubling(feature)
    left = iota((feature, channels), 1) < feature
    for layer in range(LAYERS):
        for which in range(3):
            plain = dot(weights[layer, which], twice)
            at = which * channels
            wf[layer, at : at + feature, :] = jnp.where(left, plain, 0.0).astype(BF)
            wf[layer, at + feature : at + channels, :] = jnp.where(left, 0.0, plain).astype(BF)


def prep1_body(sta_rows, src_rows, *refs):
    (_, slists, scounts, rlists, rcounts, picks, targets, weights, readout) = refs[:9]
    (tk, qk, wb, px, cnt, tgt, rl) = refs[9:]
    flag, at = even("sta")
    wide_sta(scatter_counts(slists, scounts, at * sta_rows, sta_rows, flag), tk, dot_nt, sta_rows)
    flag, at = even(SRC)
    wide_src(scatter_counts(rlists, rcounts, at * src_rows, src_rows, flag), qk, dot_nt, src_rows)
    feature = weights.shape[-1]
    channels = 2 * feature
    unit = onehot(iota((feature, feature), 0) == iota((feature, feature), 1))
    left = iota((feature, channels), 1) < feature
    for layer in range(LAYERS):
        for which in range(3):
            matrix = weights[layer, which]
            turned = dot_nt(unit, jnp.concatenate([matrix, matrix], 0))
            at = which * channels
            wb[layer, :feature, at : at + channels] = jnp.where(left, turned, 0.0).astype(BF)
            wb[layer, feature:, at : at + channels] = jnp.where(left, 0.0, turned).astype(BF)
    twice = doubling(feature)
    rl[...] = dot(jnp.broadcast_to(readout[...].astype(F32), (16, feature)).astype(BF), twice)[:8]

    window = iota((16, sta_rows), 0)
    picked = picks[...].astype(F32)
    rows = jnp.where(window == 0, picked[0:1, :], jnp.where(window == 1, picked[1:2, :], 0.0)).astype(BF)
    choose = onehot((iota((16, channels), 1) >> 6) == iota((16, channels), 0))
    chunk = 256
    for part in range(sta_rows * src_rows // chunk):
        at = part * chunk
        own = onehot((iota((chunk, sta_rows), 0) + at) >> 5 == iota((chunk, sta_rows), 1))
        wide = dot(dot_nt(own, rows).astype(BF), choose).astype(BF)
        span = chunk // src_rows
        px[part * span : (part + 1) * span] = wide.reshape(span, src_rows, channels)
    cnt[...] = dot(rows, jnp.ones((sta_rows, channels), BF))[:8]
    line = iota((8, src_rows), 0)
    aims = targets[...]
    tgt[...] = jnp.where(line == 0, aims[0:1, :], jnp.where(line == 1, aims[1:2, :], 0.0))


def starts(axis, own):
    flag, _ = even(axis)
    last = jnp.int32(own - HW)
    none = jnp.int32(0)
    return [pl.multiple_of(jnp.where(f, last, none), HW) for f in (flag, jnp.logical_not(flag))]


def edge_body(x, c1, c0, r1, r0, sems):
    rows, cols, _ = x.shape
    s0, s1 = starts(SRC, cols)
    t0, t1 = starts("sta", rows)
    copies = [
        pltpu.make_async_copy(x.at[:, pl.ds(s1, HW)], c1, sems.at[0]),
        pltpu.make_async_copy(x.at[:, pl.ds(s0, HW)], c0, sems.at[1]),
        pltpu.make_async_copy(x.at[pl.ds(t1, HW)], r1, sems.at[2]),
        pltpu.make_async_copy(x.at[pl.ds(t0, HW)], r0, sems.at[3]),
    ]
    for copy in copies:
        copy.start()
    for copy in copies:
        copy.wait()


def store_edges(by_row, by_col, c1, c0, r1, r0):
    s0, s1 = starts(SRC, by_col.shape[1])
    t0, t1 = starts("sta", by_row.shape[0])
    c1[...] = by_col[:, pl.ds(s1, HW)]
    c0[...] = by_col[:, pl.ds(s0, HW)]
    r1[...] = by_row[pl.ds(t1, HW)]
    r0[...] = by_row[pl.ds(t0, HW)]


def mix_sta(mix, own, r0, r1):
    span = own.shape[0] + 2 * HW
    parts = []
    for g in range(own.shape[1] // HW):
        cut = slice(g * HW, (g + 1) * HW)
        parts.append(jnp.concatenate([own[:, cut], r0[:, cut], r1[:, cut]], 0).reshape(span * HW, 128))
    out = dot(mix[...], jnp.concatenate(parts, 1))
    return [out[:, g * 128 : (g + 1) * 128] for g in range(len(parts))]


def mix_src(mix, own, c0, c1, first):
    parts = []
    for at in (first, first + 4):
        cut = slice(at, at + 4)
        joined = jnp.concatenate([own[cut], c0[cut], c1[cut]], 1)
        parts.append(joined.reshape(4 * joined.shape[1], 128))
    out = dot(mix[...], jnp.concatenate(parts, 1))
    return jnp.concatenate([out[:, :128], out[:, 128:]], 0)


def forward_parts(h, c1, r1, c0, r0, sk, rk, sinv, rinv, wf, states, keep, layer):
    rows, cols, _ = h.shape
    for g, part in enumerate(mix_sta(sk, h, r0, r1)):
        mean = (part * sinv[...]).astype(BF).reshape(rows, HW, 128)
        states[:, g * HW : (g + 1) * HW, 128:256] = mean
    states[:, :, :128] = h[...]
    both = jnp.concatenate([rinv[...], rinv[...]], 0)
    for p in range(rows // 8):
        cut = slice(8 * p, 8 * p + 8)
        mean = (mix_src(rk, h, c0, c1, 8 * p) * both).astype(BF)
        states[cut, :, 256:384] = mean.reshape(8, cols, 128)
        z = dot(states[cut].reshape(8 * cols, 384), wf[layer])
        t = jnp.tanh(z)
        keep[cut] = (1.0 - t * t).reshape(8, cols, 128)
        before = h[cut].reshape(8 * cols, 128).astype(F32)
        yield cut, (before + t).astype(BF)


def forward0_body(h, c1, r1, c0, r0, sk, rk, sinv, rinv, wf, nxt, e1, e0, f1, f0, states, keep):
    cols = h.shape[1]
    for cut, after in forward_parts(h, c1, r1, c0, r0, sk, rk, sinv, rinv, wf, states, keep, 0):
        nxt[cut] = after.reshape(8, cols, 128)
    store_edges(nxt, nxt, e1, e0, f1, f0)


def forward1_body(h, c1, r1, c0, r0, sk, rk, sinv, rinv, wf, px, cnt, rl, states, keep, xsum, block):
    cols = h.shape[1]
    acc = jnp.zeros((cols, 128), F32)
    for cut, after in forward_parts(h, c1, r1, c0, r0, sk, rk, sinv, rinv, wf, states, keep, 1):
        part = after.astype(F32).reshape(8, cols, 128) * px[cut].astype(F32)
        acc = acc + jnp.sum(part, axis=0)
    xsum[...] = acc
    read = jnp.where((iota((8, 128), 1) >> 6) == iota((8, 128), 0), rl[...], 0.0)
    padded = jnp.concatenate([acc, jnp.zeros((128 - cols, 128), F32)], 0)
    sums = dot_nt(read, padded, precision=lax.Precision.HIGHEST)
    mixed = jnp.where(iota((8, 128), 1) < 64, sums, cnt[...])
    block[...] = jnp.broadcast_to(mixed[None], block.shape)


def send_back(p, grad, d, layer, wb, sinv, rinv, direct, usta, usrc):
    cols = usta.shape[1]
    cut = slice(8 * p, 8 * p + 8)
    both = jnp.concatenate([rinv[...], rinv[...]], 0)
    u = dot(d, wb[layer])
    direct[cut] = (grad + u[:, :128]).reshape(8, cols, 128)
    scale = sinv[8 * HW * p : 8 * HW * (p + 1), :].reshape(8, HW, 128)
    scale = jnp.concatenate([scale] * (cols // HW), 1)
    usta[cut] = (u[:, 128:256].reshape(8, cols, 128) * scale).astype(BF)
    usrc[cut] = (u[:, 256:384] * both).astype(BF).reshape(8, cols, 128)


def outer_pairs(states, delta):
    rows, cols, _ = states.shape
    flat = states[...].reshape(rows * cols, 384)
    outer = lax.dot_general(flat, delta[...], TN, preferred_element_type=F32)
    pairs = []
    for which in range(3):
        top = outer[which * 128 : which * 128 + 64]
        low = outer[which * 128 + 64 : which * 128 + 128]
        pairs.append((top + pltpu.roll(low, 64, 1), pltpu.roll(top, 64, 1) + low))
    return pairs


def backward1_body(total, tgt, px, q, rl, wb, sinv, rinv, lik, direct, usta, usrc, e1, e0, f1, f0, errs, delta):
    rows, cols, _ = q.shape
    sums = jnp.sum(total[...], axis=0)
    counts = pltpu.roll(sums, 64, 1)[:, :cols]
    logits = sums[:, :cols] / jnp.sqrt(jnp.maximum(counts, 1.0))
    lik[...] = logits[:2, :]
    error = jax.nn.sigmoid(logits) - tgt[...]
    error = jnp.concatenate([error, jnp.zeros((8, cols), F32)], 0).astype(BF)
    unit = onehot(iota((cols, cols), 0) == iota((cols, cols), 1))
    choose = onehot((iota((16, 128), 1) >> 6) == iota((16, 128), 0))
    wide = dot(dot_nt(unit, error).astype(BF), choose)
    errs[...] = wide
    read = rl[0:1, :]
    for p in range(rows // 8):
        cut = slice(8 * p, 8 * p + 8)
        score = px[cut].astype(F32) * wide[None]
        grad = score.reshape(8 * cols, 128) * read
        d = (grad * q[cut].reshape(8 * cols, 128)).astype(BF)
        delta[8 * cols * p : 8 * cols * (p + 1), :] = d
        send_back(p, grad, d, 1, wb, sinv, rinv, direct, usta, usrc)
    store_edges(usta, usrc, e1, e0, f1, f0)


def weight1_body(states, delta, xsum, errs, wpart):
    pairs = outer_pairs(states, delta)
    lane = iota((64, 128), 1) < 64
    wpart[0:64, :] = jnp.where(lane, pairs[0][0], pairs[1][1])
    wpart[64:128, :] = pairs[2][0]
    v = jnp.sum(errs[...] * xsum[...], axis=0, keepdims=True)
    v = jnp.broadcast_to(v, (8, 128))
    wpart[128:136, :] = v + pltpu.roll(v, 64, 1)


def gathered(direct, usta, usrc, c1, r1, c0, r0, tk, qk, hold):
    rows, cols, _ = direct.shape
    for g, part in enumerate(mix_sta(tk, usta, r0, r1)):
        hold[:, g * HW : (g + 1) * HW, :] = part.reshape(rows, HW, 128)

    def make(p):
        cut = slice(8 * p, 8 * p + 8)
        base = (direct[cut] + hold[cut]).reshape(8 * cols, 128)
        return base + mix_src(qk, usrc, c0, c1, 8 * p)

    return make


def backward0_body(direct1, usta1, usrc1, c1, r1, c0, r0, tk, qk, q, states, wb, sinv, rinv, wpart, direct, usta, usrc, e1, e0, f1, f0, pay, delta, hold):
    rows, cols, _ = q.shape
    make = gathered(direct1, usta1, usrc1, c1, r1, c0, r0, tk, qk, hold)
    for p in range(rows // 8):
        grad = make(p)
        d = (grad * q[8 * p : 8 * p + 8].reshape(8 * cols, 128)).astype(BF)
        delta[8 * cols * p : 8 * cols * (p + 1), :] = d
        send_back(p, grad, d, 0, wb, sinv, rinv, direct, usta, usrc)
    store_edges(usta, usrc, e1, e0, f1, f0)
    pairs = outer_pairs(states, delta)
    lane = iota((64, 128), 1) < 64
    pay[0:64, :] = wpart[0:64, :]
    pay[64:128, :] = jnp.where(lane, wpart[64:128, :], pairs[2][1])
    pay[128:192, :] = jnp.where(lane, pairs[0][0], pairs[1][1])
    pay[192:200, :] = wpart[128:136, :]
    pay[200:, :] = jnp.zeros((pay.shape[0] - 200, 128), F32)


def last_body(direct, usta, usrc, c1, r1, c0, r0, tk, qk, out, hold):
    make = gathered(direct, usta, usrc, c1, r1, c0, r0, tk, qk, hold)
    cols = direct.shape[1]
    for p in range(direct.shape[0] // 8):
        out[8 * p : 8 * p + 8] = make(p).astype(BF).reshape(8, cols, 128)


def sum_body(x, out):
    out[...] = jnp.broadcast_to(jnp.sum(x[...], axis=0)[None], out.shape)


def unpack_body(factor, x, w, v):
    flat = x[...].reshape(-1, 128) * factor
    first = flat[0:64]
    second = flat[64:128]
    third = flat[128:192]
    w[1, 0] = first[:, :64]
    w[1, 1] = pltpu.roll(first, 64, 1)[:, :64]
    w[1, 2] = second[:, :64]
    w[0, 2] = pltpu.roll(second, 64, 1)[:, :64]
    w[0, 0] = third[:, :64]
    w[0, 1] = pltpu.roll(third, 64, 1)[:, :64]
    v[...] = flat[192:193, :64]


def scratch_call(body, outs, scratch, *args, away=0):
    vm = pl.BlockSpec(memory_space=pltpu.VMEM)
    return pl.pallas_call(
        body,
        out_shape=[jax.ShapeDtypeStruct(s, d) for s, d in outs],
        in_specs=[pl.BlockSpec(memory_space=pl.ANY)] * away + [vm] * (len(args) - away),
        out_specs=[vm] * len(outs),
        scratch_shapes=scratch,
        compiler_params=pltpu.CompilerParams(vmem_limit_bytes=VMEM_LIMIT),
    )(*args)


def pairs_of(axis):
    count = 1
    for name in axis if isinstance(axis, tuple) else (axis,):
        count *= lax.axis_size(name)
    inner = [(i, i ^ 1) for i in range(count)]
    outer = [(i, ((i + 1) ^ 1) - 1) for i in range(1, count - 1)]
    return inner, outer


def halo(e1, e0, f1, f0):
    src0, src1 = pairs_of(SRC)
    sta0, sta1 = pairs_of("sta")
    return (
        lax.ppermute(e1, SRC, src1),
        lax.ppermute(f1, "sta", sta1),
        lax.ppermute(e0, SRC, src0),
        lax.ppermute(f0, "sta", sta0),
    )


def shards(features, station_lists, station_counts, source_lists, source_counts, picks, targets, layer_weights, readout_vector):
    rows, cols, channels = features.shape
    n_sta = lax.axis_size("sta")
    n_z = lax.axis_size("z")
    n_plane = n_sta * lax.axis_size("xh")
    whole = (rows, cols, channels)
    edge_outs = [((rows, HW, channels), BF)] * 2 + [((HW, cols, channels), BF)] * 2
    ext_sta, ext_src = rows + 2 * HW, cols + 2 * HW
    tables = (station_lists, station_counts.reshape(1, -1), source_lists, source_counts.reshape(1, -1))

    edges = scratch_call(edge_body, edge_outs, [pltpu.SemaphoreType.DMA((4,))], features, away=1)
    sk, rk, sinv, rinv, wf = call(
        lambda *refs: prep0_body(rows, cols, *refs),
        [
            ((rows * HW, ext_sta * HW), BF),
            ((4 * cols, 4 * ext_src), BF),
            ((rows * HW, channels), F32),
            ((4 * cols, channels), F32),
            ((LAYERS, 3 * channels, channels), BF),
        ],
        *tables,
        layer_weights,
    )
    state_outs = [((rows, cols, 3 * channels), BF), (whole, F32)]
    h1, *edges, states0, q0 = call(
        forward0_body, [(whole, BF)] + edge_outs + state_outs, features, *halo(*edges), sk, rk, sinv, rinv, wf
    )
    tk, qk, wb, px, cnt, tgt, rl = scratch_call(
        lambda *refs: prep1_body(rows, cols, *refs),
        [
            ((rows * HW, ext_sta * HW), BF),
            ((4 * cols, 4 * ext_src), BF),
            ((LAYERS, channels, 3 * channels), BF),
            (whole, BF),
            ((8, channels), F32),
            ((8, cols), F32),
            ((8, channels), F32),
        ],
        [],
        states0,
        *tables,
        picks,
        targets,
        layer_weights,
        readout_vector.reshape(1, -1),
        away=1,
    )
    states1, q1, xsum, block = call(
        forward1_body,
        state_outs + [((cols, channels), F32), ((n_sta, 8, channels), F32)],
        h1,
        *halo(*edges),
        sk,
        rk,
        sinv,
        rinv,
        wf,
        px,
        cnt,
        rl,
    )
    total = lax.all_to_all(block, "sta", 0, 0)
    grad_outs = [(whole, F32), (whole, BF), (whole, BF)] + edge_outs
    flat = ((rows * cols, channels), BF)
    likelihood, direct, usta, usrc, *edges, errs, delta = call(
        backward1_body,
        [((2, cols), F32)] + grad_outs + [((cols, channels), F32), flat],
        total,
        tgt,
        px,
        q1,
        rl,
        wb,
        sinv,
        rinv,
    )
    (wpart,) = call(weight1_body, [((136, channels), F32)], states1, delta, xsum, errs)
    per = -(-200 // (8 * n_plane)) * 8
    direct, usta, usrc, *edges, pay = scratch_call(
        backward0_body,
        grad_outs + [((per * n_plane, channels), F32)],
        [pltpu.VMEM(*flat), pltpu.VMEM(whole, F32)],
        direct,
        usta,
        usrc,
        *halo(*edges),
        tk,
        qk,
        q0,
        states0,
        wb,
        sinv,
        rinv,
        wpart,
    )
    (feature_grad,) = scratch_call(
        last_body, [(whole, BF)], [pltpu.VMEM(whole, F32)], direct, usta, usrc, *halo(*edges), tk, qk
    )
    part = lax.all_to_all(pay.reshape(n_plane, per, channels), PLANE, 0, 0)
    (part,) = call(sum_body, [((n_z, per, channels), F32)], part)
    part = lax.all_to_all(part, "z", 0, 0)
    (part,) = call(sum_body, [((n_plane, per, channels), F32)], part)
    part = lax.all_to_all(part, PLANE, 0, 0)
    nodes = float(rows * n_sta * cols * lax.axis_size("z") * lax.axis_size("xh"))
    feature = layer_weights.shape[-1]
    weight_grad, vector_grad = call(
        lambda *refs: unpack_body(nodes**-0.5, *refs),
        [(layer_weights.shape, F32), ((1, feature), F32)],
        part,
    )
    return likelihood, feature_grad, weight_grad, vector_grad.reshape(feature)


def solution(mesh):
    n_sta, n_src = mesh.devices.shape
    near = 2
    fine = Mesh(mesh.devices.reshape(n_sta, n_src // near, near), ("sta",) + SRC)
    in_specs = (P("sta", SRC, None), P(), P(), P(), P(), P(None, "sta"), P(None, SRC), P(), P())
    out_specs = (P(None, SRC), P("sta", SRC, None), P(), P())
    return jax.shard_map(shards, mesh=fine, in_specs=in_specs, out_specs=out_specs, check_vma=False)
```

time: 136 us -> 125 us (0.919)
  waiting for transfers between devices: 25.6 us -> 7.29 us
  starting transfers between devices: 64.6 us -> 74.5 us
  blocking collectives: 29.7 us -> 25.7 us
    ppermute x16, waiting for transfers between devices: 16.7 us -> 0.84 us  [the longest x4 0.69 us: halo(): lax.ppermute(f0, 'sta', sta0)]
    ppermute x16, starting transfers between devices: 43.1 us -> 55 us  [the longest x4 31 us: halo(): lax.ppermute(e0, SRC, src0)]
    all_to_all x1, blocking collectives: 14.5 us -> 10.7 us  [shards(): total = lax.all_to_all(block, 'sta', 0, 0)]
    all_to_all x1, waiting for transfers between devices: 2.45 us -> 0.01 us  [shards(): part = lax.all_to_all(part, 'z', 0, 0)]
    all_to_all x1, starting transfers between devices: 6.8 us -> 5.21 us  [shards(): part = lax.all_to_all(part, PLANE, 0, 0)]
    pallas_call x3 -> x4, Pallas kernels: 4.19 us -> 5.29 us  [scratch_call(): pl.pallas_call(body, out_shape=[jax.ShapeDtypeStruct(s, d) for s, d in ou...]
    pallas_call x7 -> x8, Pallas kernels: 7.96 us -> 8.12 us  [call(): pl.pallas_call(body, out_shape=[jax.ShapeDtypeStruct(s, d) for s, d in ou...]
  transfers between devices with their start and end apart: 18 -> 18, of which waited for: 7 -> 3; matrix products, arithmetic and copies ran while one was open for 0% -> 0% of each run, Pallas kernels for 4% -> 5%
where the time goes in v3:
time: 125 us
  starting transfers between devices  74.5 us (60%)
  blocking collectives  25.7 us (21%)
  Pallas kernels  13.4 us (11%)
  waiting for transfers between devices  7.29 us (6%)
  local copies, waits for them, and re-layouts  2.64 us (2%)
    ppermute x4, starting transfers between devices, halo(): lax.ppermute(e0, SRC, src0)  31 us
    all_to_all x1, blocking collectives, shards(): part = lax.all_to_all(pay.reshape(n_plane, per, channels), PLANE, 0, 0)  15 us
    all_to_all x1, starting transfers between devices, shards(): part = lax.all_to_all(part, 'z', 0, 0)  14.3 us
    ppermute x4, starting transfers between devices, halo(): lax.ppermute(f1, 'sta', sta1)  13.5 us
    all_to_all x1, blocking collectives, shards(): total = lax.all_to_all(block, 'sta', 0, 0)  10.7 us
    pallas_call x8, Pallas kernels, call(): pl.pallas_call(body, out_shape=[jax.ShapeDtypeStruct(s, d) for s, d in ou...  8.12 us
    ppermute x4, starting transfers between devices, halo(): lax.ppermute(f0, 'sta', sta0)  7.81 us
    all_to_all x1, waiting for transfers between devices, shards(): part = lax.all_to_all(part, PLANE, 0, 0)  6.44 us
  transfers between devices with their start and end apart: 18, of which 3 were waited for; matrix products, arithmetic and copies ran while one was open for 0% of the time, Pallas kernels for 5%

profile of v3, /device:TPU:1, one launch (start us, length us, event | category | flops | bytes accessed | tf_op | source)
XLA Modules:
  0.0 124.6 jit_solution(17985265195771328869)
XLA Ops:
  0.6 0.0 copy-start
  0.6 0.9 copy-done
  1.6 0.4 shard_map.120
  2.0 0.7 collective-permute-start
  2.7 4.6 %collective-permute-start.1 = (bf16[16,32,128]{2,1,0:T(8,128)(2,1)S(1)}, bf16[16,32,128]{2,1,0:T(8,128)(2,1)S(1)}, u32[]{:S(2)}, u32[]{:S(2)}) collective-permute-start(bf16[16,32,128]{2,1,0:T(8,128)(2,1)S(1)} %get-tuple-element.52), channel_id=1, source_target_pairs={{32,64},{64,32},{96,128},{128,96},{160,192},{192,160},{224,256},{2... | collective-permute-start | bytes 393224 | tf_op jit(solution)/shard_map/ppermute | solution.py:415
  7.3 7.8 %collective-permute-start.2 = (bf16[32,16,128]{2,1,0:T(8,128)(2,1)S(1)}, bf16[32,16,128]{2,1,0:T(8,128)(2,1)S(1)}, u32[]{:S(2)}, u32[]{:S(2)}) collective-permute-start(bf16[32,16,128]{2,1,0:T(8,128)(2,1)S(1)} %get-tuple-element.53), channel_id=1, source_target_pairs={{0,1},{1,0},{2,3},{3,2},{4,5},{5,4},{6,7},{7,6},{8,9},{9,8},{10,11... | collective-permute-start | bytes 393224 | tf_op jit(solution)/shard_map/ppermute | solution.py:416
  15.0 0.0 copy-start.8
  15.0 2.1 %collective-permute-start.3 = (bf16[16,32,128]{2,1,0:T(8,128)(2,1)S(1)}, bf16[16,32,128]{2,1,0:T(8,128)(2,1)S(1)}, u32[]{:S(2)}, u32[]{:S(2)}) collective-permute-start(bf16[16,32,128]{2,1,0:T(8,128)(2,1)S(1)} %get-tuple-element.54), channel_id=1, source_target_pairs={{0,32},{32,0},{64,96},{96,64},{128,160},{160,128},{192,224},{224,1... | collective-permute-start | bytes 393224 | tf_op jit(solution)/shard_map/ppermute | solution.py:417
  17.1 0.1 copy.13.refs_0_.refs_1_
  17.2 0.0 copy-start.2
  17.3 0.0 copy-start.3
  17.3 0.2 copy.14.refs_2_.refs_3_
  17.5 0.0 copy-start.4
  17.5 0.7 copy-done.2
  18.1 0.0 copy-done.4
  18.2 1.6 %shard_map.121 = (bf16[512,1024]{1,0:T(8,128)(2,1)S(1)}, bf16[128,256]{1,0:T(8,128)(2,1)S(1)}, f32[512,128]{1,0:T(8,128)S(1)}, f32[128,128]{1,0:T(8,128)S(1)}, bf16[2,384,128]{2,1,0:T(8,128)(2,1)S(1)}) custom-call(s32[512,16]{1,0:T(8,128)S(1)} %copy.13.refs_0_.refs_1_, s32[1,512]{1,0:T(1,128)S(1)} %bitcast.8, s32[1024,16]{1,0:T(8,128)S(1)} %copy.14.refs_2_.refs_3_, ...), custom_call_target="tpu_custom_call" | custom-call | tf_op jit(solution)/shard_map/pallas_call | solution.py:38
  19.8 0.0 collective-permute-done.c1
  19.8 0.0 collective-permute-done.1.r1
  19.8 0.0 collective-permute-done.2.c0
  19.8 0.0 collective-permute-done.3.r0
  19.8 0.0 copy-start.6
  19.8 1.4 %shard_map.122 = (bf16[32,32,128]{2,1,0:T(8,128)(2,1)S(1)}, bf16[32,16,128]{2,1,0:T(8,128)(2,1)S(1)}, bf16[32,16,128]{2,1,0:T(8,128)(2,1)S(1)}, bf16[16,32,128]{...) custom-call(bf16[32,32,128]{2,1,0:T(8,128)(2,1)S(1)} %copy-done.1, ...), custom_call_target="tpu_custom_call" | custom-call | tf_op jit(solution)/shard_map/pallas_call | solution.py:38
  21.3 0.7 collective-permute-start.4
  21.9 3.6 %collective-permute-start.5 = (bf16[16,32,128]{2,1,0:T(8,128)(2,1)S(1)}, bf16[16,32,128]{2,1,0:T(8,128)(2,1)S(1)}, u32[]{:S(2)}, u32[]{:S(2)}) collective-permute-start(bf16[16,32,128]{2,1,0:T(8,128)(2,1)S(1)} %get-tuple-element.62), channel_id=1, source_target_pairs={{32,64},{64,32},{96,128},{128,96},{160,192},{192,160},{224,256},{2... | collective-permute-start | bytes 393224 | tf_op jit(solution)/shard_map/ppermute | solution.py:415
  25.5 7.8 %collective-permute-start.6 = (bf16[32,16,128]{2,1,0:T(8,128)(2,1)S(1)}, bf16[32,16,128]{2,1,0:T(8,128)(2,1)S(1)}, u32[]{:S(2)}, u32[]{:S(2)}) collective-permute-start(bf16[32,16,128]{2,1,0:T(8,128)(2,1)S(1)} %get-tuple-element.63), channel_id=1, source_target_pairs={{0,1},{1,0},{2,3},{3,2},{4,5},{5,4},{6,7},{7,6},{8,9},{9,8},{10,11... | collective-permute-start | bytes 393224 | tf_op jit(solution)/shard_map/ppermute | solution.py:416
  33.3 1.9 %collective-permute-start.7 = (bf16[16,32,128]{2,1,0:T(8,128)(2,1)S(1)}, bf16[16,32,128]{2,1,0:T(8,128)(2,1)S(1)}, u32[]{:S(2)}, u32[]{:S(2)}) collective-permute-start(bf16[16,32,128]{2,1,0:T(8,128)(2,1)S(1)} %get-tuple-element.64), channel_id=1, source_target_pairs={{0,32},{32,0},{64,96},{96,64},{128,160},{160,128},{192,224},{224,1... | collective-permute-start | bytes 393224 | tf_op jit(solution)/shard_map/ppermute | solution.py:417
  35.2 0.0 copy-start.5
  35.2 0.0 copy-start.7
  35.2 0.6 copy-done.5
  35.9 2.2 %shard_map.123 = (bf16[512,1024]{1,0:T(8,128)(2,1)S(1)}, bf16[128,256]{1,0:T(8,128)(2,1)S(1)}, bf16[2,128,384]{2,1,0:T(8,128)(2,1)S(1)}, bf16[32,32,128]{2,1,0:T...) custom-call(bf16[32,32,384]{2,1,0:T(8,128)(2,1)S(1)} %get-tuple-element.65.refs_0_.states, ...), custom_call_target="tpu_custom_call" | custom-call | tf_op jit(solution)/shard_map/pallas_call | solution.py:391
  38.1 0.0 collective-permute-done.4.c1
  38.1 0.0 collective-permute-done.5.r1
  38.1 0.0 collective-permute-done.6.c0
  38.1 0.0 collective-permute-done.7.r0
  38.1 1.5 %shard_map.124 = (bf16[32,32,384]{2,1,0:T(8,128)(2,1)S(1)}, f32[32,32,128]{2,1,0:T(8,128)S(1)}, f32[32,128]{1,0:T(8,128)S(1)}, f32[16,8,128]{2,1,0:T(8,128)S(1)}) custom-call(bf16[32,32,128]{2,1,0:T(8,128)(2,1)S(1)} %get-tuple-element.60.h, bf16[32,16,128]{2,1,0:T(8,128)(2,1)S(1)} %collective-permute-done.4.c1, ...), custom_call_target="tpu_custom_call" | custom-call | tf_op jit(solution)/shard_map/pallas_call | solution.py:38
  39.6 10.7 %all_to_all.20.total = f32[16,8,128]{2,1,0:T(8,128)S(1)} all-to-all(f32[16,8,128]{2,1,0:T(8,128)S(1)} %get-tuple-element.69), channel_id=1, replica_groups=mesh['sta'=16,'z'=16,'xh'=2] {'sta'}, dimensions={0} | all-to-all | bytes 131072 | tf_op jit(solution)/shard_map/all_to_all | solution.py:482
  50.4 1.0 shard_map.125
  51.4 0.7 collective-permute-start.8
  52.0 2.5 %collective-permute-start.9 = (bf16[16,32,128]{2,1,0:T(8,128)(2,1)S(1)}, bf16[16,32,128]{2,1,0:T(8,128)(2,1)S(1)}, u32[]{:S(2)}, u32[]{:S(2)}) collective-permute-start(bf16[16,32,128]{2,1,0:T(8,128)(2,1)S(1)} %get-tuple-element.78), channel_id=1, source_target_pairs={{32,64},{64,32},{96,128},{128,96},{160,192},{192,160},{224,256},{2... | collective-permute-start | bytes 393224 | tf_op jit(solution)/shard_map/ppermute | solution.py:415
  54.5 7.7 %collective-permute-start.10 = (bf16[32,16,128]{2,1,0:T(8,128)(2,1)S(1)}, bf16[32,16,128]{2,1,0:T(8,128)(2,1)S(1)}, u32[]{:S(2)}, u32[]{:S(2)}) collective-permute-start(bf16[32,16,128]{2,1,0:T(8,128)(2,1)S(1)} %get-tuple-element.79), channel_id=1, source_target_pairs={{0,1},{1,0},{2,3},{3,2},{4,5},{5,4},{6,7},{7,6},{8,9},{9,8},{10,11... | collective-permute-start | bytes 393224 | tf_op jit(solution)/shard_map/ppermute | solution.py:416
  62.3 1.9 %collective-permute-start.11 = (bf16[16,32,128]{2,1,0:T(8,128)(2,1)S(1)}, bf16[16,32,128]{2,1,0:T(8,128)(2,1)S(1)}, u32[]{:S(2)}, u32[]{:S(2)}) collective-permute-start(bf16[16,32,128]{2,1,0:T(8,128)(2,1)S(1)} %get-tuple-element.80), channel_id=1, source_target_pairs={{0,32},{32,0},{64,96},{96,64},{128,160},{160,128},{192,224},{224,1... | collective-permute-start | bytes 393224 | tf_op jit(solution)/shard_map/ppermute | solution.py:417
  64.2 0.5 shard_map.126.wpart
  64.7 0.0 collective-permute-done.8.c1
  64.7 0.0 collective-permute-done.9.r1
  64.7 0.1 collective-permute-done.10.c0
  64.8 0.7 collective-permute-done.11.r0
  65.5 1.5 %shard_map.127 = (f32[32,32,128]{2,1,0:T(8,128)S(1)}, bf16[32,32,128]{2,1,0:T(8,128)(2,1)S(1)}, bf16[32,32,128]{2,1,0:T(8,128)(2,1)S(1)}, bf16[32,16,128]{2,1,0:...) custom-call(f32[32,32,128]{2,1,0:T(8,128)S(1)} %get-tuple-element.74, ...), custom_call_target="tpu_custom_call" | custom-call | tf_op jit(solution)/shard_map/pallas_call | solution.py:391
  67.0 15.0 %all_to_all.21.x = f32[32,8,128]{2,1,0:T(8,128)S(1)} all-to-all(f32[32,8,128]{2,1,0:T(8,128)S(1)} %bitcast.5), channel_id=1, replica_groups=mesh['sta'=16,'z'=16,'xh'=2] {'sta','xh'}, dimensions={0} | all-to-all | bytes 262144 | tf_op jit(solution)/shard_map/all_to_all | solution.py:519
  82.0 0.7 shard_map.129
  82.7 14.3 %all-to-all-start.2 = ((f32[16,8,128]{2,1,0:T(8,128)}), f32[16,8,128]{2,1,0:T(8,128)S(1)}, u32[]{:S(2)}, u32[]{:S(2)}) async-start(f32[16,8,128]{2,1,0:T(8,128)} %shard_map.129), calls=%async_computation.2 | async-start | bytes 131072 | tf_op jit(solution)/shard_map/all_to_all | solution.py:521
  97.0 0.7 collective-permute-start.12
  97.7 2.9 %collective-permute-start.13 = (bf16[16,32,128]{2,1,0:T(8,128)(2,1)S(1)}, bf16[16,32,128]{2,1,0:T(8,128)(2,1)S(1)}, u32[]{:S(2)}, u32[]{:S(2)}) collective-permute-start(bf16[16,32,128]{2,1,0:T(8,128)(2,1)S(1)} %get-tuple-element.92), channel_id=1, source_target_pairs={{32,64},{64,32},{96,128},{128,96},{160,192},{192,160},{224,256},{2... | collective-permute-start | bytes 393224 | tf_op jit(solution)/shard_map/ppermute | solution.py:415
  100.5 7.7 %collective-permute-start.14 = (bf16[32,16,128]{2,1,0:T(8,128)(2,1)S(1)}, bf16[32,16,128]{2,1,0:T(8,128)(2,1)S(1)}, u32[]{:S(2)}, u32[]{:S(2)}) collective-permute-start(bf16[32,16,128]{2,1,0:T(8,128)(2,1)S(1)} %get-tuple-element.93), channel_id=1, source_target_pairs={{0,1},{1,0},{2,3},{3,2},{4,5},{5,4},{6,7},{7,6},{8,9},{9,8},{10,11... | collective-permute-start | bytes 393224 | tf_op jit(solution)/shard_map/ppermute | solution.py:416
  108.3 1.9 %collective-permute-start.15 = (bf16[16,32,128]{2,1,0:T(8,128)(2,1)S(1)}, bf16[16,32,128]{2,1,0:T(8,128)(2,1)S(1)}, u32[]{:S(2)}, u32[]{:S(2)}) collective-permute-start(bf16[16,32,128]{2,1,0:T(8,128)(2,1)S(1)} %get-tuple-element.94), channel_id=1, source_target_pairs={{0,32},{32,0},{64,96},{96,64},{128,160},{160,128},{192,224},{224,1... | collective-permute-start | bytes 393224 | tf_op jit(solution)/shard_map/ppermute | solution.py:417
  110.2 0.0 all-to-all-done.2.x
  110.2 0.7 shard_map.130
  110.9 5.2 %all-to-all-start.3 = ((f32[32,8,128]{2,1,0:T(8,128)}), f32[32,8,128]{2,1,0:T(8,128)S(1)}, u32[]{:S(2)}, u32[]{:S(2)}) async-start(f32[32,8,128]{2,1,0:T(8,128)} %shard_map.130), calls=%async_computation.3 | async-start | bytes 262144 | tf_op jit(solution)/shard_map/all_to_all | solution.py:523
  116.1 0.0 collective-permute-done.12.c1
  116.2 0.0 collective-permute-done.13.r1
  116.2 0.0 collective-permute-done.14.c0
  116.2 0.0 collective-permute-done.15.r0
  116.2 1.2 shard_map.128
  117.4 6.4 %all-to-all-done.3.refs_0_ = f32[32,8,128]{2,1,0:T(8,128)S(1)} async-done(((f32[32,8,128]{2,1,0:T(8,128)}), f32[32,8,128]{2,1,0:T(8,128)S(1)}, u32[]{:S(2)}, u32[]{:S(2)}) %all-to-all-start.3) | async-done | bytes 131104 | tf_op jit(solution)/shard_map/all_to_all | solution.py:523
  123.8 0.8 shard_map.131
  (8 shorter events, 0.0 us)
Async XLA Ops:
  0.6 1.0 copy-start
  1.6 15.5 %copy-start.9 = (s32[512,16]{0,1:T(8,128)S(1)}, s32[512,16]{0,1:T(8,128)}, u32[]{:S(2)}) copy-start(s32[512,16]{0,1:T(8,128)} %param.10) | copy-start | bytes 98308
  2.0 17.8 %collective-permute-start = (bf16[32,16,128]{2,1,0:T(8,128)(2,1)S(1)}, bf16[32,16,128]{2,1,0:T(8,128)(2,1)S(1)}, u32[]{:S(2)}, u32[]{:S(2)}) collective-permute-start(bf16[32,16,128]{2,1,0:T(8,128)(2,1)S(1)} %get-tuple-element.51), channel_id=1, source_target_pairs={{1,2},{2,1},{3,4},{4,3},{5,6},{6,5},{7,8},{8,7},{9,10},{10,9},{11,... | collective-permute-start | bytes 393224 | tf_op jit(solution)/shard_map/ppermute | solution.py:414
  2.7 17.1 %collective-permute-start.1 = (bf16[16,32,128]{2,1,0:T(8,128)(2,1)S(1)}, bf16[16,32,128]{2,1,0:T(8,128)(2,1)S(1)}, u32[]{:S(2)}, u32[]{:S(2)}) collective-permute-start(bf16[16,32,128]{2,1,0:T(8,128)(2,1)S(1)} %get-tuple-element.52), channel_id=1, source_target_pairs={{32,64},{64,32},{96,128},{128,96},{160,192},{192,160},{224,256},{2... | collective-permute-start | bytes 393224 | tf_op jit(solution)/shard_map/ppermute | solution.py:415
  7.3 12.5 %collective-permute-start.2 = (bf16[32,16,128]{2,1,0:T(8,128)(2,1)S(1)}, bf16[32,16,128]{2,1,0:T(8,128)(2,1)S(1)}, u32[]{:S(2)}, u32[]{:S(2)}) collective-permute-start(bf16[32,16,128]{2,1,0:T(8,128)(2,1)S(1)} %get-tuple-element.53), channel_id=1, source_target_pairs={{0,1},{1,0},{2,3},{3,2},{4,5},{5,4},{6,7},{7,6},{8,9},{9,8},{10,11... | collective-permute-start | bytes 393224 | tf_op jit(solution)/shard_map/ppermute | solution.py:416
  15.0 2.2 %copy-start.8 = (s32[1024,16]{0,1:T(8,128)S(1)}, s32[1024,16]{0,1:T(8,128)}, u32[]{:S(2)}) copy-start(s32[1024,16]{0,1:T(8,128)} %param.12) | copy-start | bytes 196612
  15.0 4.8 %collective-permute-start.3 = (bf16[16,32,128]{2,1,0:T(8,128)(2,1)S(1)}, bf16[16,32,128]{2,1,0:T(8,128)(2,1)S(1)}, u32[]{:S(2)}, u32[]{:S(2)}) collective-permute-start(bf16[16,32,128]{2,1,0:T(8,128)(2,1)S(1)} %get-tuple-element.54), channel_id=1, source_target_pairs={{0,32},{32,0},{64,96},{96,64},{128,160},{160,128},{192,224},{224,1... | collective-permute-start | bytes 393224 | tf_op jit(solution)/shard_map/ppermute | solution.py:417
  17.2 0.9 copy-start.2
  17.3 0.9 copy-start.3
  17.5 0.7 copy-start.4
  18.2 1.6 %copy-start.1 = (bf16[32,32,128]{2,1,0:T(8,128)(2,1)S(1)}, bf16[32,32,128]{2,1,0:T(8,128)(2,1)}, u32[]{:S(2)}) copy-start(bf16[32,32,128]{2,1,0:T(8,128)(2,1)} %h.1) | copy-start | bytes 786436
  19.8 15.4 %copy-start.6 = (f32[2,32]{1,0:T(2,128)S(1)}, f32[2,32]{1,0:T(2,128)}, u32[]{:S(2)}) copy-start(f32[2,32]{1,0:T(2,128)} %refs_6_.1) | copy-start | bytes 772
  21.3 16.8 %collective-permute-start.4 = (bf16[32,16,128]{2,1,0:T(8,128)(2,1)S(1)}, bf16[32,16,128]{2,1,0:T(8,128)(2,1)S(1)}, u32[]{:S(2)}, u32[]{:S(2)}) collective-permute-start(bf16[32,16,128]{2,1,0:T(8,128)(2,1)S(1)} %get-tuple-element.61), channel_id=1, source_target_pairs={{1,2},{2,1},{3,4},{4,3},{5,6},{6,5},{7,8},{8,7},{9,10},{10,9},{11,... | collective-permute-start | bytes 393224 | tf_op jit(solution)/shard_map/ppermute | solution.py:414
  21.9 16.2 %collective-permute-start.5 = (bf16[16,32,128]{2,1,0:T(8,128)(2,1)S(1)}, bf16[16,32,128]{2,1,0:T(8,128)(2,1)S(1)}, u32[]{:S(2)}, u32[]{:S(2)}) collective-permute-start(bf16[16,32,128]{2,1,0:T(8,128)(2,1)S(1)} %get-tuple-element.62), channel_id=1, source_target_pairs={{32,64},{64,32},{96,128},{128,96},{160,192},{192,160},{224,256},{2... | collective-permute-start | bytes 393224 | tf_op jit(solution)/shard_map/ppermute | solution.py:415
  25.5 12.6 %collective-permute-start.6 = (bf16[32,16,128]{2,1,0:T(8,128)(2,1)S(1)}, bf16[32,16,128]{2,1,0:T(8,128)(2,1)S(1)}, u32[]{:S(2)}, u32[]{:S(2)}) collective-permute-start(bf16[32,16,128]{2,1,0:T(8,128)(2,1)S(1)} %get-tuple-element.63), channel_id=1, source_target_pairs={{0,1},{1,0},{2,3},{3,2},{4,5},{5,4},{6,7},{7,6},{8,9},{9,8},{10,11... | collective-permute-start | bytes 393224 | tf_op jit(solution)/shard_map/ppermute | solution.py:416
  33.3 4.8 %collective-permute-start.7 = (bf16[16,32,128]{2,1,0:T(8,128)(2,1)S(1)}, bf16[16,32,128]{2,1,0:T(8,128)(2,1)S(1)}, u32[]{:S(2)}, u32[]{:S(2)}) collective-permute-start(bf16[16,32,128]{2,1,0:T(8,128)(2,1)S(1)} %get-tuple-element.64), channel_id=1, source_target_pairs={{0,32},{32,0},{64,96},{96,64},{128,160},{160,128},{192,224},{224,1... | collective-permute-start | bytes 393224 | tf_op jit(solution)/shard_map/ppermute | solution.py:417
  35.2 0.7 copy-start.5
  35.2 0.7 copy-start.7
  51.4 13.3 %collective-permute-start.8 = (bf16[32,16,128]{2,1,0:T(8,128)(2,1)S(1)}, bf16[32,16,128]{2,1,0:T(8,128)(2,1)S(1)}, u32[]{:S(2)}, u32[]{:S(2)}) collective-permute-start(bf16[32,16,128]{2,1,0:T(8,128)(2,1)S(1)} %get-tuple-element.77), channel_id=1, source_target_pairs={{1,2},{2,1},{3,4},{4,3},{5,6},{6,5},{7,8},{8,7},{9,10},{10,9},{11,... | collective-permute-start | bytes 393224 | tf_op jit(solution)/shard_map/ppermute | solution.py:414
  52.0 12.7 %collective-permute-start.9 = (bf16[16,32,128]{2,1,0:T(8,128)(2,1)S(1)}, bf16[16,32,128]{2,1,0:T(8,128)(2,1)S(1)}, u32[]{:S(2)}, u32[]{:S(2)}) collective-permute-start(bf16[16,32,128]{2,1,0:T(8,128)(2,1)S(1)} %get-tuple-element.78), channel_id=1, source_target_pairs={{32,64},{64,32},{96,128},{128,96},{160,192},{192,160},{224,256},{2... | collective-permute-start | bytes 393224 | tf_op jit(solution)/shard_map/ppermute | solution.py:415
  54.5 10.3 %collective-permute-start.10 = (bf16[32,16,128]{2,1,0:T(8,128)(2,1)S(1)}, bf16[32,16,128]{2,1,0:T(8,128)(2,1)S(1)}, u32[]{:S(2)}, u32[]{:S(2)}) collective-permute-start(bf16[32,16,128]{2,1,0:T(8,128)(2,1)S(1)} %get-tuple-element.79), channel_id=1, source_target_pairs={{0,1},{1,0},{2,3},{3,2},{4,5},{5,4},{6,7},{7,6},{8,9},{9,8},{10,11... | collective-permute-start | bytes 393224 | tf_op jit(solution)/shard_map/ppermute | solution.py:416
  62.3 3.2 %collective-permute-start.11 = (bf16[16,32,128]{2,1,0:T(8,128)(2,1)S(1)}, bf16[16,32,128]{2,1,0:T(8,128)(2,1)S(1)}, u32[]{:S(2)}, u32[]{:S(2)}) collective-permute-start(bf16[16,32,128]{2,1,0:T(8,128)(2,1)S(1)} %get-tuple-element.80), channel_id=1, source_target_pairs={{0,32},{32,0},{64,96},{96,64},{128,160},{160,128},{192,224},{224,1... | collective-permute-start | bytes 393224 | tf_op jit(solution)/shard_map/ppermute | solution.py:417
  82.7 27.5 %all-to-all-start.2 = ((f32[16,8,128]{2,1,0:T(8,128)}), f32[16,8,128]{2,1,0:T(8,128)S(1)}, u32[]{:S(2)}, u32[]{:S(2)}) async-start(f32[16,8,128]{2,1,0:T(8,128)} %shard_map.129), calls=%async_computation.2 | async-start | bytes 131072 | tf_op jit(solution)/shard_map/all_to_all | solution.py:521
  97.0 19.2 %collective-permute-start.12 = (bf16[32,16,128]{2,1,0:T(8,128)(2,1)S(1)}, bf16[32,16,128]{2,1,0:T(8,128)(2,1)S(1)}, u32[]{:S(2)}, u32[]{:S(2)}) collective-permute-start(bf16[32,16,128]{2,1,0:T(8,128)(2,1)S(1)} %get-tuple-element.91), channel_id=1, source_target_pairs={{1,2},{2,1},{3,4},{4,3},{5,6},{6,5},{7,8},{8,7},{9,10},{10,9},{11,... | collective-permute-start | bytes 393224 | tf_op jit(solution)/shard_map/ppermute | solution.py:414
  97.7 18.5 %collective-permute-start.13 = (bf16[16,32,128]{2,1,0:T(8,128)(2,1)S(1)}, bf16[16,32,128]{2,1,0:T(8,128)(2,1)S(1)}, u32[]{:S(2)}, u32[]{:S(2)}) collective-permute-start(bf16[16,32,128]{2,1,0:T(8,128)(2,1)S(1)} %get-tuple-element.92), channel_id=1, source_target_pairs={{32,64},{64,32},{96,128},{128,96},{160,192},{192,160},{224,256},{2... | collective-permute-start | bytes 393224 | tf_op jit(solution)/shard_map/ppermute | solution.py:415
  100.5 15.6 %collective-permute-start.14 = (bf16[32,16,128]{2,1,0:T(8,128)(2,1)S(1)}, bf16[32,16,128]{2,1,0:T(8,128)(2,1)S(1)}, u32[]{:S(2)}, u32[]{:S(2)}) collective-permute-start(bf16[32,16,128]{2,1,0:T(8,128)(2,1)S(1)} %get-tuple-element.93), channel_id=1, source_target_pairs={{0,1},{1,0},{2,3},{3,2},{4,5},{5,4},{6,7},{7,6},{8,9},{9,8},{10,11... | collective-permute-start | bytes 393224 | tf_op jit(solution)/shard_map/ppermute | solution.py:416
  108.3 7.9 %collective-permute-start.15 = (bf16[16,32,128]{2,1,0:T(8,128)(2,1)S(1)}, bf16[16,32,128]{2,1,0:T(8,128)(2,1)S(1)}, u32[]{:S(2)}, u32[]{:S(2)}) collective-permute-start(bf16[16,32,128]{2,1,0:T(8,128)(2,1)S(1)} %get-tuple-element.94), channel_id=1, source_target_pairs={{0,32},{32,0},{64,96},{96,64},{128,160},{160,128},{192,224},{224,1... | collective-permute-start | bytes 393224 | tf_op jit(solution)/shard_map/ppermute | solution.py:417
  110.9 12.9 %all-to-all-start.3 = ((f32[32,8,128]{2,1,0:T(8,128)}), f32[32,8,128]{2,1,0:T(8,128)S(1)}, u32[]{:S(2)}, u32[]{:S(2)}) async-start(f32[32,8,128]{2,1,0:T(8,128)} %shard_map.130), calls=%async_computation.3 | async-start | bytes 262144 | tf_op jit(solution)/shard_map/all_to_all | solution.py:523

commit v4 on v3

--- a/solution.py
+++ b/solution.py
@@ -58,11 +58,14 @@
     return jnp.where(spot < own, spot, jnp.where(spot < own + HW, first, second))
 
 
-def count_rows(counts_ref, first, rows, own, flag):
-    total = counts_ref.shape[1]
+def table_rows(lists_t, counts, first, rows, own, flag):
+    width, total = lists_t.shape
     hit = onehot(iota((rows, total), 1) == offsets(iota((rows, total), 0), own, flag) + first)
-    every = jnp.broadcast_to(counts_ref[...].astype(F32), (128, total)).astype(BF)
-    return dot_nt(hit, every)
+    entries = lists_t[...]
+    coarse = dot_nt(hit, (entries >> 5).astype(F32).astype(BF))
+    fine = dot_nt(hit, (entries & 31).astype(F32).astype(BF))
+    every = jnp.broadcast_to(counts[...].astype(F32), (128, total)).astype(BF)
+    return (coarse * 32.0 + fine).astype(jnp.int32), dot_nt(hit, every)
 
 
 def list_counts(lists, counts, first, places):
@@ -75,22 +78,15 @@
     return acc.astype(BF)
 
 
-def gather_counts(lists_ref, counts_ref, first, own, flag):
-    span = own + 2 * HW
-    mine = lists_ref[pl.ds(pl.multiple_of(first, HW), own), :]
-    counts = count_rows(counts_ref, first, own, own, flag)
-    return list_counts(mine, counts, first, offsets(iota((own, span), 1), own, flag)), counts
-
-
-def scatter_counts(lists_ref, counts_ref, first, own, flag):
-    total = lists_ref.shape[0]
-    above = jnp.maximum(first - HW, 0)
-    below = jnp.minimum(first + own, total - HW)
-    parts = [lists_ref[pl.ds(pl.multiple_of(first, HW), own), :]]
-    for start in (jnp.where(flag, below, above), jnp.where(flag, above, below)):
-        parts.append(lists_ref[pl.ds(pl.multiple_of(start, HW), HW), :])
-    counts = count_rows(counts_ref, first, own + 2 * HW, own, flag)
-    return list_counts(jnp.concatenate(parts, 0), counts, first, iota((own + 2 * HW, own), 1))
+def gather_counts(lists_t, counts_ref, first, own, flag):
+    lists, counts = table_rows(lists_t, counts_ref, first, own, own, flag)
+    return list_counts(lists, counts, first, offsets(iota((own, own + 2 * HW), 1), own, flag)), counts
+
+
+def scatter_counts(lists_t, counts_ref, first, own, flag):
+    ext = own + 2 * HW
+    lists, counts = table_rows(lists_t, counts_ref, first, ext, own, flag)
+    return list_counts(lists, counts, first, iota((ext, own), 1))
 
 
 def wide_sta(mix, target, form, own):
@@ -122,7 +118,18 @@
     return onehot((iota((feature, channels), 1) & (feature - 1)) == iota((feature, channels), 0))
 
 
-def prep0_body(sta_rows, src_rows, slists, scounts, rlists, rcounts, weights, sk, rk, sinv, rinv, wf):
+def fetch(sources, targets, sems):
+    copies = [pltpu.make_async_copy(a, b, sems.at[n]) for n, (a, b) in enumerate(zip(sources, targets))]
+    for copy in copies:
+        copy.start()
+    return copies
+
+
+def prep0_body(sta_rows, src_rows, *refs):
+    (sk, rk, sinv, rinv, wf, slists, scounts, rlists, rcounts, weights, sems) = refs[5:]
+    copies = fetch(refs[:5], refs[10:15], sems)
+    for copy in copies[:4]:
+        copy.wait()
     flag, at = even("sta")
     gather, counts = gather_counts(slists, scounts, at * sta_rows, sta_rows, flag)
     wide_sta(gather, sk, dot, sta_rows)
@@ -132,6 +139,7 @@
     gather, counts = gather_counts(rlists, rcounts, at * src_rows, src_rows, flag)
     wide_src(gather, rk, dot, src_rows)
     rinv[...] = 1.0 / dot(src_picks(src_rows), counts.astype(BF))
+    copies[4].wait()
     feature = weights.shape[-1]
     channels = 2 * feature
     twice = doubling(feature)
@@ -145,12 +153,11 @@
 
 
 def prep1_body(sta_rows, src_rows, *refs):
-    (_, slists, scounts, rlists, rcounts, picks, targets, weights, readout) = refs[:9]
-    (tk, qk, wb, px, cnt, tgt, rl) = refs[9:]
-    flag, at = even("sta")
-    wide_sta(scatter_counts(slists, scounts, at * sta_rows, sta_rows, flag), tk, dot_nt, sta_rows)
-    flag, at = even(SRC)
-    wide_src(scatter_counts(rlists, rcounts, at * src_rows, src_rows, flag), qk, dot_nt, src_rows)
+    sources = refs[:4]
+    (wb, px, cnt, tgt, rl) = refs[5:10]
+    picks, targets, weights, readout = refs[10:14]
+    for copy in fetch(sources, refs[10:14], refs[14]):
+        copy.wait()
     feature = weights.shape[-1]
     channels = 2 * feature
     unit = onehot(iota((feature, feature), 0) == iota((feature, feature), 1))
@@ -320,7 +327,12 @@
     store_edges(usta, usrc, e1, e0, f1, f0)
 
 
-def weight1_body(states, delta, xsum, errs, wpart):
+def weight1_body(states, delta, xsum, errs, slists, scounts, rlists, rcounts, wpart, tk, qk):
+    sta_rows, src_rows, _ = states.shape
+    flag, at = even("sta")
+    wide_sta(scatter_counts(slists, scounts, at * sta_rows, sta_rows, flag), tk, dot_nt, sta_rows)
+    flag, at = even(SRC)
+    wide_src(scatter_counts(rlists, rcounts, at * src_rows, src_rows, flag), qk, dot_nt, src_rows)
     pairs = outer_pairs(states, delta)
     lane = iota((64, 128), 1) < 64
     wpart[0:64, :] = jnp.where(lane, pairs[0][0], pairs[1][1])
@@ -388,10 +400,11 @@
 
 def scratch_call(body, outs, scratch, *args, away=0):
     vm = pl.BlockSpec(memory_space=pltpu.VMEM)
+    args = [pltpu.with_memory_space_constraint(x, pltpu.HBM) if n < away else x for n, x in enumerate(args)]
     return pl.pallas_call(
         body,
         out_shape=[jax.ShapeDtypeStruct(s, d) for s, d in outs],
-        in_specs=[pl.BlockSpec(memory_space=pl.ANY)] * away + [vm] * (len(args) - away),
+        in_specs=[pl.BlockSpec(memory_space=pltpu.HBM)] * away + [vm] * (len(args) - away),
         out_specs=[vm] * len(outs),
         scratch_shapes=scratch,
         compiler_params=pltpu.CompilerParams(vmem_limit_bytes=VMEM_LIMIT),
@@ -426,10 +439,10 @@
     whole = (rows, cols, channels)
     edge_outs = [((rows, HW, channels), BF)] * 2 + [((HW, cols, channels), BF)] * 2
     ext_sta, ext_src = rows + 2 * HW, cols + 2 * HW
-    tables = (station_lists, station_counts.reshape(1, -1), source_lists, source_counts.reshape(1, -1))
+    tables = (station_lists.T, station_counts.reshape(1, -1), source_lists.T, source_counts.reshape(1, -1))
 
     edges = scratch_call(edge_body, edge_outs, [pltpu.SemaphoreType.DMA((4,))], features, away=1)
-    sk, rk, sinv, rinv, wf = call(
+    sk, rk, sinv, rinv, wf = scratch_call(
         lambda *refs: prep0_body(rows, cols, *refs),
         [
             ((rows * HW, ext_sta * HW), BF),
@@ -438,32 +451,29 @@
             ((4 * cols, channels), F32),
             ((LAYERS, 3 * channels, channels), BF),
         ],
+        [pltpu.VMEM(x.shape, x.dtype) for x in (*tables, layer_weights)] + [pltpu.SemaphoreType.DMA((5,))],
         *tables,
         layer_weights,
+        away=5,
     )
     state_outs = [((rows, cols, 3 * channels), BF), (whole, F32)]
     h1, *edges, states0, q0 = call(
         forward0_body, [(whole, BF)] + edge_outs + state_outs, features, *halo(*edges), sk, rk, sinv, rinv, wf
     )
-    tk, qk, wb, px, cnt, tgt, rl = scratch_call(
+    small = (picks, targets, layer_weights, readout_vector.reshape(1, -1))
+    wb, px, cnt, tgt, rl = scratch_call(
         lambda *refs: prep1_body(rows, cols, *refs),
         [
-            ((rows * HW, ext_sta * HW), BF),
-            ((4 * cols, 4 * ext_src), BF),
             ((LAYERS, channels, 3 * channels), BF),
             (whole, BF),
             ((8, channels), F32),
             ((8, cols), F32),
             ((8, channels), F32),
         ],
-        [],
+        [pltpu.VMEM(x.shape, x.dtype) for x in small] + [pltpu.SemaphoreType.DMA((4,))],
+        *small,
         states0,
-        *tables,
-        picks,
-        targets,
-        layer_weights,
-        readout_vector.reshape(1, -1),
-        away=1,
+        away=4,
     )
     states1, q1, xsum, block = call(
         forward1_body,
@@ -494,7 +504,15 @@
         sinv,
         rinv,
     )
-    (wpart,) = call(weight1_body, [((136, channels), F32)], states1, delta, xsum, errs)
+    wpart, tk, qk = call(
+        weight1_body,
+        [((136, channels), F32), ((rows * HW, ext_sta * HW), BF), ((4 * cols, 4 * ext_src), BF)],
+        states1,
+        delta,
+        xsum,
+        errs,
+        *tables,
+    )
     per = -(-200 // (8 * n_plane)) * 8
     direct, usta, usrc, *edges, pay = scratch_call(
         backward0_body,

time: 125 us -> 124 us (level)
  Pallas kernels: 13.4 us -> 16.6 us
  local copies, waits for them, and re-layouts: 2.64 us -> 0.66 us
  blocking collectives: 25.7 us -> 24 us
    pallas_call x4 -> x5, Pallas kernels: 5.29 us -> 8.26 us  [scratch_call(): pl.pallas_call(body, out_shape=[jax.ShapeDtypeStruct(s, d) for s, d in ou...]
    unnamed x22 -> x10, local copies, waits for them, and re-layouts: 2.64 us -> 0.66 us
    all_to_all x1, blocking collectives: 15 us -> 13.2 us  [shards(): part = lax.all_to_all(pay.reshape(n_plane, per, channels), PLANE, 0, 0)]
    pallas_call x8 -> x7, Pallas kernels: 8.12 us -> 8.39 us  [call(): pl.pallas_call(body, out_shape=[jax.ShapeDtypeStruct(s, d) for s, d in ou...]
  transfers between devices with their start and end apart: 18 -> 18, of which waited for: 3 -> 1; matrix products, arithmetic and copies ran while one was open for 0% -> 0% of each run, Pallas kernels for 5% -> 7%
where the time goes in v4:
time: 124 us
  starting transfers between devices  74.8 us (60%)
  blocking collectives  24 us (19%)
  Pallas kernels  16.6 us (13%)
  waiting for transfers between devices  6.49 us (5%)
    ppermute x4, starting transfers between devices, halo(): lax.ppermute(e0, SRC, src0)  31 us
    all_to_all x1, starting transfers between devices, shards(): part = lax.all_to_all(part, 'z', 0, 0)  14.7 us
    ppermute x4, starting transfers between devices, halo(): lax.ppermute(f1, 'sta', sta1)  13.5 us
    all_to_all x1, blocking collectives, shards(): part = lax.all_to_all(pay.reshape(n_plane, per, channels), PLANE, 0, 0)  13.2 us
    all_to_all x1, blocking collectives, shards(): total = lax.all_to_all(block, 'sta', 0, 0)  10.7 us
    pallas_call x7, Pallas kernels, call(): pl.pallas_call(body, out_shape=[jax.ShapeDtypeStruct(s, d) for s, d in ou...  8.39 us
    pallas_call x5, Pallas kernels, scratch_call(): pl.pallas_call(body, out_shape=[jax.ShapeDtypeStruct(s, d) for s, d in ou...  8.26 us
    ppermute x4, starting transfers between devices, halo(): lax.ppermute(f0, 'sta', sta0)  7.68 us
  transfers between devices with their start and end apart: 18, of which 1 were waited for; matrix products, arithmetic and copies ran while one was open for 0% of the time, Pallas kernels for 7%

profile of v4, /device:TPU:1, one launch (start us, length us, event | category | flops | bytes accessed | tf_op | source)
XLA Modules:
  0.0 123.5 jit_solution(8790019643600352555)
XLA Ops:
  0.6 0.0 copy-start
  0.6 1.2 shard_map.120
  1.8 0.7 collective-permute-start
  2.5 4.6 %collective-permute-start.1 = (bf16[16,32,128]{2,1,0:T(8,128)(2,1)S(1)}, bf16[16,32,128]{2,1,0:T(8,128)(2,1)S(1)}, u32[]{:S(2)}, u32[]{:S(2)}) collective-permute-start(bf16[16,32,128]{2,1,0:T(8,128)(2,1)S(1)} %get-tuple-element.53), channel_id=1, source_target_pairs={{32,64},{64,32},{96,128},{128,96},{160,192},{192,160},{224,256},{2... | collective-permute-start | bytes 393224 | tf_op jit(solution)/shard_map/ppermute | solution.py:428
  7.1 7.8 %collective-permute-start.2 = (bf16[32,16,128]{2,1,0:T(8,128)(2,1)S(1)}, bf16[32,16,128]{2,1,0:T(8,128)(2,1)S(1)}, u32[]{:S(2)}, u32[]{:S(2)}) collective-permute-start(bf16[32,16,128]{2,1,0:T(8,128)(2,1)S(1)} %get-tuple-element.54), channel_id=1, source_target_pairs={{0,1},{1,0},{2,3},{3,2},{4,5},{5,4},{6,7},{7,6},{8,9},{9,8},{10,11... | collective-permute-start | bytes 393224 | tf_op jit(solution)/shard_map/ppermute | solution.py:429
  14.9 1.9 %collective-permute-start.3 = (bf16[16,32,128]{2,1,0:T(8,128)(2,1)S(1)}, bf16[16,32,128]{2,1,0:T(8,128)(2,1)S(1)}, u32[]{:S(2)}, u32[]{:S(2)}) collective-permute-start(bf16[16,32,128]{2,1,0:T(8,128)(2,1)S(1)} %get-tuple-element.55), channel_id=1, source_target_pairs={{0,32},{32,0},{64,96},{96,64},{128,160},{160,128},{192,224},{224,1... | collective-permute-start | bytes 393224 | tf_op jit(solution)/shard_map/ppermute | solution.py:430
  16.8 2.9 %shard_map.121 = (bf16[512,1024]{1,0:T(8,128)(2,1)S(1)}, bf16[128,256]{1,0:T(8,128)(2,1)S(1)}, f32[512,128]{1,0:T(8,128)S(1)}, f32[128,128]{1,0:T(8,128)S(1)}, bf16[2,384,128]{2,1,0:T(8,128)(2,1)S(1)}) custom-call(s32[16,512]{1,0:T(8,128)} %bitcast.9, s32[1,512]{1,0:T(1,128)} %bitcast.14, s32[16,1024]{1,0:T(8,128)} %bitcast.7, s32[1,1024]{1,0:T(1,128)} %bitcast.12, ...), custom_call_target="tpu_custom_call" | custom-call | tf_op jit(solution)/shard_map/pallas_call | solution.py:404
  19.7 0.0 collective-permute-done.c1
  19.7 0.0 collective-permute-done.1.r1
  19.7 0.0 collective-permute-done.2.c0
  19.7 0.0 collective-permute-done.3.r0
  19.7 0.0 copy-done
  19.7 1.4 %shard_map.122 = (bf16[32,32,128]{2,1,0:T(8,128)(2,1)S(1)}, bf16[32,16,128]{2,1,0:T(8,128)(2,1)S(1)}, bf16[32,16,128]{2,1,0:T(8,128)(2,1)S(1)}, bf16[16,32,128]{...) custom-call(bf16[32,32,128]{2,1,0:T(8,128)(2,1)S(1)} %copy-done, ...), custom_call_target="tpu_custom_call" | custom-call | tf_op jit(solution)/shard_map/pallas_call | solution.py:38
  21.1 0.7 collective-permute-start.4
  21.8 3.6 %collective-permute-start.5 = (bf16[16,32,128]{2,1,0:T(8,128)(2,1)S(1)}, bf16[16,32,128]{2,1,0:T(8,128)(2,1)S(1)}, u32[]{:S(2)}, u32[]{:S(2)}) collective-permute-start(bf16[16,32,128]{2,1,0:T(8,128)(2,1)S(1)} %get-tuple-element.63), channel_id=1, source_target_pairs={{32,64},{64,32},{96,128},{128,96},{160,192},{192,160},{224,256},{2... | collective-permute-start | bytes 393224 | tf_op jit(solution)/shard_map/ppermute | solution.py:428
  25.4 7.8 %collective-permute-start.6 = (bf16[32,16,128]{2,1,0:T(8,128)(2,1)S(1)}, bf16[32,16,128]{2,1,0:T(8,128)(2,1)S(1)}, u32[]{:S(2)}, u32[]{:S(2)}) collective-permute-start(bf16[32,16,128]{2,1,0:T(8,128)(2,1)S(1)} %get-tuple-element.64), channel_id=1, source_target_pairs={{0,1},{1,0},{2,3},{3,2},{4,5},{5,4},{6,7},{7,6},{8,9},{9,8},{10,11... | collective-permute-start | bytes 393224 | tf_op jit(solution)/shard_map/ppermute | solution.py:429
  33.2 1.9 %collective-permute-start.7 = (bf16[16,32,128]{2,1,0:T(8,128)(2,1)S(1)}, bf16[16,32,128]{2,1,0:T(8,128)(2,1)S(1)}, u32[]{:S(2)}, u32[]{:S(2)}) collective-permute-start(bf16[16,32,128]{2,1,0:T(8,128)(2,1)S(1)} %get-tuple-element.65), channel_id=1, source_target_pairs={{0,32},{32,0},{64,96},{96,64},{128,160},{160,128},{192,224},{224,1... | collective-permute-start | bytes 393224 | tf_op jit(solution)/shard_map/ppermute | solution.py:430
  35.1 1.5 %shard_map.123 = (bf16[2,128,384]{2,1,0:T(8,128)(2,1)S(1)}, bf16[32,32,128]{2,1,0:T(8,128)(2,1)S(1)}, f32[8,128]{1,0:T(8,128)S(1)}, f32[8,32]{1,0:T(8,128)S(1)}, f32[8,128]{1,0:T(8,128)S(1)}) custom-call(s32[2,32]{1,0:T(2,128)} %refs_0_.1, f32[2,32]{1,0:T(2,128)} %refs_1_.1, bf16[2,3,64,64]{3,2,1,0:T(8,128)(2,1)} %refs_2_.1, bf16[1,64]{1,0:T(2,128)(2,1)} %bitcast.16, ...), custom_call_target="tpu_custom_call" | custom-call | tf_op jit(solution)/shard_map/pallas_call | solution.py:404
  36.6 0.0 collective-permute-done.4.c1
  36.6 0.0 collective-permute-done.5.r1
  36.6 0.0 collective-permute-done.6.c0
  36.6 0.0 collective-permute-done.7.r0
  36.6 1.5 %shard_map.124 = (bf16[32,32,384]{2,1,0:T(8,128)(2,1)S(1)}, f32[32,32,128]{2,1,0:T(8,128)S(1)}, f32[32,128]{1,0:T(8,128)S(1)}, f32[16,8,128]{2,1,0:T(8,128)S(1)}) custom-call(bf16[32,32,128]{2,1,0:T(8,128)(2,1)S(1)} %get-tuple-element.61.h, bf16[32,16,128]{2,1,0:T(8,128)(2,1)S(1)} %collective-permute-done.4.c1, ...), custom_call_target="tpu_custom_call" | custom-call | tf_op jit(solution)/shard_map/pallas_call | solution.py:38
  38.1 10.7 %all_to_all.20.total = f32[16,8,128]{2,1,0:T(8,128)S(1)} all-to-all(f32[16,8,128]{2,1,0:T(8,128)S(1)} %get-tuple-element.70), channel_id=1, replica_groups=mesh['sta'=16,'z'=16,'xh'=2] {'sta'}, dimensions={0} | all-to-all | bytes 131072 | tf_op jit(solution)/shard_map/all_to_all | solution.py:492
  48.8 0.0 copy-start.1
  48.8 0.0 copy-start.2
  48.8 1.0 shard_map.125
  49.9 0.7 collective-permute-start.8
  50.5 2.5 %collective-permute-start.9 = (bf16[16,32,128]{2,1,0:T(8,128)(2,1)S(1)}, bf16[16,32,128]{2,1,0:T(8,128)(2,1)S(1)}, u32[]{:S(2)}, u32[]{:S(2)}) collective-permute-start(bf16[16,32,128]{2,1,0:T(8,128)(2,1)S(1)} %get-tuple-element.79), channel_id=1, source_target_pairs={{32,64},{64,32},{96,128},{128,96},{160,192},{192,160},{224,256},{2... | collective-permute-start | bytes 393224 | tf_op jit(solution)/shard_map/ppermute | solution.py:428
  53.0 7.8 %collective-permute-start.10 = (bf16[32,16,128]{2,1,0:T(8,128)(2,1)S(1)}, bf16[32,16,128]{2,1,0:T(8,128)(2,1)S(1)}, u32[]{:S(2)}, u32[]{:S(2)}) collective-permute-start(bf16[32,16,128]{2,1,0:T(8,128)(2,1)S(1)} %get-tuple-element.80), channel_id=1, source_target_pairs={{0,1},{1,0},{2,3},{3,2},{4,5},{5,4},{6,7},{7,6},{8,9},{9,8},{10,11... | collective-permute-start | bytes 393224 | tf_op jit(solution)/shard_map/ppermute | solution.py:429
  60.8 0.0 copy-start.3
  60.8 1.9 %collective-permute-start.11 = (bf16[16,32,128]{2,1,0:T(8,128)(2,1)S(1)}, bf16[16,32,128]{2,1,0:T(8,128)(2,1)S(1)}, u32[]{:S(2)}, u32[]{:S(2)}) collective-permute-start(bf16[16,32,128]{2,1,0:T(8,128)(2,1)S(1)} %get-tuple-element.81), channel_id=1, source_target_pairs={{0,32},{32,0},{64,96},{96,64},{128,160},{160,128},{192,224},{224,1... | collective-permute-start | bytes 393224 | tf_op jit(solution)/shard_map/ppermute | solution.py:430
  62.7 0.0 copy-start.4
  62.7 0.0 copy-done.1
  62.8 0.0 copy-done.2
  62.8 0.0 copy-done.3
  62.8 0.6 copy-done.4
  63.4 2.3 %shard_map.126 = (f32[136,128]{1,0:T(8,128)S(1)}, bf16[512,1024]{1,0:T(8,128)(2,1)S(1)}, bf16[128,256]{1,0:T(8,128)(2,1)S(1)}) custom-call(bf16[32,32,384]{2,1,0:T(8,128)(2,1)S(1)} %get-tuple-element.82.states, bf16[1024,128]{1,0:T(8,128)(2,1)S(1)} %get-tuple-element.83.delta, f32[32,128]{1,0:T(8,128)S(1)} %get-tuple-element.84.xsum, ...), custom_call_target="tpu_custom_call" | custom-call | tf_op jit(solution)/shard_map/pallas_call | solution.py:38
  65.8 0.0 collective-permute-done.8.c1
  65.8 0.0 collective-permute-done.9.r1
  65.8 0.0 collective-permute-done.10.c0
  65.8 0.0 collective-permute-done.11.r0
  65.8 1.5 %shard_map.127 = (f32[32,32,128]{2,1,0:T(8,128)S(1)}, bf16[32,32,128]{2,1,0:T(8,128)(2,1)S(1)}, bf16[32,32,128]{2,1,0:T(8,128)(2,1)S(1)}, bf16[32,16,128]{2,1,0:...) custom-call(f32[32,32,128]{2,1,0:T(8,128)S(1)} %get-tuple-element.75, ...), custom_call_target="tpu_custom_call" | custom-call | tf_op jit(solution)/shard_map/pallas_call | solution.py:404
  67.3 13.2 %all_to_all.21.x = f32[32,8,128]{2,1,0:T(8,128)S(1)} all-to-all(f32[32,8,128]{2,1,0:T(8,128)S(1)} %bitcast.11), channel_id=1, replica_groups=mesh['sta'=16,'z'=16,'xh'=2] {'sta','xh'}, dimensions={0} | all-to-all | bytes 262144 | tf_op jit(solution)/shard_map/all_to_all | solution.py:537
  80.6 0.7 shard_map.129
  81.2 14.7 %all-to-all-start.2 = ((f32[16,8,128]{2,1,0:T(8,128)}), f32[16,8,128]{2,1,0:T(8,128)S(1)}, u32[]{:S(2)}, u32[]{:S(2)}) async-start(f32[16,8,128]{2,1,0:T(8,128)} %shard_map.129), calls=%async_computation.2 | async-start | bytes 131072 | tf_op jit(solution)/shard_map/all_to_all | solution.py:539
  95.9 0.7 collective-permute-start.12
  96.6 2.9 %collective-permute-start.13 = (bf16[16,32,128]{2,1,0:T(8,128)(2,1)S(1)}, bf16[16,32,128]{2,1,0:T(8,128)(2,1)S(1)}, u32[]{:S(2)}, u32[]{:S(2)}) collective-permute-start(bf16[16,32,128]{2,1,0:T(8,128)(2,1)S(1)} %get-tuple-element.94), channel_id=1, source_target_pairs={{32,64},{64,32},{96,128},{128,96},{160,192},{192,160},{224,256},{2... | collective-permute-start | bytes 393224 | tf_op jit(solution)/shard_map/ppermute | solution.py:428
  99.5 7.7 %collective-permute-start.14 = (bf16[32,16,128]{2,1,0:T(8,128)(2,1)S(1)}, bf16[32,16,128]{2,1,0:T(8,128)(2,1)S(1)}, u32[]{:S(2)}, u32[]{:S(2)}) collective-permute-start(bf16[32,16,128]{2,1,0:T(8,128)(2,1)S(1)} %get-tuple-element.95), channel_id=1, source_target_pairs={{0,1},{1,0},{2,3},{3,2},{4,5},{5,4},{6,7},{7,6},{8,9},{9,8},{10,11... | collective-permute-start | bytes 393224 | tf_op jit(solution)/shard_map/ppermute | solution.py:429
  107.2 1.9 %collective-permute-start.15 = (bf16[16,32,128]{2,1,0:T(8,128)(2,1)S(1)}, bf16[16,32,128]{2,1,0:T(8,128)(2,1)S(1)}, u32[]{:S(2)}, u32[]{:S(2)}) collective-permute-start(bf16[16,32,128]{2,1,0:T(8,128)(2,1)S(1)} %get-tuple-element.96), channel_id=1, source_target_pairs={{0,32},{32,0},{64,96},{96,64},{128,160},{160,128},{192,224},{224,1... | collective-permute-start | bytes 393224 | tf_op jit(solution)/shard_map/ppermute | solution.py:430
  109.2 0.0 all-to-all-done.2.x
  109.2 0.7 shard_map.130
  109.8 5.2 %all-to-all-start.3 = ((f32[32,8,128]{2,1,0:T(8,128)}), f32[32,8,128]{2,1,0:T(8,128)S(1)}, u32[]{:S(2)}, u32[]{:S(2)}) async-start(f32[32,8,128]{2,1,0:T(8,128)} %shard_map.130), calls=%async_computation.3 | async-start | bytes 262144 | tf_op jit(solution)/shard_map/all_to_all | solution.py:541
  115.1 0.0 collective-permute-done.12.c1
  115.1 0.0 collective-permute-done.13.r1
  115.1 0.0 collective-permute-done.14.c0
  115.1 0.0 collective-permute-done.15.r0
  115.1 1.2 shard_map.128
  116.3 6.4 %all-to-all-done.3.refs_0_ = f32[32,8,128]{2,1,0:T(8,128)S(1)} async-done(((f32[32,8,128]{2,1,0:T(8,128)}), f32[32,8,128]{2,1,0:T(8,128)S(1)}, u32[]{:S(2)}, u32[]{:S(2)}) %all-to-all-start.3) | async-done | bytes 131104 | tf_op jit(solution)/shard_map/all_to_all | solution.py:541
  122.8 0.8 shard_map.131
Async XLA Ops:
  0.6 19.1 %copy-start = (bf16[32,32,128]{2,1,0:T(8,128)(2,1)S(1)}, bf16[32,32,128]{2,1,0:T(8,128)(2,1)}, u32[]{:S(2)}) copy-start(bf16[32,32,128]{2,1,0:T(8,128)(2,1)} %h.1) | copy-start | bytes 786436
  1.8 17.8 %collective-permute-start = (bf16[32,16,128]{2,1,0:T(8,128)(2,1)S(1)}, bf16[32,16,128]{2,1,0:T(8,128)(2,1)S(1)}, u32[]{:S(2)}, u32[]{:S(2)}) collective-permute-start(bf16[32,16,128]{2,1,0:T(8,128)(2,1)S(1)} %get-tuple-element.52), channel_id=1, source_target_pairs={{1,2},{2,1},{3,4},{4,3},{5,6},{6,5},{7,8},{8,7},{9,10},{10,9},{11,... | collective-permute-start | bytes 393224 | tf_op jit(solution)/shard_map/ppermute | solution.py:427
  2.5 17.2 %collective-permute-start.1 = (bf16[16,32,128]{2,1,0:T(8,128)(2,1)S(1)}, bf16[16,32,128]{2,1,0:T(8,128)(2,1)S(1)}, u32[]{:S(2)}, u32[]{:S(2)}) collective-permute-start(bf16[16,32,128]{2,1,0:T(8,128)(2,1)S(1)} %get-tuple-element.53), channel_id=1, source_target_pairs={{32,64},{64,32},{96,128},{128,96},{160,192},{192,160},{224,256},{2... | collective-permute-start | bytes 393224 | tf_op jit(solution)/shard_map/ppermute | solution.py:428
  7.1 12.6 %collective-permute-start.2 = (bf16[32,16,128]{2,1,0:T(8,128)(2,1)S(1)}, bf16[32,16,128]{2,1,0:T(8,128)(2,1)S(1)}, u32[]{:S(2)}, u32[]{:S(2)}) collective-permute-start(bf16[32,16,128]{2,1,0:T(8,128)(2,1)S(1)} %get-tuple-element.54), channel_id=1, source_target_pairs={{0,1},{1,0},{2,3},{3,2},{4,5},{5,4},{6,7},{7,6},{8,9},{9,8},{10,11... | collective-permute-start | bytes 393224 | tf_op jit(solution)/shard_map/ppermute | solution.py:429
  14.9 4.8 %collective-permute-start.3 = (bf16[16,32,128]{2,1,0:T(8,128)(2,1)S(1)}, bf16[16,32,128]{2,1,0:T(8,128)(2,1)S(1)}, u32[]{:S(2)}, u32[]{:S(2)}) collective-permute-start(bf16[16,32,128]{2,1,0:T(8,128)(2,1)S(1)} %get-tuple-element.55), channel_id=1, source_target_pairs={{0,32},{32,0},{64,96},{96,64},{128,160},{160,128},{192,224},{224,1... | collective-permute-start | bytes 393224 | tf_op jit(solution)/shard_map/ppermute | solution.py:430
  21.1 15.4 %collective-permute-start.4 = (bf16[32,16,128]{2,1,0:T(8,128)(2,1)S(1)}, bf16[32,16,128]{2,1,0:T(8,128)(2,1)S(1)}, u32[]{:S(2)}, u32[]{:S(2)}) collective-permute-start(bf16[32,16,128]{2,1,0:T(8,128)(2,1)S(1)} %get-tuple-element.62), channel_id=1, source_target_pairs={{1,2},{2,1},{3,4},{4,3},{5,6},{6,5},{7,8},{8,7},{9,10},{10,9},{11,... | collective-permute-start | bytes 393224 | tf_op jit(solution)/shard_map/ppermute | solution.py:427
  21.8 14.8 %collective-permute-start.5 = (bf16[16,32,128]{2,1,0:T(8,128)(2,1)S(1)}, bf16[16,32,128]{2,1,0:T(8,128)(2,1)S(1)}, u32[]{:S(2)}, u32[]{:S(2)}) collective-permute-start(bf16[16,32,128]{2,1,0:T(8,128)(2,1)S(1)} %get-tuple-element.63), channel_id=1, source_target_pairs={{32,64},{64,32},{96,128},{128,96},{160,192},{192,160},{224,256},{2... | collective-permute-start | bytes 393224 | tf_op jit(solution)/shard_map/ppermute | solution.py:428
  25.4 11.2 %collective-permute-start.6 = (bf16[32,16,128]{2,1,0:T(8,128)(2,1)S(1)}, bf16[32,16,128]{2,1,0:T(8,128)(2,1)S(1)}, u32[]{:S(2)}, u32[]{:S(2)}) collective-permute-start(bf16[32,16,128]{2,1,0:T(8,128)(2,1)S(1)} %get-tuple-element.64), channel_id=1, source_target_pairs={{0,1},{1,0},{2,3},{3,2},{4,5},{5,4},{6,7},{7,6},{8,9},{9,8},{10,11... | collective-permute-start | bytes 393224 | tf_op jit(solution)/shard_map/ppermute | solution.py:429
  33.2 3.4 %collective-permute-start.7 = (bf16[16,32,128]{2,1,0:T(8,128)(2,1)S(1)}, bf16[16,32,128]{2,1,0:T(8,128)(2,1)S(1)}, u32[]{:S(2)}, u32[]{:S(2)}) collective-permute-start(bf16[16,32,128]{2,1,0:T(8,128)(2,1)S(1)} %get-tuple-element.65), channel_id=1, source_target_pairs={{0,32},{32,0},{64,96},{96,64},{128,160},{160,128},{192,224},{224,1... | collective-permute-start | bytes 393224 | tf_op jit(solution)/shard_map/ppermute | solution.py:430
  48.8 13.9 %copy-start.1 = (s32[1024,16]{0,1:T(8,128)S(1)}, s32[1024,16]{0,1:T(8,128)}, u32[]{:S(2)}) copy-start(s32[1024,16]{0,1:T(8,128)} %param.12) | copy-start | bytes 196612
  48.8 13.9 %copy-start.2 = (s32[512,16]{0,1:T(8,128)S(1)}, s32[512,16]{0,1:T(8,128)}, u32[]{:S(2)}) copy-start(s32[512,16]{0,1:T(8,128)} %param.10) | copy-start | bytes 98308
  49.9 15.9 %collective-permute-start.8 = (bf16[32,16,128]{2,1,0:T(8,128)(2,1)S(1)}, bf16[32,16,128]{2,1,0:T(8,128)(2,1)S(1)}, u32[]{:S(2)}, u32[]{:S(2)}) collective-permute-start(bf16[32,16,128]{2,1,0:T(8,128)(2,1)S(1)} %get-tuple-element.78), channel_id=1, source_target_pairs={{1,2},{2,1},{3,4},{4,3},{5,6},{6,5},{7,8},{8,7},{9,10},{10,9},{11,... | collective-permute-start | bytes 393224 | tf_op jit(solution)/shard_map/ppermute | solution.py:427
  50.5 15.2 %collective-permute-start.9 = (bf16[16,32,128]{2,1,0:T(8,128)(2,1)S(1)}, bf16[16,32,128]{2,1,0:T(8,128)(2,1)S(1)}, u32[]{:S(2)}, u32[]{:S(2)}) collective-permute-start(bf16[16,32,128]{2,1,0:T(8,128)(2,1)S(1)} %get-tuple-element.79), channel_id=1, source_target_pairs={{32,64},{64,32},{96,128},{128,96},{160,192},{192,160},{224,256},{2... | collective-permute-start | bytes 393224 | tf_op jit(solution)/shard_map/ppermute | solution.py:428
  53.0 12.8 %collective-permute-start.10 = (bf16[32,16,128]{2,1,0:T(8,128)(2,1)S(1)}, bf16[32,16,128]{2,1,0:T(8,128)(2,1)S(1)}, u32[]{:S(2)}, u32[]{:S(2)}) collective-permute-start(bf16[32,16,128]{2,1,0:T(8,128)(2,1)S(1)} %get-tuple-element.80), channel_id=1, source_target_pairs={{0,1},{1,0},{2,3},{3,2},{4,5},{5,4},{6,7},{7,6},{8,9},{9,8},{10,11... | collective-permute-start | bytes 393224 | tf_op jit(solution)/shard_map/ppermute | solution.py:429
  60.8 2.0 %copy-start.3 = (s32[1024]{0:T(1024)S(1)}, s32[1024]{0:T(1024)}, u32[]{:S(2)}) copy-start(s32[1024]{0:T(1024)} %param.13) | copy-start | bytes 12292
  60.8 5.0 %collective-permute-start.11 = (bf16[16,32,128]{2,1,0:T(8,128)(2,1)S(1)}, bf16[16,32,128]{2,1,0:T(8,128)(2,1)S(1)}, u32[]{:S(2)}, u32[]{:S(2)}) collective-permute-start(bf16[16,32,128]{2,1,0:T(8,128)(2,1)S(1)} %get-tuple-element.81), channel_id=1, source_target_pairs={{0,32},{32,0},{64,96},{96,64},{128,160},{160,128},{192,224},{224,1... | collective-permute-start | bytes 393224 | tf_op jit(solution)/shard_map/ppermute | solution.py:430
  62.7 0.7 copy-start.4
  81.2 27.9 %all-to-all-start.2 = ((f32[16,8,128]{2,1,0:T(8,128)}), f32[16,8,128]{2,1,0:T(8,128)S(1)}, u32[]{:S(2)}, u32[]{:S(2)}) async-start(f32[16,8,128]{2,1,0:T(8,128)} %shard_map.129), calls=%async_computation.2 | async-start | bytes 131072 | tf_op jit(solution)/shard_map/all_to_all | solution.py:539
  95.9 19.1 %collective-permute-start.12 = (bf16[32,16,128]{2,1,0:T(8,128)(2,1)S(1)}, bf16[32,16,128]{2,1,0:T(8,128)(2,1)S(1)}, u32[]{:S(2)}, u32[]{:S(2)}) collective-permute-start(bf16[32,16,128]{2,1,0:T(8,128)(2,1)S(1)} %get-tuple-element.93), channel_id=1, source_target_pairs={{1,2},{2,1},{3,4},{4,3},{5,6},{6,5},{7,8},{8,7},{9,10},{10,9},{11,... | collective-permute-start | bytes 393224 | tf_op jit(solution)/shard_map/ppermute | solution.py:427
  96.6 18.5 %collective-permute-start.13 = (bf16[16,32,128]{2,1,0:T(8,128)(2,1)S(1)}, bf16[16,32,128]{2,1,0:T(8,128)(2,1)S(1)}, u32[]{:S(2)}, u32[]{:S(2)}) collective-permute-start(bf16[16,32,128]{2,1,0:T(8,128)(2,1)S(1)} %get-tuple-element.94), channel_id=1, source_target_pairs={{32,64},{64,32},{96,128},{128,96},{160,192},{192,160},{224,256},{2... | collective-permute-start | bytes 393224 | tf_op jit(solution)/shard_map/ppermute | solution.py:428
  99.5 15.6 %collective-permute-start.14 = (bf16[32,16,128]{2,1,0:T(8,128)(2,1)S(1)}, bf16[32,16,128]{2,1,0:T(8,128)(2,1)S(1)}, u32[]{:S(2)}, u32[]{:S(2)}) collective-permute-start(bf16[32,16,128]{2,1,0:T(8,128)(2,1)S(1)} %get-tuple-element.95), channel_id=1, source_target_pairs={{0,1},{1,0},{2,3},{3,2},{4,5},{5,4},{6,7},{7,6},{8,9},{9,8},{10,11... | collective-permute-start | bytes 393224 | tf_op jit(solution)/shard_map/ppermute | solution.py:429
  107.2 7.9 %collective-permute-start.15 = (bf16[16,32,128]{2,1,0:T(8,128)(2,1)S(1)}, bf16[16,32,128]{2,1,0:T(8,128)(2,1)S(1)}, u32[]{:S(2)}, u32[]{:S(2)}) collective-permute-start(bf16[16,32,128]{2,1,0:T(8,128)(2,1)S(1)} %get-tuple-element.96), channel_id=1, source_target_pairs={{0,32},{32,0},{64,96},{96,64},{128,160},{160,128},{192,224},{224,1... | collective-permute-start | bytes 393224 | tf_op jit(solution)/shard_map/ppermute | solution.py:430
  109.8 12.9 %all-to-all-start.3 = ((f32[32,8,128]{2,1,0:T(8,128)}), f32[32,8,128]{2,1,0:T(8,128)S(1)}, u32[]{:S(2)}, u32[]{:S(2)}) async-start(f32[32,8,128]{2,1,0:T(8,128)} %shard_map.130), calls=%async_computation.3 | async-start | bytes 262144 | tf_op jit(solution)/shard_map/all_to_all | solution.py:541

commit v5 on v4

--- a/solution.py
+++ b/solution.py
@@ -118,18 +118,7 @@
     return onehot((iota((feature, channels), 1) & (feature - 1)) == iota((feature, channels), 0))
 
 
-def fetch(sources, targets, sems):
-    copies = [pltpu.make_async_copy(a, b, sems.at[n]) for n, (a, b) in enumerate(zip(sources, targets))]
-    for copy in copies:
-        copy.start()
-    return copies
-
-
-def prep0_body(sta_rows, src_rows, *refs):
-    (sk, rk, sinv, rinv, wf, slists, scounts, rlists, rcounts, weights, sems) = refs[5:]
-    copies = fetch(refs[:5], refs[10:15], sems)
-    for copy in copies[:4]:
-        copy.wait()
+def prep0_body(sta_rows, src_rows, slists, scounts, rlists, rcounts, weights, sk, rk, sinv, rinv, wf):
     flag, at = even("sta")
     gather, counts = gather_counts(slists, scounts, at * sta_rows, sta_rows, flag)
     wide_sta(gather, sk, dot, sta_rows)
@@ -139,7 +128,6 @@
     gather, counts = gather_counts(rlists, rcounts, at * src_rows, src_rows, flag)
     wide_src(gather, rk, dot, src_rows)
     rinv[...] = 1.0 / dot(src_picks(src_rows), counts.astype(BF))
-    copies[4].wait()
     feature = weights.shape[-1]
     channels = 2 * feature
     twice = doubling(feature)
@@ -152,12 +140,7 @@
             wf[layer, at + feature : at + channels, :] = jnp.where(left, 0.0, plain).astype(BF)
 
 
-def prep1_body(sta_rows, src_rows, *refs):
-    sources = refs[:4]
-    (wb, px, cnt, tgt, rl) = refs[5:10]
-    picks, targets, weights, readout = refs[10:14]
-    for copy in fetch(sources, refs[10:14], refs[14]):
-        copy.wait()
+def prep1_body(sta_rows, src_rows, _, picks, targets, weights, readout, wb, px, cnt, tgt, rl):
     feature = weights.shape[-1]
     channels = 2 * feature
     unit = onehot(iota((feature, feature), 0) == iota((feature, feature), 1))
@@ -196,16 +179,17 @@
     return [pl.multiple_of(jnp.where(f, last, none), HW) for f in (flag, jnp.logical_not(flag))]
 
 
-def edge_body(x, c1, c0, r1, r0, sems):
+def edge_body(count, *refs):
+    x, rest = refs[0], refs[1:count]
+    c1, c0, r1, r0 = refs[count : count + 4]
+    sems = refs[-1]
     rows, cols, _ = x.shape
     s0, s1 = starts(SRC, cols)
     t0, t1 = starts("sta", rows)
-    copies = [
-        pltpu.make_async_copy(x.at[:, pl.ds(s1, HW)], c1, sems.at[0]),
-        pltpu.make_async_copy(x.at[:, pl.ds(s0, HW)], c0, sems.at[1]),
-        pltpu.make_async_copy(x.at[pl.ds(t1, HW)], r1, sems.at[2]),
-        pltpu.make_async_copy(x.at[pl.ds(t0, HW)], r0, sems.at[3]),
-    ]
+    moves = [(x.at[:, pl.ds(s1, HW)], c1), (x.at[pl.ds(t1, HW)], r1)]
+    moves += [(x.at[:, pl.ds(s0, HW)], c0), (x.at[pl.ds(t0, HW)], r0)]
+    moves += list(zip(rest, refs[count + 4 : -1]))
+    copies = [pltpu.make_async_copy(a, b, sems.at[n]) for n, (a, b) in enumerate(moves)]
     for copy in copies:
         copy.start()
     for copy in copies:
@@ -441,7 +425,17 @@
     ext_sta, ext_src = rows + 2 * HW, cols + 2 * HW
     tables = (station_lists.T, station_counts.reshape(1, -1), source_lists.T, source_counts.reshape(1, -1))
 
-    edges = scratch_call(edge_body, edge_outs, [pltpu.SemaphoreType.DMA((4,))], features, away=1)
+    small = tables + (layer_weights, picks, targets, readout_vector.reshape(1, -1))
+    c1, c0, r1, r0, *small = scratch_call(
+        lambda *refs: edge_body(1 + len(small), *refs),
+        edge_outs + [(x.shape, x.dtype) for x in small],
+        [pltpu.SemaphoreType.DMA((4 + len(small),))],
+        features,
+        *small,
+        away=1 + len(small),
+    )
+    edges = (c1, c0, r1, r0)
+    tables, (weights, picks, targets, readout) = small[:4], small[4:]
     sk, rk, sinv, rinv, wf = scratch_call(
         lambda *refs: prep0_body(rows, cols, *refs),
         [
@@ -451,16 +445,14 @@
             ((4 * cols, channels), F32),
             ((LAYERS, 3 * channels, channels), BF),
         ],
-        [pltpu.VMEM(x.shape, x.dtype) for x in (*tables, layer_weights)] + [pltpu.SemaphoreType.DMA((5,))],
+        [],
         *tables,
-        layer_weights,
-        away=5,
+        weights,
     )
     state_outs = [((rows, cols, 3 * channels), BF), (whole, F32)]
     h1, *edges, states0, q0 = call(
         forward0_body, [(whole, BF)] + edge_outs + state_outs, features, *halo(*edges), sk, rk, sinv, rinv, wf
     )
-    small = (picks, targets, layer_weights, readout_vector.reshape(1, -1))
     wb, px, cnt, tgt, rl = scratch_call(
         lambda *refs: prep1_body(rows, cols, *refs),
         [
@@ -470,10 +462,12 @@
             ((8, cols), F32),
             ((8, channels), F32),
         ],
-        [pltpu.VMEM(x.shape, x.dtype) for x in small] + [pltpu.SemaphoreType.DMA((4,))],
-        *small,
+        [],
         states0,
-        away=4,
+        picks,
+        targets,
+        weights,
+        readout,
     )
     states1, q1, xsum, block = call(
         forward1_body,

time: 124 us -> 124 us (level)
  Pallas kernels: 16.6 us -> 14.8 us
  blocking collectives: 24 us -> 25.3 us
    pallas_call x5, Pallas kernels: 8.26 us -> 6.41 us  [scratch_call(): pl.pallas_call(body, out_shape=[jax.ShapeDtypeStruct(s, d) for s, d in ou...]
  transfers between devices with their start and end apart: 18 -> 18, of which waited for: 1 -> 2; matrix products, arithmetic and copies ran while one was open for 0% -> 0% of each run, Pallas kernels for 7% -> 5%
where the time goes in v5:
time: 124 us; the launch traced here: 123 us
  starting transfers between devices  74.6 us (60%)
  blocking collectives  25.3 us (20%)
  Pallas kernels  14.8 us (12%)
  waiting for transfers between devices  7.27 us (6%)
    ppermute x4, starting transfers between devices, halo(): lax.ppermute(e0, SRC, src0)  31 us
    all_to_all x1, starting transfers between devices, shards(): part = lax.all_to_all(part, 'z', 0, 0)  14.5 us
    all_to_all x1, blocking collectives, shards(): part = lax.all_to_all(pay.reshape(n_plane, per, channels), PLANE, 0, 0)  13.9 us
    ppermute x4, starting transfers between devices, halo(): lax.ppermute(f1, 'sta', sta1)  13.5 us
    all_to_all x1, blocking collectives, shards(): total = lax.all_to_all(block, 'sta', 0, 0)  11.3 us
    pallas_call x7, Pallas kernels, call(): pl.pallas_call(body, out_shape=[jax.ShapeDtypeStruct(s, d) for s, d in ou...  8.38 us
    ppermute x4, starting transfers between devices, halo(): lax.ppermute(f0, 'sta', sta0)  7.68 us
    all_to_all x1, waiting for transfers between devices, shards(): part = lax.all_to_all(part, PLANE, 0, 0)  6.44 us
  transfers between devices with their start and end apart: 18, of which 2 were waited for; matrix products, arithmetic and copies ran while one was open for 0% of the time, Pallas kernels for 5%

profile of v5, /device:TPU:1, one launch (start us, length us, event | category | flops | bytes accessed | tf_op | source)
XLA Modules:
  0.0 122.9 jit_solution(9768721095873402633)
XLA Ops:
  0.6 0.0 copy-start
  0.6 1.4 %shard_map.120 = (bf16[32,16,128]{2,1,0:T(8,128)(2,1)S(1)}, bf16[32,16,128]{2,1,0:T(8,128)(2,1)S(1)}, bf16[16,32,128]{2,1,0:T(8,128)(2,1)S(1)}, bf16[16,32,128]{...) custom-call(bf16[32,32,128]{2,1,0:T(8,128)(2,1)} %h.1, ...), custom_call_target="tpu_custom_call" | custom-call | tf_op jit(solution)/shard_map/pallas_call | solution.py:388
  2.0 0.7 collective-permute-start
  2.7 4.6 %collective-permute-start.1 = (bf16[16,32,128]{2,1,0:T(8,128)(2,1)S(1)}, bf16[16,32,128]{2,1,0:T(8,128)(2,1)S(1)}, u32[]{:S(2)}, u32[]{:S(2)}) collective-permute-start(bf16[16,32,128]{2,1,0:T(8,128)(2,1)S(1)} %get-tuple-element.61), channel_id=1, source_target_pairs={{32,64},{64,32},{96,128},{128,96},{160,192},{192,160},{224,256},{2... | collective-permute-start | bytes 393224 | tf_op jit(solution)/shard_map/ppermute | solution.py:412
  7.3 7.8 %collective-permute-start.2 = (bf16[32,16,128]{2,1,0:T(8,128)(2,1)S(1)}, bf16[32,16,128]{2,1,0:T(8,128)(2,1)S(1)}, u32[]{:S(2)}, u32[]{:S(2)}) collective-permute-start(bf16[32,16,128]{2,1,0:T(8,128)(2,1)S(1)} %get-tuple-element.62), channel_id=1, source_target_pairs={{0,1},{1,0},{2,3},{3,2},{4,5},{5,4},{6,7},{7,6},{8,9},{9,8},{10,11... | collective-permute-start | bytes 393224 | tf_op jit(solution)/shard_map/ppermute | solution.py:413
  15.1 1.9 %collective-permute-start.3 = (bf16[16,32,128]{2,1,0:T(8,128)(2,1)S(1)}, bf16[16,32,128]{2,1,0:T(8,128)(2,1)S(1)}, u32[]{:S(2)}, u32[]{:S(2)}) collective-permute-start(bf16[16,32,128]{2,1,0:T(8,128)(2,1)S(1)} %get-tuple-element.63), channel_id=1, source_target_pairs={{0,32},{32,0},{64,96},{96,64},{128,160},{160,128},{192,224},{224,1... | collective-permute-start | bytes 393224 | tf_op jit(solution)/shard_map/ppermute | solution.py:414
  17.0 1.8 %shard_map.121 = (bf16[512,1024]{1,0:T(8,128)(2,1)S(1)}, bf16[128,256]{1,0:T(8,128)(2,1)S(1)}, f32[512,128]{1,0:T(8,128)S(1)}, f32[128,128]{1,0:T(8,128)S(1)}, bf16[2,384,128]{2,1,0:T(8,128)(2,1)S(1)}) custom-call(s32[16,512]{1,0:T(8,128)S(1)} %get-tuple-element.64.refs_0_.slists, s32[1,512]{1,0:T(1,128)S(1)} %get-tuple-element.65.refs_1_.scounts, ...), custom_call_target="tpu_custom_call" | custom-call | tf_op jit(solution)/shard_map/pallas_call | solution.py:388
  18.8 0.0 collective-permute-done.c1
  18.8 0.0 collective-permute-done.1.r1
  18.8 0.0 collective-permute-done.2.c0
  18.8 0.0 collective-permute-done.3.r0
  18.8 0.0 copy-done
  18.9 1.4 %shard_map.122 = (bf16[32,32,128]{2,1,0:T(8,128)(2,1)S(1)}, bf16[32,16,128]{2,1,0:T(8,128)(2,1)S(1)}, bf16[32,16,128]{2,1,0:T(8,128)(2,1)S(1)}, bf16[16,32,128]{...) custom-call(bf16[32,32,128]{2,1,0:T(8,128)(2,1)S(1)} %copy-done, ...), custom_call_target="tpu_custom_call" | custom-call | tf_op jit(solution)/shard_map/pallas_call | solution.py:38
  20.3 0.7 collective-permute-start.4
  20.9 3.6 %collective-permute-start.5 = (bf16[16,32,128]{2,1,0:T(8,128)(2,1)S(1)}, bf16[16,32,128]{2,1,0:T(8,128)(2,1)S(1)}, u32[]{:S(2)}, u32[]{:S(2)}) collective-permute-start(bf16[16,32,128]{2,1,0:T(8,128)(2,1)S(1)} %get-tuple-element.76), channel_id=1, source_target_pairs={{32,64},{64,32},{96,128},{128,96},{160,192},{192,160},{224,256},{2... | collective-permute-start | bytes 393224 | tf_op jit(solution)/shard_map/ppermute | solution.py:412
  24.5 7.8 %collective-permute-start.6 = (bf16[32,16,128]{2,1,0:T(8,128)(2,1)S(1)}, bf16[32,16,128]{2,1,0:T(8,128)(2,1)S(1)}, u32[]{:S(2)}, u32[]{:S(2)}) collective-permute-start(bf16[32,16,128]{2,1,0:T(8,128)(2,1)S(1)} %get-tuple-element.77), channel_id=1, source_target_pairs={{0,1},{1,0},{2,3},{3,2},{4,5},{5,4},{6,7},{7,6},{8,9},{9,8},{10,11... | collective-permute-start | bytes 393224 | tf_op jit(solution)/shard_map/ppermute | solution.py:413
  32.3 1.9 %collective-permute-start.7 = (bf16[16,32,128]{2,1,0:T(8,128)(2,1)S(1)}, bf16[16,32,128]{2,1,0:T(8,128)(2,1)S(1)}, u32[]{:S(2)}, u32[]{:S(2)}) collective-permute-start(bf16[16,32,128]{2,1,0:T(8,128)(2,1)S(1)} %get-tuple-element.78), channel_id=1, source_target_pairs={{0,32},{32,0},{64,96},{96,64},{128,160},{160,128},{192,224},{224,1... | collective-permute-start | bytes 393224 | tf_op jit(solution)/shard_map/ppermute | solution.py:414
  34.2 0.5 shard_map.123
  34.7 0.0 collective-permute-done.4.c1
  34.7 0.0 collective-permute-done.5.r1
  34.8 0.0 collective-permute-done.6.c0
  34.8 0.8 collective-permute-done.7.r0
  35.6 1.5 %shard_map.124 = (bf16[32,32,384]{2,1,0:T(8,128)(2,1)S(1)}, f32[32,32,128]{2,1,0:T(8,128)S(1)}, f32[32,128]{1,0:T(8,128)S(1)}, f32[16,8,128]{2,1,0:T(8,128)S(1)}) custom-call(bf16[32,32,128]{2,1,0:T(8,128)(2,1)S(1)} %get-tuple-element.74.h, bf16[32,16,128]{2,1,0:T(8,128)(2,1)S(1)} %collective-permute-done.4.c1, ...), custom_call_target="tpu_custom_call" | custom-call | tf_op jit(solution)/shard_map/pallas_call | solution.py:38
  37.0 11.3 %all_to_all.20.total = f32[16,8,128]{2,1,0:T(8,128)S(1)} all-to-all(f32[16,8,128]{2,1,0:T(8,128)S(1)} %get-tuple-element.86), channel_id=1, replica_groups=mesh['sta'=16,'z'=16,'xh'=2] {'sta'}, dimensions={0} | all-to-all | bytes 131072 | tf_op jit(solution)/shard_map/all_to_all | solution.py:486
  48.4 1.0 shard_map.125
  49.4 0.7 collective-permute-start.8
  50.1 2.5 %collective-permute-start.9 = (bf16[16,32,128]{2,1,0:T(8,128)(2,1)S(1)}, bf16[16,32,128]{2,1,0:T(8,128)(2,1)S(1)}, u32[]{:S(2)}, u32[]{:S(2)}) collective-permute-start(bf16[16,32,128]{2,1,0:T(8,128)(2,1)S(1)} %get-tuple-element.95), channel_id=1, source_target_pairs={{32,64},{64,32},{96,128},{128,96},{160,192},{192,160},{224,256},{2... | collective-permute-start | bytes 393224 | tf_op jit(solution)/shard_map/ppermute | solution.py:412
  52.6 7.8 %collective-permute-start.10 = (bf16[32,16,128]{2,1,0:T(8,128)(2,1)S(1)}, bf16[32,16,128]{2,1,0:T(8,128)(2,1)S(1)}, u32[]{:S(2)}, u32[]{:S(2)}) collective-permute-start(bf16[32,16,128]{2,1,0:T(8,128)(2,1)S(1)} %get-tuple-element.96), channel_id=1, source_target_pairs={{0,1},{1,0},{2,3},{3,2},{4,5},{5,4},{6,7},{7,6},{8,9},{9,8},{10,11... | collective-permute-start | bytes 393224 | tf_op jit(solution)/shard_map/ppermute | solution.py:413
  60.3 1.9 %collective-permute-start.11 = (bf16[16,32,128]{2,1,0:T(8,128)(2,1)S(1)}, bf16[16,32,128]{2,1,0:T(8,128)(2,1)S(1)}, u32[]{:S(2)}, u32[]{:S(2)}) collective-permute-start(bf16[16,32,128]{2,1,0:T(8,128)(2,1)S(1)} %get-tuple-element.97), channel_id=1, source_target_pairs={{0,32},{32,0},{64,96},{96,64},{128,160},{160,128},{192,224},{224,1... | collective-permute-start | bytes 393224 | tf_op jit(solution)/shard_map/ppermute | solution.py:414
  62.3 2.3 %shard_map.126 = (f32[136,128]{1,0:T(8,128)S(1)}, bf16[512,1024]{1,0:T(8,128)(2,1)S(1)}, bf16[128,256]{1,0:T(8,128)(2,1)S(1)}) custom-call(bf16[32,32,384]{2,1,0:T(8,128)(2,1)S(1)} %get-tuple-element.98.states, bf16[1024,128]{1,0:T(8,128)(2,1)S(1)} %get-tuple-element.99.delta, f32[32,128]{1,0:T(8,128)S(1)} %get-tuple-element.100.xsum, ...), custom_call_target="tpu_custom_call" | custom-call | tf_op jit(solution)/shard_map/pallas_call | solution.py:38
  64.6 0.0 collective-permute-done.8.c1
  64.6 0.0 collective-permute-done.9.r1
  64.6 0.0 collective-permute-done.10.c0
  64.6 0.0 collective-permute-done.11.r0
  64.6 1.5 %shard_map.127 = (f32[32,32,128]{2,1,0:T(8,128)S(1)}, bf16[32,32,128]{2,1,0:T(8,128)(2,1)S(1)}, bf16[32,32,128]{2,1,0:T(8,128)(2,1)S(1)}, bf16[32,16,128]{2,1,0:...) custom-call(f32[32,32,128]{2,1,0:T(8,128)S(1)} %get-tuple-element.91, ...), custom_call_target="tpu_custom_call" | custom-call | tf_op jit(solution)/shard_map/pallas_call | solution.py:388
  66.2 13.9 %all_to_all.21.x = f32[32,8,128]{2,1,0:T(8,128)S(1)} all-to-all(f32[32,8,128]{2,1,0:T(8,128)S(1)} %bitcast.7), channel_id=1, replica_groups=mesh['sta'=16,'z'=16,'xh'=2] {'sta','xh'}, dimensions={0} | all-to-all | bytes 262144 | tf_op jit(solution)/shard_map/all_to_all | solution.py:531
  80.1 0.7 shard_map.129
  80.7 14.5 %all-to-all-start.2 = ((f32[16,8,128]{2,1,0:T(8,128)}), f32[16,8,128]{2,1,0:T(8,128)S(1)}, u32[]{:S(2)}, u32[]{:S(2)}) async-start(f32[16,8,128]{2,1,0:T(8,128)} %shard_map.129), calls=%async_computation.2 | async-start | bytes 131072 | tf_op jit(solution)/shard_map/all_to_all | solution.py:533
  95.3 0.7 collective-permute-start.12
  95.9 2.9 %collective-permute-start.13 = (bf16[16,32,128]{2,1,0:T(8,128)(2,1)S(1)}, bf16[16,32,128]{2,1,0:T(8,128)(2,1)S(1)}, u32[]{:S(2)}, u32[]{:S(2)}) collective-permute-start(bf16[16,32,128]{2,1,0:T(8,128)(2,1)S(1)} %get-tuple-element.110), channel_id=1, source_target_pairs={{32,64},{64,32},{96,128},{128,96},{160,192},{192,160},{224,256},{2... | collective-permute-start | bytes 393224 | tf_op jit(solution)/shard_map/ppermute | solution.py:412
  98.8 7.7 %collective-permute-start.14 = (bf16[32,16,128]{2,1,0:T(8,128)(2,1)S(1)}, bf16[32,16,128]{2,1,0:T(8,128)(2,1)S(1)}, u32[]{:S(2)}, u32[]{:S(2)}) collective-permute-start(bf16[32,16,128]{2,1,0:T(8,128)(2,1)S(1)} %get-tuple-element.111), channel_id=1, source_target_pairs={{0,1},{1,0},{2,3},{3,2},{4,5},{5,4},{6,7},{7,6},{8,9},{9,8},{10,11... | collective-permute-start | bytes 393224 | tf_op jit(solution)/shard_map/ppermute | solution.py:413
  106.6 1.9 %collective-permute-start.15 = (bf16[16,32,128]{2,1,0:T(8,128)(2,1)S(1)}, bf16[16,32,128]{2,1,0:T(8,128)(2,1)S(1)}, u32[]{:S(2)}, u32[]{:S(2)}) collective-permute-start(bf16[16,32,128]{2,1,0:T(8,128)(2,1)S(1)} %get-tuple-element.112), channel_id=1, source_target_pairs={{0,32},{32,0},{64,96},{96,64},{128,160},{160,128},{192,224},{224,1... | collective-permute-start | bytes 393224 | tf_op jit(solution)/shard_map/ppermute | solution.py:414
  108.5 0.0 all-to-all-done.2.x
  108.5 0.7 shard_map.130
  109.2 5.2 %all-to-all-start.3 = ((f32[32,8,128]{2,1,0:T(8,128)}), f32[32,8,128]{2,1,0:T(8,128)S(1)}, u32[]{:S(2)}, u32[]{:S(2)}) async-start(f32[32,8,128]{2,1,0:T(8,128)} %shard_map.130), calls=%async_computation.3 | async-start | bytes 262144 | tf_op jit(solution)/shard_map/all_to_all | solution.py:535
  114.4 0.0 collective-permute-done.12.c1
  114.4 0.0 collective-permute-done.13.r1
  114.4 0.0 collective-permute-done.14.c0
  114.4 0.0 collective-permute-done.15.r0
  114.4 1.2 shard_map.128
  115.7 6.4 %all-to-all-done.3.refs_0_ = f32[32,8,128]{2,1,0:T(8,128)S(1)} async-done(((f32[32,8,128]{2,1,0:T(8,128)}), f32[32,8,128]{2,1,0:T(8,128)S(1)}, u32[]{:S(2)}, u32[]{:S(2)}) %all-to-all-start.3) | async-done | bytes 131104 | tf_op jit(solution)/shard_map/all_to_all | solution.py:535
  122.1 0.8 shard_map.131
Async XLA Ops:
  0.6 18.2 %copy-start = (bf16[32,32,128]{2,1,0:T(8,128)(2,1)S(1)}, bf16[32,32,128]{2,1,0:T(8,128)(2,1)}, u32[]{:S(2)}) copy-start(bf16[32,32,128]{2,1,0:T(8,128)(2,1)} %h.1) | copy-start | bytes 786436
  2.0 16.8 %collective-permute-start = (bf16[32,16,128]{2,1,0:T(8,128)(2,1)S(1)}, bf16[32,16,128]{2,1,0:T(8,128)(2,1)S(1)}, u32[]{:S(2)}, u32[]{:S(2)}) collective-permute-start(bf16[32,16,128]{2,1,0:T(8,128)(2,1)S(1)} %get-tuple-element.60), channel_id=1, source_target_pairs={{1,2},{2,1},{3,4},{4,3},{5,6},{6,5},{7,8},{8,7},{9,10},{10,9},{11,... | collective-permute-start | bytes 393224 | tf_op jit(solution)/shard_map/ppermute | solution.py:411
  2.7 16.1 %collective-permute-start.1 = (bf16[16,32,128]{2,1,0:T(8,128)(2,1)S(1)}, bf16[16,32,128]{2,1,0:T(8,128)(2,1)S(1)}, u32[]{:S(2)}, u32[]{:S(2)}) collective-permute-start(bf16[16,32,128]{2,1,0:T(8,128)(2,1)S(1)} %get-tuple-element.61), channel_id=1, source_target_pairs={{32,64},{64,32},{96,128},{128,96},{160,192},{192,160},{224,256},{2... | collective-permute-start | bytes 393224 | tf_op jit(solution)/shard_map/ppermute | solution.py:412
  7.3 11.5 %collective-permute-start.2 = (bf16[32,16,128]{2,1,0:T(8,128)(2,1)S(1)}, bf16[32,16,128]{2,1,0:T(8,128)(2,1)S(1)}, u32[]{:S(2)}, u32[]{:S(2)}) collective-permute-start(bf16[32,16,128]{2,1,0:T(8,128)(2,1)S(1)} %get-tuple-element.62), channel_id=1, source_target_pairs={{0,1},{1,0},{2,3},{3,2},{4,5},{5,4},{6,7},{7,6},{8,9},{9,8},{10,11... | collective-permute-start | bytes 393224 | tf_op jit(solution)/shard_map/ppermute | solution.py:413
  15.1 3.8 %collective-permute-start.3 = (bf16[16,32,128]{2,1,0:T(8,128)(2,1)S(1)}, bf16[16,32,128]{2,1,0:T(8,128)(2,1)S(1)}, u32[]{:S(2)}, u32[]{:S(2)}) collective-permute-start(bf16[16,32,128]{2,1,0:T(8,128)(2,1)S(1)} %get-tuple-element.63), channel_id=1, source_target_pairs={{0,32},{32,0},{64,96},{96,64},{128,160},{160,128},{192,224},{224,1... | collective-permute-start | bytes 393224 | tf_op jit(solution)/shard_map/ppermute | solution.py:414
  20.3 14.5 %collective-permute-start.4 = (bf16[32,16,128]{2,1,0:T(8,128)(2,1)S(1)}, bf16[32,16,128]{2,1,0:T(8,128)(2,1)S(1)}, u32[]{:S(2)}, u32[]{:S(2)}) collective-permute-start(bf16[32,16,128]{2,1,0:T(8,128)(2,1)S(1)} %get-tuple-element.75), channel_id=1, source_target_pairs={{1,2},{2,1},{3,4},{4,3},{5,6},{6,5},{7,8},{8,7},{9,10},{10,9},{11,... | collective-permute-start | bytes 393224 | tf_op jit(solution)/shard_map/ppermute | solution.py:411
  20.9 13.8 %collective-permute-start.5 = (bf16[16,32,128]{2,1,0:T(8,128)(2,1)S(1)}, bf16[16,32,128]{2,1,0:T(8,128)(2,1)S(1)}, u32[]{:S(2)}, u32[]{:S(2)}) collective-permute-start(bf16[16,32,128]{2,1,0:T(8,128)(2,1)S(1)} %get-tuple-element.76), channel_id=1, source_target_pairs={{32,64},{64,32},{96,128},{128,96},{160,192},{192,160},{224,256},{2... | collective-permute-start | bytes 393224 | tf_op jit(solution)/shard_map/ppermute | solution.py:412
  24.5 10.2 %collective-permute-start.6 = (bf16[32,16,128]{2,1,0:T(8,128)(2,1)S(1)}, bf16[32,16,128]{2,1,0:T(8,128)(2,1)S(1)}, u32[]{:S(2)}, u32[]{:S(2)}) collective-permute-start(bf16[32,16,128]{2,1,0:T(8,128)(2,1)S(1)} %get-tuple-element.77), channel_id=1, source_target_pairs={{0,1},{1,0},{2,3},{3,2},{4,5},{5,4},{6,7},{7,6},{8,9},{9,8},{10,11... | collective-permute-start | bytes 393224 | tf_op jit(solution)/shard_map/ppermute | solution.py:413
  32.3 3.2 %collective-permute-start.7 = (bf16[16,32,128]{2,1,0:T(8,128)(2,1)S(1)}, bf16[16,32,128]{2,1,0:T(8,128)(2,1)S(1)}, u32[]{:S(2)}, u32[]{:S(2)}) collective-permute-start(bf16[16,32,128]{2,1,0:T(8,128)(2,1)S(1)} %get-tuple-element.78), channel_id=1, source_target_pairs={{0,32},{32,0},{64,96},{96,64},{128,160},{160,128},{192,224},{224,1... | collective-permute-start | bytes 393224 | tf_op jit(solution)/shard_map/ppermute | solution.py:414
  49.4 15.2 %collective-permute-start.8 = (bf16[32,16,128]{2,1,0:T(8,128)(2,1)S(1)}, bf16[32,16,128]{2,1,0:T(8,128)(2,1)S(1)}, u32[]{:S(2)}, u32[]{:S(2)}) collective-permute-start(bf16[32,16,128]{2,1,0:T(8,128)(2,1)S(1)} %get-tuple-element.94), channel_id=1, source_target_pairs={{1,2},{2,1},{3,4},{4,3},{5,6},{6,5},{7,8},{8,7},{9,10},{10,9},{11,... | collective-permute-start | bytes 393224 | tf_op jit(solution)/shard_map/ppermute | solution.py:411
  50.1 14.5 %collective-permute-start.9 = (bf16[16,32,128]{2,1,0:T(8,128)(2,1)S(1)}, bf16[16,32,128]{2,1,0:T(8,128)(2,1)S(1)}, u32[]{:S(2)}, u32[]{:S(2)}) collective-permute-start(bf16[16,32,128]{2,1,0:T(8,128)(2,1)S(1)} %get-tuple-element.95), channel_id=1, source_target_pairs={{32,64},{64,32},{96,128},{128,96},{160,192},{192,160},{224,256},{2... | collective-permute-start | bytes 393224 | tf_op jit(solution)/shard_map/ppermute | solution.py:412
  52.6 12.0 %collective-permute-start.10 = (bf16[32,16,128]{2,1,0:T(8,128)(2,1)S(1)}, bf16[32,16,128]{2,1,0:T(8,128)(2,1)S(1)}, u32[]{:S(2)}, u32[]{:S(2)}) collective-permute-start(bf16[32,16,128]{2,1,0:T(8,128)(2,1)S(1)} %get-tuple-element.96), channel_id=1, source_target_pairs={{0,1},{1,0},{2,3},{3,2},{4,5},{5,4},{6,7},{7,6},{8,9},{9,8},{10,11... | collective-permute-start | bytes 393224 | tf_op jit(solution)/shard_map/ppermute | solution.py:413
  60.3 4.3 %collective-permute-start.11 = (bf16[16,32,128]{2,1,0:T(8,128)(2,1)S(1)}, bf16[16,32,128]{2,1,0:T(8,128)(2,1)S(1)}, u32[]{:S(2)}, u32[]{:S(2)}) collective-permute-start(bf16[16,32,128]{2,1,0:T(8,128)(2,1)S(1)} %get-tuple-element.97), channel_id=1, source_target_pairs={{0,32},{32,0},{64,96},{96,64},{128,160},{160,128},{192,224},{224,1... | collective-permute-start | bytes 393224 | tf_op jit(solution)/shard_map/ppermute | solution.py:414
  80.7 27.8 %all-to-all-start.2 = ((f32[16,8,128]{2,1,0:T(8,128)}), f32[16,8,128]{2,1,0:T(8,128)S(1)}, u32[]{:S(2)}, u32[]{:S(2)}) async-start(f32[16,8,128]{2,1,0:T(8,128)} %shard_map.129), calls=%async_computation.2 | async-start | bytes 131072 | tf_op jit(solution)/shard_map/all_to_all | solution.py:533
  95.3 19.1 %collective-permute-start.12 = (bf16[32,16,128]{2,1,0:T(8,128)(2,1)S(1)}, bf16[32,16,128]{2,1,0:T(8,128)(2,1)S(1)}, u32[]{:S(2)}, u32[]{:S(2)}) collective-permute-start(bf16[32,16,128]{2,1,0:T(8,128)(2,1)S(1)} %get-tuple-element.109), channel_id=1, source_target_pairs={{1,2},{2,1},{3,4},{4,3},{5,6},{6,5},{7,8},{8,7},{9,10},{10,9},{11,... | collective-permute-start | bytes 393224 | tf_op jit(solution)/shard_map/ppermute | solution.py:411
  95.9 18.5 %collective-permute-start.13 = (bf16[16,32,128]{2,1,0:T(8,128)(2,1)S(1)}, bf16[16,32,128]{2,1,0:T(8,128)(2,1)S(1)}, u32[]{:S(2)}, u32[]{:S(2)}) collective-permute-start(bf16[16,32,128]{2,1,0:T(8,128)(2,1)S(1)} %get-tuple-element.110), channel_id=1, source_target_pairs={{32,64},{64,32},{96,128},{128,96},{160,192},{192,160},{224,256},{2... | collective-permute-start | bytes 393224 | tf_op jit(solution)/shard_map/ppermute | solution.py:412
  98.8 15.6 %collective-permute-start.14 = (bf16[32,16,128]{2,1,0:T(8,128)(2,1)S(1)}, bf16[32,16,128]{2,1,0:T(8,128)(2,1)S(1)}, u32[]{:S(2)}, u32[]{:S(2)}) collective-permute-start(bf16[32,16,128]{2,1,0:T(8,128)(2,1)S(1)} %get-tuple-element.111), channel_id=1, source_target_pairs={{0,1},{1,0},{2,3},{3,2},{4,5},{5,4},{6,7},{7,6},{8,9},{9,8},{10,11... | collective-permute-start | bytes 393224 | tf_op jit(solution)/shard_map/ppermute | solution.py:413
  106.6 7.9 %collective-permute-start.15 = (bf16[16,32,128]{2,1,0:T(8,128)(2,1)S(1)}, bf16[16,32,128]{2,1,0:T(8,128)(2,1)S(1)}, u32[]{:S(2)}, u32[]{:S(2)}) collective-permute-start(bf16[16,32,128]{2,1,0:T(8,128)(2,1)S(1)} %get-tuple-element.112), channel_id=1, source_target_pairs={{0,32},{32,0},{64,96},{96,64},{128,160},{160,128},{192,224},{224,1... | collective-permute-start | bytes 393224 | tf_op jit(solution)/shard_map/ppermute | solution.py:414
  109.2 12.9 %all-to-all-start.3 = ((f32[32,8,128]{2,1,0:T(8,128)}), f32[32,8,128]{2,1,0:T(8,128)S(1)}, u32[]{:S(2)}, u32[]{:S(2)}) async-start(f32[32,8,128]{2,1,0:T(8,128)} %shard_map.130), calls=%async_computation.3 | async-start | bytes 262144 | tf_op jit(solution)/shard_map/all_to_all | solution.py:535

commit v6 on v5

--- a/solution.py
+++ b/solution.py
@@ -365,11 +365,12 @@
 
 
 def sum_body(x, out):
-    out[...] = jnp.broadcast_to(jnp.sum(x[...], axis=0)[None], out.shape)
+    total = jnp.sum(x[...].astype(F32), axis=0).astype(out.dtype)
+    out[...] = jnp.broadcast_to(total[None], out.shape)
 
 
 def unpack_body(factor, x, w, v):
-    flat = x[...].reshape(-1, 128) * factor
+    flat = x[...].astype(F32).reshape(-1, 128) * factor
     first = flat[0:64]
     second = flat[64:128]
     third = flat[128:192]
@@ -529,9 +530,9 @@
         last_body, [(whole, BF)], [pltpu.VMEM(whole, F32)], direct, usta, usrc, *halo(*edges), tk, qk
     )
     part = lax.all_to_all(pay.reshape(n_plane, per, channels), PLANE, 0, 0)
-    (part,) = call(sum_body, [((n_z, per, channels), F32)], part)
+    (part,) = call(sum_body, [((n_z, per, channels), BF)], part)
     part = lax.all_to_all(part, "z", 0, 0)
-    (part,) = call(sum_body, [((n_plane, per, channels), F32)], part)
+    (part,) = call(sum_body, [((n_plane, per, channels), BF)], part)
     part = lax.all_to_all(part, PLANE, 0, 0)
     nodes = float(rows * n_sta * cols * lax.axis_size("z") * lax.axis_size("xh"))
     feature = layer_weights.shape[-1]

time: 124 us -> 123 us (level)
  no operation moved by 1% of the time
where the time goes in v6:
time: 123 us; the launch traced here: 122 us
  starting transfers between devices  74.6 us (61%)
  blocking collectives  25.3 us (21%)
  Pallas kernels  14.7 us (12%)
  waiting for transfers between devices  6.78 us (6%)
    ppermute x4, starting transfers between devices, halo(): lax.ppermute(e0, SRC, src0)  31 us
    all_to_all x1, starting transfers between devices, shards(): part = lax.all_to_all(part, 'z', 0, 0)  14.5 us
    all_to_all x1, blocking collectives, shards(): part = lax.all_to_all(pay.reshape(n_plane, per, channels), PLANE, 0, 0)  13.9 us
    ppermute x4, starting transfers between devices, halo(): lax.ppermute(f1, 'sta', sta1)  13.5 us
    all_to_all x1, blocking collectives, shards(): total = lax.all_to_all(block, 'sta', 0, 0)  11.3 us
    pallas_call x7, Pallas kernels, call(): pl.pallas_call(body, out_shape=[jax.ShapeDtypeStruct(s, d) for s, d in ou...  8.34 us
    ppermute x4, starting transfers between devices, halo(): lax.ppermute(f0, 'sta', sta0)  7.68 us
    pallas_call x5, Pallas kernels, scratch_call(): pl.pallas_call(body, out_shape=[jax.ShapeDtypeStruct(s, d) for s, d in ou...  6.41 us
  transfers between devices with their start and end apart: 18, of which 2 were waited for; matrix products, arithmetic and copies ran while one was open for 0% of the time, Pallas kernels for 5%

profile of v6, /device:TPU:1, one launch (start us, length us, event | category | flops | bytes accessed | tf_op | source)
XLA Modules:
  0.0 122.4 jit_solution(11834177126861665332)
XLA Ops:
  0.6 0.0 copy-start
  0.6 1.4 %shard_map.120 = (bf16[32,16,128]{2,1,0:T(8,128)(2,1)S(1)}, bf16[32,16,128]{2,1,0:T(8,128)(2,1)S(1)}, bf16[16,32,128]{2,1,0:T(8,128)(2,1)S(1)}, bf16[16,32,128]{...) custom-call(bf16[32,32,128]{2,1,0:T(8,128)(2,1)} %h.1, ...), custom_call_target="tpu_custom_call" | custom-call | tf_op jit(solution)/shard_map/pallas_call | solution.py:389
  2.0 0.7 collective-permute-start
  2.7 4.6 %collective-permute-start.1 = (bf16[16,32,128]{2,1,0:T(8,128)(2,1)S(1)}, bf16[16,32,128]{2,1,0:T(8,128)(2,1)S(1)}, u32[]{:S(2)}, u32[]{:S(2)}) collective-permute-start(bf16[16,32,128]{2,1,0:T(8,128)(2,1)S(1)} %get-tuple-element.61), channel_id=1, source_target_pairs={{32,64},{64,32},{96,128},{128,96},{160,192},{192,160},{224,256},{2... | collective-permute-start | bytes 393224 | tf_op jit(solution)/shard_map/ppermute | solution.py:413
  7.3 7.8 %collective-permute-start.2 = (bf16[32,16,128]{2,1,0:T(8,128)(2,1)S(1)}, bf16[32,16,128]{2,1,0:T(8,128)(2,1)S(1)}, u32[]{:S(2)}, u32[]{:S(2)}) collective-permute-start(bf16[32,16,128]{2,1,0:T(8,128)(2,1)S(1)} %get-tuple-element.62), channel_id=1, source_target_pairs={{0,1},{1,0},{2,3},{3,2},{4,5},{5,4},{6,7},{7,6},{8,9},{9,8},{10,11... | collective-permute-start | bytes 393224 | tf_op jit(solution)/shard_map/ppermute | solution.py:414
  15.1 1.9 %collective-permute-start.3 = (bf16[16,32,128]{2,1,0:T(8,128)(2,1)S(1)}, bf16[16,32,128]{2,1,0:T(8,128)(2,1)S(1)}, u32[]{:S(2)}, u32[]{:S(2)}) collective-permute-start(bf16[16,32,128]{2,1,0:T(8,128)(2,1)S(1)} %get-tuple-element.63), channel_id=1, source_target_pairs={{0,32},{32,0},{64,96},{96,64},{128,160},{160,128},{192,224},{224,1... | collective-permute-start | bytes 393224 | tf_op jit(solution)/shard_map/ppermute | solution.py:415
  17.0 1.8 %shard_map.121 = (bf16[512,1024]{1,0:T(8,128)(2,1)S(1)}, bf16[128,256]{1,0:T(8,128)(2,1)S(1)}, f32[512,128]{1,0:T(8,128)S(1)}, f32[128,128]{1,0:T(8,128)S(1)}, bf16[2,384,128]{2,1,0:T(8,128)(2,1)S(1)}) custom-call(s32[16,512]{1,0:T(8,128)S(1)} %get-tuple-element.64.refs_0_.slists, s32[1,512]{1,0:T(1,128)S(1)} %get-tuple-element.65.refs_1_.scounts, ...), custom_call_target="tpu_custom_call" | custom-call | tf_op jit(solution)/shard_map/pallas_call | solution.py:389
  18.8 0.0 collective-permute-done.c1
  18.8 0.0 collective-permute-done.1.r1
  18.8 0.0 collective-permute-done.2.c0
  18.8 0.0 collective-permute-done.3.r0
  18.8 0.0 copy-done
  18.9 1.4 %shard_map.122 = (bf16[32,32,128]{2,1,0:T(8,128)(2,1)S(1)}, bf16[32,16,128]{2,1,0:T(8,128)(2,1)S(1)}, bf16[32,16,128]{2,1,0:T(8,128)(2,1)S(1)}, bf16[16,32,128]{...) custom-call(bf16[32,32,128]{2,1,0:T(8,128)(2,1)S(1)} %copy-done, ...), custom_call_target="tpu_custom_call" | custom-call | tf_op jit(solution)/shard_map/pallas_call | solution.py:38
  20.3 0.7 collective-permute-start.4
  20.9 3.6 %collective-permute-start.5 = (bf16[16,32,128]{2,1,0:T(8,128)(2,1)S(1)}, bf16[16,32,128]{2,1,0:T(8,128)(2,1)S(1)}, u32[]{:S(2)}, u32[]{:S(2)}) collective-permute-start(bf16[16,32,128]{2,1,0:T(8,128)(2,1)S(1)} %get-tuple-element.76), channel_id=1, source_target_pairs={{32,64},{64,32},{96,128},{128,96},{160,192},{192,160},{224,256},{2... | collective-permute-start | bytes 393224 | tf_op jit(solution)/shard_map/ppermute | solution.py:413
  24.5 7.8 %collective-permute-start.6 = (bf16[32,16,128]{2,1,0:T(8,128)(2,1)S(1)}, bf16[32,16,128]{2,1,0:T(8,128)(2,1)S(1)}, u32[]{:S(2)}, u32[]{:S(2)}) collective-permute-start(bf16[32,16,128]{2,1,0:T(8,128)(2,1)S(1)} %get-tuple-element.77), channel_id=1, source_target_pairs={{0,1},{1,0},{2,3},{3,2},{4,5},{5,4},{6,7},{7,6},{8,9},{9,8},{10,11... | collective-permute-start | bytes 393224 | tf_op jit(solution)/shard_map/ppermute | solution.py:414
  32.3 1.9 %collective-permute-start.7 = (bf16[16,32,128]{2,1,0:T(8,128)(2,1)S(1)}, bf16[16,32,128]{2,1,0:T(8,128)(2,1)S(1)}, u32[]{:S(2)}, u32[]{:S(2)}) collective-permute-start(bf16[16,32,128]{2,1,0:T(8,128)(2,1)S(1)} %get-tuple-element.78), channel_id=1, source_target_pairs={{0,32},{32,0},{64,96},{96,64},{128,160},{160,128},{192,224},{224,1... | collective-permute-start | bytes 393224 | tf_op jit(solution)/shard_map/ppermute | solution.py:415
  34.2 0.5 shard_map.123
  34.7 0.0 collective-permute-done.4.c1
  34.7 0.0 collective-permute-done.5.r1
  34.8 0.0 collective-permute-done.6.c0
  34.8 0.8 collective-permute-done.7.r0
  35.6 1.5 %shard_map.124 = (bf16[32,32,384]{2,1,0:T(8,128)(2,1)S(1)}, f32[32,32,128]{2,1,0:T(8,128)S(1)}, f32[32,128]{1,0:T(8,128)S(1)}, f32[16,8,128]{2,1,0:T(8,128)S(1)}) custom-call(bf16[32,32,128]{2,1,0:T(8,128)(2,1)S(1)} %get-tuple-element.74.h, bf16[32,16,128]{2,1,0:T(8,128)(2,1)S(1)} %collective-permute-done.4.c1, ...), custom_call_target="tpu_custom_call" | custom-call | tf_op jit(solution)/shard_map/pallas_call | solution.py:38
  37.0 11.3 %all_to_all.20.total = f32[16,8,128]{2,1,0:T(8,128)S(1)} all-to-all(f32[16,8,128]{2,1,0:T(8,128)S(1)} %get-tuple-element.86), channel_id=1, replica_groups=mesh['sta'=16,'z'=16,'xh'=2] {'sta'}, dimensions={0} | all-to-all | bytes 131072 | tf_op jit(solution)/shard_map/all_to_all | solution.py:487
  48.4 1.0 shard_map.125
  49.4 0.7 collective-permute-start.8
  50.1 2.5 %collective-permute-start.9 = (bf16[16,32,128]{2,1,0:T(8,128)(2,1)S(1)}, bf16[16,32,128]{2,1,0:T(8,128)(2,1)S(1)}, u32[]{:S(2)}, u32[]{:S(2)}) collective-permute-start(bf16[16,32,128]{2,1,0:T(8,128)(2,1)S(1)} %get-tuple-element.95), channel_id=1, source_target_pairs={{32,64},{64,32},{96,128},{128,96},{160,192},{192,160},{224,256},{2... | collective-permute-start | bytes 393224 | tf_op jit(solution)/shard_map/ppermute | solution.py:413
  52.6 7.8 %collective-permute-start.10 = (bf16[32,16,128]{2,1,0:T(8,128)(2,1)S(1)}, bf16[32,16,128]{2,1,0:T(8,128)(2,1)S(1)}, u32[]{:S(2)}, u32[]{:S(2)}) collective-permute-start(bf16[32,16,128]{2,1,0:T(8,128)(2,1)S(1)} %get-tuple-element.96), channel_id=1, source_target_pairs={{0,1},{1,0},{2,3},{3,2},{4,5},{5,4},{6,7},{7,6},{8,9},{9,8},{10,11... | collective-permute-start | bytes 393224 | tf_op jit(solution)/shard_map/ppermute | solution.py:414
  60.3 1.9 %collective-permute-start.11 = (bf16[16,32,128]{2,1,0:T(8,128)(2,1)S(1)}, bf16[16,32,128]{2,1,0:T(8,128)(2,1)S(1)}, u32[]{:S(2)}, u32[]{:S(2)}) collective-permute-start(bf16[16,32,128]{2,1,0:T(8,128)(2,1)S(1)} %get-tuple-element.97), channel_id=1, source_target_pairs={{0,32},{32,0},{64,96},{96,64},{128,160},{160,128},{192,224},{224,1... | collective-permute-start | bytes 393224 | tf_op jit(solution)/shard_map/ppermute | solution.py:415
  62.3 2.3 %shard_map.126 = (f32[136,128]{1,0:T(8,128)S(1)}, bf16[512,1024]{1,0:T(8,128)(2,1)S(1)}, bf16[128,256]{1,0:T(8,128)(2,1)S(1)}) custom-call(bf16[32,32,384]{2,1,0:T(8,128)(2,1)S(1)} %get-tuple-element.98.states, bf16[1024,128]{1,0:T(8,128)(2,1)S(1)} %get-tuple-element.99.delta, f32[32,128]{1,0:T(8,128)S(1)} %get-tuple-element.100.xsum, ...), custom_call_target="tpu_custom_call" | custom-call | tf_op jit(solution)/shard_map/pallas_call | solution.py:38
  64.6 0.0 collective-permute-done.8.c1
  64.6 0.0 collective-permute-done.9.r1
  64.6 0.0 collective-permute-done.10.c0
  64.6 0.0 collective-permute-done.11.r0
  64.6 1.5 %shard_map.127 = (f32[32,32,128]{2,1,0:T(8,128)S(1)}, bf16[32,32,128]{2,1,0:T(8,128)(2,1)S(1)}, bf16[32,32,128]{2,1,0:T(8,128)(2,1)S(1)}, bf16[32,16,128]{2,1,0:...) custom-call(f32[32,32,128]{2,1,0:T(8,128)S(1)} %get-tuple-element.91, ...), custom_call_target="tpu_custom_call" | custom-call | tf_op jit(solution)/shard_map/pallas_call | solution.py:389
  66.2 13.9 %all_to_all.21.x = f32[32,8,128]{2,1,0:T(8,128)S(1)} all-to-all(f32[32,8,128]{2,1,0:T(8,128)S(1)} %bitcast.7), channel_id=1, replica_groups=mesh['sta'=16,'z'=16,'xh'=2] {'sta','xh'}, dimensions={0} | all-to-all | bytes 262144 | tf_op jit(solution)/shard_map/all_to_all | solution.py:532
  80.1 0.7 shard_map.129
  80.7 14.5 %all-to-all-start.2 = ((bf16[16,8,128]{2,1,0:T(8,128)(2,1)}), bf16[16,8,128]{2,1,0:T(8,128)(2,1)S(1)}, u32[]{:S(2)}, u32[]{:S(2)}) async-start(bf16[16,8,128]{2,1,0:T(8,128)(2,1)} %shard_map.129), calls=%async_computation.2 | async-start | bytes 65536 | tf_op jit(solution)/shard_map/all_to_all | solution.py:534
  95.2 0.7 collective-permute-start.12
  95.9 2.9 %collective-permute-start.13 = (bf16[16,32,128]{2,1,0:T(8,128)(2,1)S(1)}, bf16[16,32,128]{2,1,0:T(8,128)(2,1)S(1)}, u32[]{:S(2)}, u32[]{:S(2)}) collective-permute-start(bf16[16,32,128]{2,1,0:T(8,128)(2,1)S(1)} %get-tuple-element.110), channel_id=1, source_target_pairs={{32,64},{64,32},{96,128},{128,96},{160,192},{192,160},{224,256},{2... | collective-permute-start | bytes 393224 | tf_op jit(solution)/shard_map/ppermute | solution.py:413
  98.8 7.7 %collective-permute-start.14 = (bf16[32,16,128]{2,1,0:T(8,128)(2,1)S(1)}, bf16[32,16,128]{2,1,0:T(8,128)(2,1)S(1)}, u32[]{:S(2)}, u32[]{:S(2)}) collective-permute-start(bf16[32,16,128]{2,1,0:T(8,128)(2,1)S(1)} %get-tuple-element.111), channel_id=1, source_target_pairs={{0,1},{1,0},{2,3},{3,2},{4,5},{5,4},{6,7},{7,6},{8,9},{9,8},{10,11... | collective-permute-start | bytes 393224 | tf_op jit(solution)/shard_map/ppermute | solution.py:414
  106.6 1.9 %collective-permute-start.15 = (bf16[16,32,128]{2,1,0:T(8,128)(2,1)S(1)}, bf16[16,32,128]{2,1,0:T(8,128)(2,1)S(1)}, u32[]{:S(2)}, u32[]{:S(2)}) collective-permute-start(bf16[16,32,128]{2,1,0:T(8,128)(2,1)S(1)} %get-tuple-element.112), channel_id=1, source_target_pairs={{0,32},{32,0},{64,96},{96,64},{128,160},{160,128},{192,224},{224,1... | collective-permute-start | bytes 393224 | tf_op jit(solution)/shard_map/ppermute | solution.py:415
  108.5 0.0 all-to-all-done.2.x
  108.5 0.7 shard_map.130
  109.2 5.2 %all-to-all-start.3 = ((bf16[32,8,128]{2,1,0:T(8,128)(2,1)}), bf16[32,8,128]{2,1,0:T(8,128)(2,1)S(1)}, u32[]{:S(2)}, u32[]{:S(2)}) async-start(bf16[32,8,128]{2,1,0:T(8,128)(2,1)} %shard_map.130), calls=%async_computation.3 | async-start | bytes 131072 | tf_op jit(solution)/shard_map/all_to_all | solution.py:536
  114.4 0.0 collective-permute-done.12.c1
  114.4 0.0 collective-permute-done.13.r1
  114.4 0.0 collective-permute-done.14.c0
  114.4 0.0 collective-permute-done.15.r0
  114.4 1.2 shard_map.128
  115.6 6.0 %all-to-all-done.3.refs_0_ = bf16[32,8,128]{2,1,0:T(8,128)(2,1)S(1)} async-done(((bf16[32,8,128]{2,1,0:T(8,128)(2,1)}), bf16[32,8,128]{2,1,0:T(8,128)(2,1)S(1)}, u32[]{:S(2)}, u32[]{:S(2)}) %all-to-all-start.3) | async-done | bytes 65568 | tf_op jit(solution)/shard_map/all_to_all | solution.py:536
  121.6 0.8 shard_map.131
Async XLA Ops:
  0.6 18.2 %copy-start = (bf16[32,32,128]{2,1,0:T(8,128)(2,1)S(1)}, bf16[32,32,128]{2,1,0:T(8,128)(2,1)}, u32[]{:S(2)}) copy-start(bf16[32,32,128]{2,1,0:T(8,128)(2,1)} %h.1) | copy-start | bytes 786436
  2.0 16.8 %collective-permute-start = (bf16[32,16,128]{2,1,0:T(8,128)(2,1)S(1)}, bf16[32,16,128]{2,1,0:T(8,128)(2,1)S(1)}, u32[]{:S(2)}, u32[]{:S(2)}) collective-permute-start(bf16[32,16,128]{2,1,0:T(8,128)(2,1)S(1)} %get-tuple-element.60), channel_id=1, source_target_pairs={{1,2},{2,1},{3,4},{4,3},{5,6},{6,5},{7,8},{8,7},{9,10},{10,9},{11,... | collective-permute-start | bytes 393224 | tf_op jit(solution)/shard_map/ppermute | solution.py:412
  2.7 16.1 %collective-permute-start.1 = (bf16[16,32,128]{2,1,0:T(8,128)(2,1)S(1)}, bf16[16,32,128]{2,1,0:T(8,128)(2,1)S(1)}, u32[]{:S(2)}, u32[]{:S(2)}) collective-permute-start(bf16[16,32,128]{2,1,0:T(8,128)(2,1)S(1)} %get-tuple-element.61), channel_id=1, source_target_pairs={{32,64},{64,32},{96,128},{128,96},{160,192},{192,160},{224,256},{2... | collective-permute-start | bytes 393224 | tf_op jit(solution)/shard_map/ppermute | solution.py:413
  7.3 11.5 %collective-permute-start.2 = (bf16[32,16,128]{2,1,0:T(8,128)(2,1)S(1)}, bf16[32,16,128]{2,1,0:T(8,128)(2,1)S(1)}, u32[]{:S(2)}, u32[]{:S(2)}) collective-permute-start(bf16[32,16,128]{2,1,0:T(8,128)(2,1)S(1)} %get-tuple-element.62), channel_id=1, source_target_pairs={{0,1},{1,0},{2,3},{3,2},{4,5},{5,4},{6,7},{7,6},{8,9},{9,8},{10,11... | collective-permute-start | bytes 393224 | tf_op jit(solution)/shard_map/ppermute | solution.py:414
  15.1 3.8 %collective-permute-start.3 = (bf16[16,32,128]{2,1,0:T(8,128)(2,1)S(1)}, bf16[16,32,128]{2,1,0:T(8,128)(2,1)S(1)}, u32[]{:S(2)}, u32[]{:S(2)}) collective-permute-start(bf16[16,32,128]{2,1,0:T(8,128)(2,1)S(1)} %get-tuple-element.63), channel_id=1, source_target_pairs={{0,32},{32,0},{64,96},{96,64},{128,160},{160,128},{192,224},{224,1... | collective-permute-start | bytes 393224 | tf_op jit(solution)/shard_map/ppermute | solution.py:415
  20.3 14.5 %collective-permute-start.4 = (bf16[32,16,128]{2,1,0:T(8,128)(2,1)S(1)}, bf16[32,16,128]{2,1,0:T(8,128)(2,1)S(1)}, u32[]{:S(2)}, u32[]{:S(2)}) collective-permute-start(bf16[32,16,128]{2,1,0:T(8,128)(2,1)S(1)} %get-tuple-element.75), channel_id=1, source_target_pairs={{1,2},{2,1},{3,4},{4,3},{5,6},{6,5},{7,8},{8,7},{9,10},{10,9},{11,... | collective-permute-start | bytes 393224 | tf_op jit(solution)/shard_map/ppermute | solution.py:412
  20.9 13.8 %collective-permute-start.5 = (bf16[16,32,128]{2,1,0:T(8,128)(2,1)S(1)}, bf16[16,32,128]{2,1,0:T(8,128)(2,1)S(1)}, u32[]{:S(2)}, u32[]{:S(2)}) collective-permute-start(bf16[16,32,128]{2,1,0:T(8,128)(2,1)S(1)} %get-tuple-element.76), channel_id=1, source_target_pairs={{32,64},{64,32},{96,128},{128,96},{160,192},{192,160},{224,256},{2... | collective-permute-start | bytes 393224 | tf_op jit(solution)/shard_map/ppermute | solution.py:413
  24.5 10.2 %collective-permute-start.6 = (bf16[32,16,128]{2,1,0:T(8,128)(2,1)S(1)}, bf16[32,16,128]{2,1,0:T(8,128)(2,1)S(1)}, u32[]{:S(2)}, u32[]{:S(2)}) collective-permute-start(bf16[32,16,128]{2,1,0:T(8,128)(2,1)S(1)} %get-tuple-element.77), channel_id=1, source_target_pairs={{0,1},{1,0},{2,3},{3,2},{4,5},{5,4},{6,7},{7,6},{8,9},{9,8},{10,11... | collective-permute-start | bytes 393224 | tf_op jit(solution)/shard_map/ppermute | solution.py:414
  32.3 3.2 %collective-permute-start.7 = (bf16[16,32,128]{2,1,0:T(8,128)(2,1)S(1)}, bf16[16,32,128]{2,1,0:T(8,128)(2,1)S(1)}, u32[]{:S(2)}, u32[]{:S(2)}) collective-permute-start(bf16[16,32,128]{2,1,0:T(8,128)(2,1)S(1)} %get-tuple-element.78), channel_id=1, source_target_pairs={{0,32},{32,0},{64,96},{96,64},{128,160},{160,128},{192,224},{224,1... | collective-permute-start | bytes 393224 | tf_op jit(solution)/shard_map/ppermute | solution.py:415
  49.4 15.2 %collective-permute-start.8 = (bf16[32,16,128]{2,1,0:T(8,128)(2,1)S(1)}, bf16[32,16,128]{2,1,0:T(8,128)(2,1)S(1)}, u32[]{:S(2)}, u32[]{:S(2)}) collective-permute-start(bf16[32,16,128]{2,1,0:T(8,128)(2,1)S(1)} %get-tuple-element.94), channel_id=1, source_target_pairs={{1,2},{2,1},{3,4},{4,3},{5,6},{6,5},{7,8},{8,7},{9,10},{10,9},{11,... | collective-permute-start | bytes 393224 | tf_op jit(solution)/shard_map/ppermute | solution.py:412
  50.1 14.5 %collective-permute-start.9 = (bf16[16,32,128]{2,1,0:T(8,128)(2,1)S(1)}, bf16[16,32,128]{2,1,0:T(8,128)(2,1)S(1)}, u32[]{:S(2)}, u32[]{:S(2)}) collective-permute-start(bf16[16,32,128]{2,1,0:T(8,128)(2,1)S(1)} %get-tuple-element.95), channel_id=1, source_target_pairs={{32,64},{64,32},{96,128},{128,96},{160,192},{192,160},{224,256},{2... | collective-permute-start | bytes 393224 | tf_op jit(solution)/shard_map/ppermute | solution.py:413
  52.6 12.0 %collective-permute-start.10 = (bf16[32,16,128]{2,1,0:T(8,128)(2,1)S(1)}, bf16[32,16,128]{2,1,0:T(8,128)(2,1)S(1)}, u32[]{:S(2)}, u32[]{:S(2)}) collective-permute-start(bf16[32,16,128]{2,1,0:T(8,128)(2,1)S(1)} %get-tuple-element.96), channel_id=1, source_target_pairs={{0,1},{1,0},{2,3},{3,2},{4,5},{5,4},{6,7},{7,6},{8,9},{9,8},{10,11... | collective-permute-start | bytes 393224 | tf_op jit(solution)/shard_map/ppermute | solution.py:414
  60.3 4.3 %collective-permute-start.11 = (bf16[16,32,128]{2,1,0:T(8,128)(2,1)S(1)}, bf16[16,32,128]{2,1,0:T(8,128)(2,1)S(1)}, u32[]{:S(2)}, u32[]{:S(2)}) collective-permute-start(bf16[16,32,128]{2,1,0:T(8,128)(2,1)S(1)} %get-tuple-element.97), channel_id=1, source_target_pairs={{0,32},{32,0},{64,96},{96,64},{128,160},{160,128},{192,224},{224,1... | collective-permute-start | bytes 393224 | tf_op jit(solution)/shard_map/ppermute | solution.py:415
  80.7 27.8 %all-to-all-start.2 = ((bf16[16,8,128]{2,1,0:T(8,128)(2,1)}), bf16[16,8,128]{2,1,0:T(8,128)(2,1)S(1)}, u32[]{:S(2)}, u32[]{:S(2)}) async-start(bf16[16,8,128]{2,1,0:T(8,128)(2,1)} %shard_map.129), calls=%async_computation.2 | async-start | bytes 65536 | tf_op jit(solution)/shard_map/all_to_all | solution.py:534
  95.2 19.1 %collective-permute-start.12 = (bf16[32,16,128]{2,1,0:T(8,128)(2,1)S(1)}, bf16[32,16,128]{2,1,0:T(8,128)(2,1)S(1)}, u32[]{:S(2)}, u32[]{:S(2)}) collective-permute-start(bf16[32,16,128]{2,1,0:T(8,128)(2,1)S(1)} %get-tuple-element.109), channel_id=1, source_target_pairs={{1,2},{2,1},{3,4},{4,3},{5,6},{6,5},{7,8},{8,7},{9,10},{10,9},{11,... | collective-permute-start | bytes 393224 | tf_op jit(solution)/shard_map/ppermute | solution.py:412
  95.9 18.5 %collective-permute-start.13 = (bf16[16,32,128]{2,1,0:T(8,128)(2,1)S(1)}, bf16[16,32,128]{2,1,0:T(8,128)(2,1)S(1)}, u32[]{:S(2)}, u32[]{:S(2)}) collective-permute-start(bf16[16,32,128]{2,1,0:T(8,128)(2,1)S(1)} %get-tuple-element.110), channel_id=1, source_target_pairs={{32,64},{64,32},{96,128},{128,96},{160,192},{192,160},{224,256},{2... | collective-permute-start | bytes 393224 | tf_op jit(solution)/shard_map/ppermute | solution.py:413
  98.8 15.6 %collective-permute-start.14 = (bf16[32,16,128]{2,1,0:T(8,128)(2,1)S(1)}, bf16[32,16,128]{2,1,0:T(8,128)(2,1)S(1)}, u32[]{:S(2)}, u32[]{:S(2)}) collective-permute-start(bf16[32,16,128]{2,1,0:T(8,128)(2,1)S(1)} %get-tuple-element.111), channel_id=1, source_target_pairs={{0,1},{1,0},{2,3},{3,2},{4,5},{5,4},{6,7},{7,6},{8,9},{9,8},{10,11... | collective-permute-start | bytes 393224 | tf_op jit(solution)/shard_map/ppermute | solution.py:414
  106.6 7.8 %collective-permute-start.15 = (bf16[16,32,128]{2,1,0:T(8,128)(2,1)S(1)}, bf16[16,32,128]{2,1,0:T(8,128)(2,1)S(1)}, u32[]{:S(2)}, u32[]{:S(2)}) collective-permute-start(bf16[16,32,128]{2,1,0:T(8,128)(2,1)S(1)} %get-tuple-element.112), channel_id=1, source_target_pairs={{0,32},{32,0},{64,96},{96,64},{128,160},{160,128},{192,224},{224,1... | collective-permute-start | bytes 393224 | tf_op jit(solution)/shard_map/ppermute | solution.py:415
  109.2 12.4 %all-to-all-start.3 = ((bf16[32,8,128]{2,1,0:T(8,128)(2,1)}), bf16[32,8,128]{2,1,0:T(8,128)(2,1)S(1)}, u32[]{:S(2)}, u32[]{:S(2)}) async-start(bf16[32,8,128]{2,1,0:T(8,128)(2,1)} %shard_map.130), calls=%async_computation.3 | async-start | bytes 131072 | tf_op jit(solution)/shard_map/all_to_all | solution.py:536

commit v7 on v5

--- a/solution.py
+++ b/solution.py
@@ -118,7 +118,11 @@
     return onehot((iota((feature, channels), 1) & (feature - 1)) == iota((feature, channels), 0))
 
 
-def prep0_body(sta_rows, src_rows, slists, scounts, rlists, rcounts, weights, sk, rk, sinv, rinv, wf):
+def prep0_body(sta_rows, src_rows, slists, scounts, rlists, rcounts, weights, sk, rk, sinv, rinv, wf, tk, qk):
+    flag, at = even("sta")
+    wide_sta(scatter_counts(slists, scounts, at * sta_rows, sta_rows, flag), tk, dot_nt, sta_rows)
+    flag, at = even(SRC)
+    wide_src(scatter_counts(rlists, rcounts, at * src_rows, src_rows, flag), qk, dot_nt, src_rows)
     flag, at = even("sta")
     gather, counts = gather_counts(slists, scounts, at * sta_rows, sta_rows, flag)
     wide_sta(gather, sk, dot, sta_rows)
@@ -311,12 +315,7 @@
     store_edges(usta, usrc, e1, e0, f1, f0)
 
 
-def weight1_body(states, delta, xsum, errs, slists, scounts, rlists, rcounts, wpart, tk, qk):
-    sta_rows, src_rows, _ = states.shape
-    flag, at = even("sta")
-    wide_sta(scatter_counts(slists, scounts, at * sta_rows, sta_rows, flag), tk, dot_nt, sta_rows)
-    flag, at = even(SRC)
-    wide_src(scatter_counts(rlists, rcounts, at * src_rows, src_rows, flag), qk, dot_nt, src_rows)
+def weight1_body(states, delta, xsum, errs, wpart):
     pairs = outer_pairs(states, delta)
     lane = iota((64, 128), 1) < 64
     wpart[0:64, :] = jnp.where(lane, pairs[0][0], pairs[1][1])
@@ -436,7 +435,7 @@
     )
     edges = (c1, c0, r1, r0)
     tables, (weights, picks, targets, readout) = small[:4], small[4:]
-    sk, rk, sinv, rinv, wf = scratch_call(
+    sk, rk, sinv, rinv, wf, tk, qk = scratch_call(
         lambda *refs: prep0_body(rows, cols, *refs),
         [
             ((rows * HW, ext_sta * HW), BF),
@@ -444,6 +443,8 @@
             ((rows * HW, channels), F32),
             ((4 * cols, channels), F32),
             ((LAYERS, 3 * channels, channels), BF),
+            ((rows * HW, ext_sta * HW), BF),
+            ((4 * cols, 4 * ext_src), BF),
         ],
         [],
         *tables,
@@ -498,15 +499,7 @@
         sinv,
         rinv,
     )
-    wpart, tk, qk = call(
-        weight1_body,
-        [((136, channels), F32), ((rows * HW, ext_sta * HW), BF), ((4 * cols, 4 * ext_src), BF)],
-        states1,
-        delta,
-        xsum,
-        errs,
-        *tables,
-    )
+    (wpart,) = call(weight1_body, [((136, channels), F32)], states1, delta, xsum, errs)
     per = -(-200 // (8 * n_plane)) * 8
     direct, usta, usrc, *edges, pay = scratch_call(
         backward0_body,

time: 124 us -> 125 us (level)
    pallas_call x5, Pallas kernels: 6.41 us -> 8.31 us  [scratch_call(): pl.pallas_call(body, out_shape=[jax.ShapeDtypeStruct(s, d) for s, d in ou...]
    pallas_call x7, Pallas kernels: 8.38 us -> 6.56 us  [call(): pl.pallas_call(body, out_shape=[jax.ShapeDtypeStruct(s, d) for s, d in ou...]
  transfers between devices with their start and end apart: 18 -> 18, of which waited for: 2 -> 4; matrix products, arithmetic and copies ran while one was open for 0% -> 0% of each run, Pallas kernels for 5% -> 5%
where the time goes in v7:
time: 125 us; the launch traced here: 124 us
  starting transfers between devices  74.4 us (60%)
  blocking collectives  25.5 us (20%)
  Pallas kernels  14.9 us (12%)
  waiting for transfers between devices  8.06 us (6%)
    ppermute x4, starting transfers between devices, halo(): lax.ppermute(e0, SRC, src0)  31 us
    all_to_all x1, blocking collectives, shards(): part = lax.all_to_all(pay.reshape(n_plane, per, channels), PLANE, 0, 0)  15 us
    all_to_all x1, starting transfers between devices, shards(): part = lax.all_to_all(part, 'z', 0, 0)  14.3 us
    ppermute x4, starting transfers between devices, halo(): lax.ppermute(f1, 'sta', sta1)  13.5 us
    all_to_all x1, blocking collectives, shards(): total = lax.all_to_all(block, 'sta', 0, 0)  10.5 us
    pallas_call x5, Pallas kernels, scratch_call(): pl.pallas_call(body, out_shape=[jax.ShapeDtypeStruct(s, d) for s, d in ou...  8.31 us
    ppermute x4, starting transfers between devices, halo(): lax.ppermute(f0, 'sta', sta0)  7.68 us
    pallas_call x7, Pallas kernels, call(): pl.pallas_call(body, out_shape=[jax.ShapeDtypeStruct(s, d) for s, d in ou...  6.56 us
  transfers between devices with their start and end apart: 18, of which 4 were waited for; matrix products, arithmetic and copies ran while one was open for 0% of the time, Pallas kernels for 5%

profile of v7, /device:TPU:1, one launch (start us, length us, event | category | flops | bytes accessed | tf_op | source)
XLA Modules:
  0.0 123.8 jit_solution(8448841776949741286)
XLA Ops:
  0.6 0.0 copy-start
  0.6 1.4 %shard_map.120 = (bf16[32,16,128]{2,1,0:T(8,128)(2,1)S(1)}, bf16[32,16,128]{2,1,0:T(8,128)(2,1)S(1)}, bf16[16,32,128]{2,1,0:T(8,128)(2,1)S(1)}, bf16[16,32,128]{...) custom-call(bf16[32,32,128]{2,1,0:T(8,128)(2,1)} %h.1, ...), custom_call_target="tpu_custom_call" | custom-call | tf_op jit(solution)/shard_map/pallas_call | solution.py:387
  2.0 0.7 collective-permute-start
  2.7 4.6 %collective-permute-start.1 = (bf16[16,32,128]{2,1,0:T(8,128)(2,1)S(1)}, bf16[16,32,128]{2,1,0:T(8,128)(2,1)S(1)}, u32[]{:S(2)}, u32[]{:S(2)}) collective-permute-start(bf16[16,32,128]{2,1,0:T(8,128)(2,1)S(1)} %get-tuple-element.60), channel_id=1, source_target_pairs={{32,64},{64,32},{96,128},{128,96},{160,192},{192,160},{224,256},{2... | collective-permute-start | bytes 393224 | tf_op jit(solution)/shard_map/ppermute | solution.py:411
  7.3 7.8 %collective-permute-start.2 = (bf16[32,16,128]{2,1,0:T(8,128)(2,1)S(1)}, bf16[32,16,128]{2,1,0:T(8,128)(2,1)S(1)}, u32[]{:S(2)}, u32[]{:S(2)}) collective-permute-start(bf16[32,16,128]{2,1,0:T(8,128)(2,1)S(1)} %get-tuple-element.61), channel_id=1, source_target_pairs={{0,1},{1,0},{2,3},{3,2},{4,5},{5,4},{6,7},{7,6},{8,9},{9,8},{10,11... | collective-permute-start | bytes 393224 | tf_op jit(solution)/shard_map/ppermute | solution.py:412
  15.1 1.9 %collective-permute-start.3 = (bf16[16,32,128]{2,1,0:T(8,128)(2,1)S(1)}, bf16[16,32,128]{2,1,0:T(8,128)(2,1)S(1)}, u32[]{:S(2)}, u32[]{:S(2)}) collective-permute-start(bf16[16,32,128]{2,1,0:T(8,128)(2,1)S(1)} %get-tuple-element.62), channel_id=1, source_target_pairs={{0,32},{32,0},{64,96},{96,64},{128,160},{160,128},{192,224},{224,1... | collective-permute-start | bytes 393224 | tf_op jit(solution)/shard_map/ppermute | solution.py:413
  17.0 3.7 %shard_map.121 = (bf16[512,1024]{1,0:T(8,128)(2,1)S(1)}, bf16[128,256]{1,0:T(8,128)(2,1)S(1)}, f32[512,128]{1,0:T(8,128)S(1)}, f32[128,128]{1,0:T(8,128)S(1)}, b...) custom-call(s32[16,512]{1,0:T(8,128)S(1)} %get-tuple-element.63.refs_0_, ...), custom_call_target="tpu_custom_call" | custom-call | tf_op jit(solution)/shard_map/pallas_call | solution.py:387
  20.7 0.0 collective-permute-done.c1
  20.7 0.0 collective-permute-done.1.r1
  20.7 0.0 collective-permute-done.2.c0
  20.8 0.0 collective-permute-done.3.r0
  20.8 0.0 copy-done
  20.8 1.4 %shard_map.122 = (bf16[32,32,128]{2,1,0:T(8,128)(2,1)S(1)}, bf16[32,16,128]{2,1,0:T(8,128)(2,1)S(1)}, bf16[32,16,128]{2,1,0:T(8,128)(2,1)S(1)}, bf16[16,32,128]{...) custom-call(bf16[32,32,128]{2,1,0:T(8,128)(2,1)S(1)} %copy-done, ...), custom_call_target="tpu_custom_call" | custom-call | tf_op jit(solution)/shard_map/pallas_call | solution.py:38
  22.2 0.7 collective-permute-start.4
  22.9 3.6 %collective-permute-start.5 = (bf16[16,32,128]{2,1,0:T(8,128)(2,1)S(1)}, bf16[16,32,128]{2,1,0:T(8,128)(2,1)S(1)}, u32[]{:S(2)}, u32[]{:S(2)}) collective-permute-start(bf16[16,32,128]{2,1,0:T(8,128)(2,1)S(1)} %get-tuple-element.75), channel_id=1, source_target_pairs={{32,64},{64,32},{96,128},{128,96},{160,192},{192,160},{224,256},{2... | collective-permute-start | bytes 393224 | tf_op jit(solution)/shard_map/ppermute | solution.py:411
  26.5 7.7 %collective-permute-start.6 = (bf16[32,16,128]{2,1,0:T(8,128)(2,1)S(1)}, bf16[32,16,128]{2,1,0:T(8,128)(2,1)S(1)}, u32[]{:S(2)}, u32[]{:S(2)}) collective-permute-start(bf16[32,16,128]{2,1,0:T(8,128)(2,1)S(1)} %get-tuple-element.76), channel_id=1, source_target_pairs={{0,1},{1,0},{2,3},{3,2},{4,5},{5,4},{6,7},{7,6},{8,9},{9,8},{10,11... | collective-permute-start | bytes 393224 | tf_op jit(solution)/shard_map/ppermute | solution.py:412
  34.2 1.9 %collective-permute-start.7 = (bf16[16,32,128]{2,1,0:T(8,128)(2,1)S(1)}, bf16[16,32,128]{2,1,0:T(8,128)(2,1)S(1)}, u32[]{:S(2)}, u32[]{:S(2)}) collective-permute-start(bf16[16,32,128]{2,1,0:T(8,128)(2,1)S(1)} %get-tuple-element.77), channel_id=1, source_target_pairs={{0,32},{32,0},{64,96},{96,64},{128,160},{160,128},{192,224},{224,1... | collective-permute-start | bytes 393224 | tf_op jit(solution)/shard_map/ppermute | solution.py:413
  36.1 0.5 shard_map.123
  36.6 0.0 collective-permute-done.4.c1
  36.6 0.0 collective-permute-done.5.r1
  36.7 0.0 collective-permute-done.6.c0
  36.7 0.8 collective-permute-done.7.r0
  37.5 1.5 %shard_map.124 = (bf16[32,32,384]{2,1,0:T(8,128)(2,1)S(1)}, f32[32,32,128]{2,1,0:T(8,128)S(1)}, f32[32,128]{1,0:T(8,128)S(1)}, f32[16,8,128]{2,1,0:T(8,128)S(1)}) custom-call(bf16[32,32,128]{2,1,0:T(8,128)(2,1)S(1)} %get-tuple-element.73.h, bf16[32,16,128]{2,1,0:T(8,128)(2,1)S(1)} %collective-permute-done.4.c1, ...), custom_call_target="tpu_custom_call" | custom-call | tf_op jit(solution)/shard_map/pallas_call | solution.py:38
  39.0 10.5 %all_to_all.20.total = f32[16,8,128]{2,1,0:T(8,128)S(1)} all-to-all(f32[16,8,128]{2,1,0:T(8,128)S(1)} %get-tuple-element.85), channel_id=1, replica_groups=mesh['sta'=16,'z'=16,'xh'=2] {'sta'}, dimensions={0} | all-to-all | bytes 131072 | tf_op jit(solution)/shard_map/all_to_all | solution.py:487
  49.5 1.0 shard_map.125
  50.5 0.7 collective-permute-start.8
  51.2 2.5 %collective-permute-start.9 = (bf16[16,32,128]{2,1,0:T(8,128)(2,1)S(1)}, bf16[16,32,128]{2,1,0:T(8,128)(2,1)S(1)}, u32[]{:S(2)}, u32[]{:S(2)}) collective-permute-start(bf16[16,32,128]{2,1,0:T(8,128)(2,1)S(1)} %get-tuple-element.94), channel_id=1, source_target_pairs={{32,64},{64,32},{96,128},{128,96},{160,192},{192,160},{224,256},{2... | collective-permute-start | bytes 393224 | tf_op jit(solution)/shard_map/ppermute | solution.py:411
  53.7 7.8 %collective-permute-start.10 = (bf16[32,16,128]{2,1,0:T(8,128)(2,1)S(1)}, bf16[32,16,128]{2,1,0:T(8,128)(2,1)S(1)}, u32[]{:S(2)}, u32[]{:S(2)}) collective-permute-start(bf16[32,16,128]{2,1,0:T(8,128)(2,1)S(1)} %get-tuple-element.95), channel_id=1, source_target_pairs={{0,1},{1,0},{2,3},{3,2},{4,5},{5,4},{6,7},{7,6},{8,9},{9,8},{10,11... | collective-permute-start | bytes 393224 | tf_op jit(solution)/shard_map/ppermute | solution.py:412
  61.4 1.9 %collective-permute-start.11 = (bf16[16,32,128]{2,1,0:T(8,128)(2,1)S(1)}, bf16[16,32,128]{2,1,0:T(8,128)(2,1)S(1)}, u32[]{:S(2)}, u32[]{:S(2)}) collective-permute-start(bf16[16,32,128]{2,1,0:T(8,128)(2,1)S(1)} %get-tuple-element.96), channel_id=1, source_target_pairs={{0,32},{32,0},{64,96},{96,64},{128,160},{160,128},{192,224},{224,1... | collective-permute-start | bytes 393224 | tf_op jit(solution)/shard_map/ppermute | solution.py:413
  63.4 0.5 shard_map.126.wpart
  63.9 0.0 collective-permute-done.8.c1
  63.9 0.0 collective-permute-done.9.r1
  63.9 0.1 collective-permute-done.10.c0
  64.0 0.7 collective-permute-done.11.r0
  64.7 1.5 %shard_map.127 = (f32[32,32,128]{2,1,0:T(8,128)S(1)}, bf16[32,32,128]{2,1,0:T(8,128)(2,1)S(1)}, bf16[32,32,128]{2,1,0:T(8,128)(2,1)S(1)}, bf16[32,16,128]{2,1,0:...) custom-call(f32[32,32,128]{2,1,0:T(8,128)S(1)} %get-tuple-element.90, ...), custom_call_target="tpu_custom_call" | custom-call | tf_op jit(solution)/shard_map/pallas_call | solution.py:387
  66.2 15.0 %all_to_all.21.x = f32[32,8,128]{2,1,0:T(8,128)S(1)} all-to-all(f32[32,8,128]{2,1,0:T(8,128)S(1)} %bitcast.7), channel_id=1, replica_groups=mesh['sta'=16,'z'=16,'xh'=2] {'sta','xh'}, dimensions={0} | all-to-all | bytes 262144 | tf_op jit(solution)/shard_map/all_to_all | solution.py:524
  81.2 0.7 shard_map.129
  81.9 14.3 %all-to-all-start.2 = ((f32[16,8,128]{2,1,0:T(8,128)}), f32[16,8,128]{2,1,0:T(8,128)S(1)}, u32[]{:S(2)}, u32[]{:S(2)}) async-start(f32[16,8,128]{2,1,0:T(8,128)} %shard_map.129), calls=%async_computation.2 | async-start | bytes 131072 | tf_op jit(solution)/shard_map/all_to_all | solution.py:526
  96.2 0.7 collective-permute-start.12
  96.9 2.9 %collective-permute-start.13 = (bf16[16,32,128]{2,1,0:T(8,128)(2,1)S(1)}, bf16[16,32,128]{2,1,0:T(8,128)(2,1)S(1)}, u32[]{:S(2)}, u32[]{:S(2)}) collective-permute-start(bf16[16,32,128]{2,1,0:T(8,128)(2,1)S(1)} %get-tuple-element.108), channel_id=1, source_target_pairs={{32,64},{64,32},{96,128},{128,96},{160,192},{192,160},{224,256},{2... | collective-permute-start | bytes 393224 | tf_op jit(solution)/shard_map/ppermute | solution.py:411
  99.7 7.7 %collective-permute-start.14 = (bf16[32,16,128]{2,1,0:T(8,128)(2,1)S(1)}, bf16[32,16,128]{2,1,0:T(8,128)(2,1)S(1)}, u32[]{:S(2)}, u32[]{:S(2)}) collective-permute-start(bf16[32,16,128]{2,1,0:T(8,128)(2,1)S(1)} %get-tuple-element.109), channel_id=1, source_target_pairs={{0,1},{1,0},{2,3},{3,2},{4,5},{5,4},{6,7},{7,6},{8,9},{9,8},{10,11... | collective-permute-start | bytes 393224 | tf_op jit(solution)/shard_map/ppermute | solution.py:412
  107.5 1.9 %collective-permute-start.15 = (bf16[16,32,128]{2,1,0:T(8,128)(2,1)S(1)}, bf16[16,32,128]{2,1,0:T(8,128)(2,1)S(1)}, u32[]{:S(2)}, u32[]{:S(2)}) collective-permute-start(bf16[16,32,128]{2,1,0:T(8,128)(2,1)S(1)} %get-tuple-element.110), channel_id=1, source_target_pairs={{0,32},{32,0},{64,96},{96,64},{128,160},{160,128},{192,224},{224,1... | collective-permute-start | bytes 393224 | tf_op jit(solution)/shard_map/ppermute | solution.py:413
  109.4 0.0 all-to-all-done.2.x
  109.4 0.7 shard_map.130
  110.1 5.2 %all-to-all-start.3 = ((f32[32,8,128]{2,1,0:T(8,128)}), f32[32,8,128]{2,1,0:T(8,128)S(1)}, u32[]{:S(2)}, u32[]{:S(2)}) async-start(f32[32,8,128]{2,1,0:T(8,128)} %shard_map.130), calls=%async_computation.3 | async-start | bytes 262144 | tf_op jit(solution)/shard_map/all_to_all | solution.py:528
  115.3 0.0 collective-permute-done.12.c1
  115.3 0.0 collective-permute-done.13.r1
  115.3 0.0 collective-permute-done.14.c0
  115.4 0.0 collective-permute-done.15.r0
  115.4 1.2 shard_map.128
  116.6 6.4 %all-to-all-done.3.refs_0_ = f32[32,8,128]{2,1,0:T(8,128)S(1)} async-done(((f32[32,8,128]{2,1,0:T(8,128)}), f32[32,8,128]{2,1,0:T(8,128)S(1)}, u32[]{:S(2)}, u32[]{:S(2)}) %all-to-all-start.3) | async-done | bytes 131104 | tf_op jit(solution)/shard_map/all_to_all | solution.py:528
  123.0 0.8 shard_map.131
Async XLA Ops:
  0.6 20.1 %copy-start = (bf16[32,32,128]{2,1,0:T(8,128)(2,1)S(1)}, bf16[32,32,128]{2,1,0:T(8,128)(2,1)}, u32[]{:S(2)}) copy-start(bf16[32,32,128]{2,1,0:T(8,128)(2,1)} %h.1) | copy-start | bytes 786436
  2.0 18.7 %collective-permute-start = (bf16[32,16,128]{2,1,0:T(8,128)(2,1)S(1)}, bf16[32,16,128]{2,1,0:T(8,128)(2,1)S(1)}, u32[]{:S(2)}, u32[]{:S(2)}) collective-permute-start(bf16[32,16,128]{2,1,0:T(8,128)(2,1)S(1)} %get-tuple-element.59), channel_id=1, source_target_pairs={{1,2},{2,1},{3,4},{4,3},{5,6},{6,5},{7,8},{8,7},{9,10},{10,9},{11,... | collective-permute-start | bytes 393224 | tf_op jit(solution)/shard_map/ppermute | solution.py:410
  2.7 18.0 %collective-permute-start.1 = (bf16[16,32,128]{2,1,0:T(8,128)(2,1)S(1)}, bf16[16,32,128]{2,1,0:T(8,128)(2,1)S(1)}, u32[]{:S(2)}, u32[]{:S(2)}) collective-permute-start(bf16[16,32,128]{2,1,0:T(8,128)(2,1)S(1)} %get-tuple-element.60), channel_id=1, source_target_pairs={{32,64},{64,32},{96,128},{128,96},{160,192},{192,160},{224,256},{2... | collective-permute-start | bytes 393224 | tf_op jit(solution)/shard_map/ppermute | solution.py:411
  7.3 13.4 %collective-permute-start.2 = (bf16[32,16,128]{2,1,0:T(8,128)(2,1)S(1)}, bf16[32,16,128]{2,1,0:T(8,128)(2,1)S(1)}, u32[]{:S(2)}, u32[]{:S(2)}) collective-permute-start(bf16[32,16,128]{2,1,0:T(8,128)(2,1)S(1)} %get-tuple-element.61), channel_id=1, source_target_pairs={{0,1},{1,0},{2,3},{3,2},{4,5},{5,4},{6,7},{7,6},{8,9},{9,8},{10,11... | collective-permute-start | bytes 393224 | tf_op jit(solution)/shard_map/ppermute | solution.py:412
  15.1 5.7 %collective-permute-start.3 = (bf16[16,32,128]{2,1,0:T(8,128)(2,1)S(1)}, bf16[16,32,128]{2,1,0:T(8,128)(2,1)S(1)}, u32[]{:S(2)}, u32[]{:S(2)}) collective-permute-start(bf16[16,32,128]{2,1,0:T(8,128)(2,1)S(1)} %get-tuple-element.62), channel_id=1, source_target_pairs={{0,32},{32,0},{64,96},{96,64},{128,160},{160,128},{192,224},{224,1... | collective-permute-start | bytes 393224 | tf_op jit(solution)/shard_map/ppermute | solution.py:413
  22.2 14.4 %collective-permute-start.4 = (bf16[32,16,128]{2,1,0:T(8,128)(2,1)S(1)}, bf16[32,16,128]{2,1,0:T(8,128)(2,1)S(1)}, u32[]{:S(2)}, u32[]{:S(2)}) collective-permute-start(bf16[32,16,128]{2,1,0:T(8,128)(2,1)S(1)} %get-tuple-element.74), channel_id=1, source_target_pairs={{1,2},{2,1},{3,4},{4,3},{5,6},{6,5},{7,8},{8,7},{9,10},{10,9},{11,... | collective-permute-start | bytes 393224 | tf_op jit(solution)/shard_map/ppermute | solution.py:410
  22.9 13.8 %collective-permute-start.5 = (bf16[16,32,128]{2,1,0:T(8,128)(2,1)S(1)}, bf16[16,32,128]{2,1,0:T(8,128)(2,1)S(1)}, u32[]{:S(2)}, u32[]{:S(2)}) collective-permute-start(bf16[16,32,128]{2,1,0:T(8,128)(2,1)S(1)} %get-tuple-element.75), channel_id=1, source_target_pairs={{32,64},{64,32},{96,128},{128,96},{160,192},{192,160},{224,256},{2... | collective-permute-start | bytes 393224 | tf_op jit(solution)/shard_map/ppermute | solution.py:411
  26.5 10.2 %collective-permute-start.6 = (bf16[32,16,128]{2,1,0:T(8,128)(2,1)S(1)}, bf16[32,16,128]{2,1,0:T(8,128)(2,1)S(1)}, u32[]{:S(2)}, u32[]{:S(2)}) collective-permute-start(bf16[32,16,128]{2,1,0:T(8,128)(2,1)S(1)} %get-tuple-element.76), channel_id=1, source_target_pairs={{0,1},{1,0},{2,3},{3,2},{4,5},{5,4},{6,7},{7,6},{8,9},{9,8},{10,11... | collective-permute-start | bytes 393224 | tf_op jit(solution)/shard_map/ppermute | solution.py:412
  34.2 3.2 %collective-permute-start.7 = (bf16[16,32,128]{2,1,0:T(8,128)(2,1)S(1)}, bf16[16,32,128]{2,1,0:T(8,128)(2,1)S(1)}, u32[]{:S(2)}, u32[]{:S(2)}) collective-permute-start(bf16[16,32,128]{2,1,0:T(8,128)(2,1)S(1)} %get-tuple-element.77), channel_id=1, source_target_pairs={{0,32},{32,0},{64,96},{96,64},{128,160},{160,128},{192,224},{224,1... | collective-permute-start | bytes 393224 | tf_op jit(solution)/shard_map/ppermute | solution.py:413
  50.5 13.3 %collective-permute-start.8 = (bf16[32,16,128]{2,1,0:T(8,128)(2,1)S(1)}, bf16[32,16,128]{2,1,0:T(8,128)(2,1)S(1)}, u32[]{:S(2)}, u32[]{:S(2)}) collective-permute-start(bf16[32,16,128]{2,1,0:T(8,128)(2,1)S(1)} %get-tuple-element.93), channel_id=1, source_target_pairs={{1,2},{2,1},{3,4},{4,3},{5,6},{6,5},{7,8},{8,7},{9,10},{10,9},{11,... | collective-permute-start | bytes 393224 | tf_op jit(solution)/shard_map/ppermute | solution.py:410
  51.2 12.7 %collective-permute-start.9 = (bf16[16,32,128]{2,1,0:T(8,128)(2,1)S(1)}, bf16[16,32,128]{2,1,0:T(8,128)(2,1)S(1)}, u32[]{:S(2)}, u32[]{:S(2)}) collective-permute-start(bf16[16,32,128]{2,1,0:T(8,128)(2,1)S(1)} %get-tuple-element.94), channel_id=1, source_target_pairs={{32,64},{64,32},{96,128},{128,96},{160,192},{192,160},{224,256},{2... | collective-permute-start | bytes 393224 | tf_op jit(solution)/shard_map/ppermute | solution.py:411
  53.7 10.3 %collective-permute-start.10 = (bf16[32,16,128]{2,1,0:T(8,128)(2,1)S(1)}, bf16[32,16,128]{2,1,0:T(8,128)(2,1)S(1)}, u32[]{:S(2)}, u32[]{:S(2)}) collective-permute-start(bf16[32,16,128]{2,1,0:T(8,128)(2,1)S(1)} %get-tuple-element.95), channel_id=1, source_target_pairs={{0,1},{1,0},{2,3},{3,2},{4,5},{5,4},{6,7},{7,6},{8,9},{9,8},{10,11... | collective-permute-start | bytes 393224 | tf_op jit(solution)/shard_map/ppermute | solution.py:412
  61.4 3.2 %collective-permute-start.11 = (bf16[16,32,128]{2,1,0:T(8,128)(2,1)S(1)}, bf16[16,32,128]{2,1,0:T(8,128)(2,1)S(1)}, u32[]{:S(2)}, u32[]{:S(2)}) collective-permute-start(bf16[16,32,128]{2,1,0:T(8,128)(2,1)S(1)} %get-tuple-element.96), channel_id=1, source_target_pairs={{0,32},{32,0},{64,96},{96,64},{128,160},{160,128},{192,224},{224,1... | collective-permute-start | bytes 393224 | tf_op jit(solution)/shard_map/ppermute | solution.py:413
  81.9 27.6 %all-to-all-start.2 = ((f32[16,8,128]{2,1,0:T(8,128)}), f32[16,8,128]{2,1,0:T(8,128)S(1)}, u32[]{:S(2)}, u32[]{:S(2)}) async-start(f32[16,8,128]{2,1,0:T(8,128)} %shard_map.129), calls=%async_computation.2 | async-start | bytes 131072 | tf_op jit(solution)/shard_map/all_to_all | solution.py:526
  96.2 19.1 %collective-permute-start.12 = (bf16[32,16,128]{2,1,0:T(8,128)(2,1)S(1)}, bf16[32,16,128]{2,1,0:T(8,128)(2,1)S(1)}, u32[]{:S(2)}, u32[]{:S(2)}) collective-permute-start(bf16[32,16,128]{2,1,0:T(8,128)(2,1)S(1)} %get-tuple-element.107), channel_id=1, source_target_pairs={{1,2},{2,1},{3,4},{4,3},{5,6},{6,5},{7,8},{8,7},{9,10},{10,9},{11,... | collective-permute-start | bytes 393224 | tf_op jit(solution)/shard_map/ppermute | solution.py:410
  96.9 18.5 %collective-permute-start.13 = (bf16[16,32,128]{2,1,0:T(8,128)(2,1)S(1)}, bf16[16,32,128]{2,1,0:T(8,128)(2,1)S(1)}, u32[]{:S(2)}, u32[]{:S(2)}) collective-permute-start(bf16[16,32,128]{2,1,0:T(8,128)(2,1)S(1)} %get-tuple-element.108), channel_id=1, source_target_pairs={{32,64},{64,32},{96,128},{128,96},{160,192},{192,160},{224,256},{2... | collective-permute-start | bytes 393224 | tf_op jit(solution)/shard_map/ppermute | solution.py:411
  99.7 15.6 %collective-permute-start.14 = (bf16[32,16,128]{2,1,0:T(8,128)(2,1)S(1)}, bf16[32,16,128]{2,1,0:T(8,128)(2,1)S(1)}, u32[]{:S(2)}, u32[]{:S(2)}) collective-permute-start(bf16[32,16,128]{2,1,0:T(8,128)(2,1)S(1)} %get-tuple-element.109), channel_id=1, source_target_pairs={{0,1},{1,0},{2,3},{3,2},{4,5},{5,4},{6,7},{7,6},{8,9},{9,8},{10,11... | collective-permute-start | bytes 393224 | tf_op jit(solution)/shard_map/ppermute | solution.py:412
  107.5 7.9 %collective-permute-start.15 = (bf16[16,32,128]{2,1,0:T(8,128)(2,1)S(1)}, bf16[16,32,128]{2,1,0:T(8,128)(2,1)S(1)}, u32[]{:S(2)}, u32[]{:S(2)}) collective-permute-start(bf16[16,32,128]{2,1,0:T(8,128)(2,1)S(1)} %get-tuple-element.110), channel_id=1, source_target_pairs={{0,32},{32,0},{64,96},{96,64},{128,160},{160,128},{192,224},{224,1... | collective-permute-start | bytes 393224 | tf_op jit(solution)/shard_map/ppermute | solution.py:413
  110.1 12.9 %all-to-all-start.3 = ((f32[32,8,128]{2,1,0:T(8,128)}), f32[32,8,128]{2,1,0:T(8,128)S(1)}, u32[]{:S(2)}, u32[]{:S(2)}) async-start(f32[32,8,128]{2,1,0:T(8,128)} %shard_map.130), calls=%async_computation.3 | async-start | bytes 262144 | tf_op jit(solution)/shard_map/all_to_all | solution.py:528
